TPU v7x, 32 devices: a whole 2x2x4 slice. The times are simulated.
32 devices in a mesh: tm: 2 (over x), row: 4 (over z), col: 4 (over y, core).
Axes of the slice: x: 2, y: 2, z: 4, core: 2. Of those that a mesh axis runs over, the one named last changes fastest.
Arguments:
- occ_orbitals: bfloat16 [1024, 2048], P(('col', 'row'), 'tm'), may hold values from -0.4375 to 0.4375
- empty_orbitals: bfloat16 [1024, 2048], P(('col', 'row'), 'tm'), may hold values from -0.4375 to 0.4375
- occ_rate: float32 [2048], replicated, may hold values from 0.05 to 4
- empty_rate: float32 [2048], replicated, may hold values from 0.05 to 4
- columns: bfloat16 [1024, 256], P(('col', 'row')), may hold values from -6 to 6
Outputs:
- screened_columns: float32 [1024, 16, 256], P(('col', 'row'), 'tm')
All inputs are finite; a program needn't handle non-finite values.
Results may differ from a plain program's by a relative error of at most 0.018.
Values may be sent and summed in bfloat16 or wider, within the bound.
No kernel may reach another device: no remote copies, remote signals or barrier semaphores. Data moves between devices by JAX's collectives and lax.ppermute only.
A program may use at most 64 MiB of HBM per device.

v0:
```python
import jax
import jax.numpy as jnp
from jax import lax
from jax.sharding import PartitionSpec as P

NT = 16
NF = 16


damping = 0.3


def time_tables(count_times, count_freqs):
    moments = 0.25 * (jnp.arange(count_times).astype(jnp.float32) + 0.5)
    omegas = 0.4 * (jnp.arange(count_freqs).astype(jnp.float32) + 0.5)
    cosine = (0.5 * jnp.cos(omegas[:, None] * moments[None, :])).astype(jnp.bfloat16)
    return (moments, cosine)


def shards(occ_orbitals, empty_orbitals, occ_rate, empty_rate, columns):
    tm_count = lax.axis_size("tm")
    occ_part, empty_part, rhs_block = (
        lax.all_gather(occ_orbitals, "row", axis=0, tiled=True),
        lax.all_gather(empty_orbitals, "row", axis=0, tiled=True),
        lax.all_gather(columns, "row", axis=0, tiled=True),
    )
    occ_block, empty_block = (
        lax.all_gather(occ_part, "tm", axis=1, tiled=True),
        lax.all_gather(empty_part, "tm", axis=1, tiled=True),
    )
    shard_rows = occ_orbitals.shape[0]
    row_index = lax.axis_index("row")
    own_start = row_index * shard_rows
    own_occ = lax.dynamic_slice_in_dim(occ_block, own_start, shard_rows, 0)
    own_empty = lax.dynamic_slice_in_dim(empty_block, own_start, shard_rows, 0)
    occ_rows, empty_rows, rhs_rows = (
        lax.all_gather(own_occ, "col", axis=0, tiled=True),
        lax.all_gather(own_empty, "col", axis=0, tiled=True),
        lax.all_gather(columns, "col", axis=0, tiled=True),
    )
    moments, cosine = time_tables(NT, NF)
    local_times = NT // tm_count
    first_time = lax.axis_index("tm") * local_times
    occ_wide = occ_rows.astype(jnp.float32)
    empty_wide = empty_rows.astype(jnp.float32)
    tiles = []
    for step in range(local_times):
        moment = moments[first_time + step]
        scaled_occ = (occ_wide * jnp.exp(-occ_rate * moment)[None, :]).astype(jnp.bfloat16)
        scaled_empty = (empty_wide * jnp.exp(-empty_rate * moment)[None, :]).astype(jnp.bfloat16)
        green_occ = jnp.einsum(
            "ro,co->rc", scaled_occ, occ_block, preferred_element_type=jnp.float32
        )
        green_empty = jnp.einsum(
            "ro,co->rc", scaled_empty, empty_block, preferred_element_type=jnp.float32
        )
        tiles.append((-2.0 * green_occ * green_empty).astype(jnp.bfloat16))
    polar = jnp.stack(tiles)
    spectral = jnp.einsum(
        "kj,jrc->krc",
        cosine,
        lax.all_to_all(polar, "tm", split_axis=2, concat_axis=0, tiled=True),
        preferred_element_type=jnp.float32,
    ).astype(jnp.bfloat16)
    screened = lax.all_to_all(spectral, "tm", split_axis=0, concat_axis=2, tiled=True)
    partial_value = jnp.einsum(
        "frc,cn->frn", screened, rhs_block, preferred_element_type=jnp.float32
    )
    first = lax.psum(partial_value.astype(jnp.bfloat16), "col").astype(jnp.float32)
    middle = (rhs_rows.astype(jnp.float32)[None, :, :] + damping * first).astype(jnp.bfloat16)
    second = lax.psum_scatter(
        jnp.einsum("frc,frn->cfn", screened, middle, preferred_element_type=jnp.float32).astype(
            jnp.bfloat16
        ),
        "row",
        scatter_dimension=0,
        tiled=True,
    ).astype(jnp.float32)
    return columns.astype(jnp.float32)[:, None, :] + damping * second


def solution(mesh):
    placed = (P(("col", "row"), "tm"), P(("col", "row"), "tm"), P(), P(), P(("col", "row"), None))
    return jax.shard_map(
        shards, mesh=mesh, in_specs=placed, out_specs=P(("col", "row"), "tm", None), check_vma=False
    )
```

profile of v0, /device:TPU:0, one launch (start us, length us, event | category | flops | bytes accessed | tf_op | source)
XLA Modules:
  0.0 232.5 jit_solution(16432727972130530147)
XLA Ops:
  6.5 0.0 all-gather.5.cloned.1.call-start
  6.5 19.5 %all_gather.25 = bf16[256,1024]{1,0:T(8,128)(2,1)} all-gather(bf16[64,1024]{1,0:T(8,128)(2,1)} %param.5), channel_id=1, replica_groups=mesh['tm'=2,'row'=4,'col'=4] {'row'}, dimensions={0}, use_global_device_ids=true | all-gather | bytes 655360 | tf_op jit(solution)/shard_map/all_gather | solution.py:23
  26.0 0.0 all-gather.5.cloned.1.call-update
  26.0 0.0 copy-start.4
  26.1 0.0 copy-start.5
  26.1 0.0 all-gather.9.cloned.1.call-start
  26.1 0.0 copy-done.1
  26.1 16.4 %all_gather.28 = bf16[256,1024]{1,0:T(8,128)(2,1)} all-gather(bf16[64,1024]{1,0:T(8,128)(2,1)S(1)} %copy-done.1), channel_id=1, replica_groups=mesh['tm'=2,'row'=4,'col'=4] {'row'}, dimensions={0}, use_global_device_ids=true | all-gather | bytes 655360 | tf_op jit(solution)/shard_map/all_gather | solution.py:24
  42.5 0.0 all-gather.9.cloned.1.call-update
  42.5 0.0 all-gather.7.cloned.1.call-start
  42.6 4.6 %all-gather.5.cloned.1.call-done = bf16[256,2048]{1,0:T(8,128)(2,1)} async-done(((bf16[256,1024]{1,0:T(8,128)(2,1)}), bf16[256,2048]{1,0:T(8,128)(2,1)}) %all-gather.5.cloned.1.call-update) | async-done | bytes 1048592 | tf_op jit(solution)/shard_map/all_gather | solution.py:28
  47.2 1.8 constant_dynamic-slice_fusion.1
  48.9 0.0 all-gather.7.cloned.1.call-update
  49.0 0.0 all-gather.11.cloned.1.call-start
  49.0 0.7 fusion.86
  49.7 0.0 copy-done.4
  49.7 4.9 %multiply_exponential_fusion = (f32[2048]{0:T(1024)S(1)}, f32[2048]{0:T(1024)S(1)}, f32[2048]{0:T(1024)S(1)}, f32[2048]{0:T(1024)S(1)}, f32[2048]{0:T(1024)S(1)}...) fusion(f32[2048]{0:T(1024)S(1)} %copy-done.4, f32[]{:T(128)} %bitcast.15, f32[]{:T(128)} %bitcast.3, ...), kind=kLoop, calls=%fused_computation.99 | loop fusion | flops 18432 | bytes 73760 | tf_op jit(solution)/shard_map/exp | solution.py:50
  54.7 4.9 %multiply_exponential_fusion.1 = (f32[2048]{0:T(1024)S(1)}, f32[2048]{0:T(1024)S(1)}, f32[2048]{0:T(1024)S(1)}, f32[2048]{0:T(1024)S(1)}, f32[2048]{0:T(1024)S(1...) fusion(f32[2048]{0:T(1024)S(1)} %copy-done.5, f32[]{:T(128)} %bitcast.15, f32[]{:T(128)} %bitcast.3, ...), kind=kLoop, calls=%fused_computation.100 | loop fusion | flops 18432 | bytes 73760 | tf_op jit(solution)/shard_map/exp | solution.py:49
  59.6 10.4 %all-gather.9.cloned.1.call-done = bf16[256,2048]{1,0:T(8,128)(2,1)} async-done(((bf16[256,1024]{1,0:T(8,128)(2,1)}), bf16[256,2048]{1,0:T(8,128)(2,1)}) %all-gather.9.cloned.1.call-update) | async-done | bytes 1048592 | tf_op jit(solution)/shard_map/all_gather | solution.py:29
  70.0 1.7 constant_dynamic-slice_fusion
  71.7 0.0 all-gather.11.cloned.1.call-update
  71.7 16.6 %all-gather.7.cloned.1.call-done = bf16[256,2048]{1,0:T(8,128)(2,1)} async-done(((bf16[64,2048]{1,0:T(8,128)(2,1)}), bf16[256,2048]{1,0:T(8,128)(2,1)}) %all-gather.7.cloned.1.call-update) | async-done | bytes 1048592 | tf_op jit(solution)/shard_map/all_gather | solution.py:37
  88.4 0.0 copy-done.3
  88.4 2.5 %convolution_multiply_fusion.13 = f32[256,256]{1,0:T(8,128)} fusion(bf16[256,2048]{1,0:T(8,128)(2,1)S(1)} %copy-done.3, bf16[256,2048]{1,0:T(8,128)(2,1)} %all-gather.7.cloned.1.call-done, f32[2048]{0:T(1024)S(1)} %get-tuple-element.14), kind=kOutput, calls=%fused_computation.50 | convolution fusion | flops 270073856 | bytes 2367488 | tf_op jit(solution)/shard_map/ro,co->rc/dot_general | solution.py:51
  90.9 1.2 convolution_multiply_fusion.11
  92.0 0.5 convolution_multiply_fusion.9
  92.5 0.5 convolution_multiply_fusion.7
  93.0 0.5 convolution_multiply_fusion.5
  93.5 0.5 convolution_multiply_fusion.3
  94.0 0.5 convolution_multiply_fusion.1
  94.5 1.2 convolution_multiply_fusion.15
  95.7 10.8 %all-gather.11.cloned.1.call-done = bf16[256,2048]{1,0:T(8,128)(2,1)} async-done(((bf16[64,2048]{1,0:T(8,128)(2,1)}), bf16[256,2048]{1,0:T(8,128)(2,1)}) %all-gather.11.cloned.1.call-update) | async-done | bytes 1048592 | tf_op jit(solution)/shard_map/all_gather | solution.py:38
  106.5 1.8 fusion.40
  108.4 0.5 fusion.38
  108.9 0.4 copy-done.8
  109.3 0.5 fusion.36
  109.8 0.5 fusion.34
  110.3 0.5 fusion.32
  110.8 0.5 fusion.30
  111.3 0.5 fusion.28
  111.8 0.5 fusion.26
  112.3 1.8 copy.12
  114.1 3.6 %all-to-all-start = ((bf16[8,256,256]{1,0,2:T(8,128)(2,1)}), bf16[8,256,256]{1,0,2:T(8,128)(2,1)S(1)}, u32[]{:S(2)}, u32[]{:S(2)}) async-start(bf16[8,256,256]{1,0,2:T(8,128)(2,1)} %copy.12), calls=%async_computation | async-start | bytes 2097152 | tf_op jit(solution)/shard_map/all_to_all | solution.py:62
  117.7 14.2 %all-to-all-done = bf16[8,256,256]{1,0,2:T(8,128)(2,1)S(1)} async-done(((bf16[8,256,256]{1,0,2:T(8,128)(2,1)}), bf16[8,256,256]{1,0,2:T(8,128)(2,1)S(1)}, u32[]{:S(2)}, u32[]{:S(2)}) %all-to-all-start) | async-done | bytes 1048608 | tf_op jit(solution)/shard_map/all_to_all | solution.py:62
  131.9 1.3 copy.13
  133.2 0.5 convolution_convert_fusion.2
  133.8 1.3 copy.14
  135.0 3.7 %all-to-all-start.1 = ((bf16[16,256,128]{2,1,0:T(8,128)(2,1)}), bf16[16,256,128]{2,1,0:T(8,128)(2,1)S(1)}, u32[]{:S(2)}, u32[]{:S(2)}) async-start(bf16[16,256,128]{2,1,0:T(8,128)(2,1)} %copy.14), calls=%async_computation.1 | async-start | bytes 2097152 | tf_op jit(solution)/shard_map/all_to_all | solution.py:65
  138.7 0.0 all-reduce.2.cloned.1.call-start
  138.8 13.4 %all_gather.31 = bf16[256,256]{1,0:T(8,128)(2,1)S(1)} all-gather(bf16[64,256]{1,0:T(8,128)(2,1)S(1)} %copy-done), channel_id=1, replica_groups=mesh['tm'=2,'row'=4,'col'=4] {'row'}, dimensions={0}, use_global_device_ids=true | all-gather | bytes 163840 | tf_op jit(solution)/shard_map/all_gather | solution.py:25
  152.2 0.0 all-to-all-done.1
  152.2 1.1 copy.18
  153.3 0.7 all_to_all.33
  154.0 1.4 convolution_convert_fusion.1
  155.5 0.0 all-reduce.2.cloned.1.call-update
  155.5 0.0 reduce-scatter.2.cloned.1.call-start
  155.5 5.4 %all_gather.24 = bf16[256,256]{1,0:T(8,128)(2,1)S(1)} all-gather(bf16[64,256]{1,0:T(8,128)(2,1)S(1)} %copy-done), channel_id=1, replica_groups=mesh['tm'=2,'row'=4,'col'=4] {'col'}, dimensions={0}, use_global_device_ids=true | all-gather | bytes 163840 | tf_op jit(solution)/shard_map/all_gather | solution.py:39
  161.0 0.1 copy.11
  161.1 31.3 %all-reduce.2.cloned.1.call-done = bf16[8,256,256]{1,2,0:T(8,128)(2,1)} async-done(((bf16[8,256,256]{1,2,0:T(8,128)(2,1)}), bf16[8,256,256]{1,2,0:T(8,128)(2,1)}) %all-reduce.2.cloned.1.call-update) | async-done | bytes 1048592 | tf_op jit(solution)/shard_map/psum | solution.py:69
  192.4 1.7 fusion.16
  194.1 1.8 copy.16
  195.9 0.0 reduce-scatter.2.cloned.1.call-update
  195.9 27.9 %reduce-scatter.2.cloned.1.call-done = bf16[64,8,256]{2,1,0:T(8,128)(2,1)} async-done(((bf16[256,8,256]{2,1,0:T(8,128)(2,1)}), bf16[64,8,256]{2,1,0:T(8,128)(2,1)}) %reduce-scatter.2.cloned.1.call-update) | async-done | bytes 262160 | tf_op jit(solution)/shard_map/reduce_scatter | solution.py:71
  223.8 1.8 multiply_add_fusion
  (17 shorter events, 0.0 us)
Async XLA Ops:
  6.5 19.6 %copy-start.1 = (bf16[64,1024]{1,0:T(8,128)(2,1)S(1)}, bf16[64,1024]{1,0:T(8,128)(2,1)}, u32[]{:S(2)}) copy-start(bf16[64,1024]{1,0:T(8,128)(2,1)} %param.6) | copy-start | bytes 393220
  6.5 40.7 %all-gather.5.cloned.1.call-start = ((), (), s32[]{:S(2)}) async-start(), calls=%async_computation.3 | async-start | bytes 1572864 | tf_op jit(solution)/shard_map/all_gather | solution.py:28
  26.0 23.7 %copy-start.4 = (f32[2048]{0:T(1024)S(1)}, f32[2048]{0:T(1024)}, u32[]{:S(2)}) copy-start(f32[2048]{0:T(1024)} %param.8) | copy-start | bytes 24580
  26.1 28.6 %copy-start.5 = (f32[2048]{0:T(1024)S(1)}, f32[2048]{0:T(1024)}, u32[]{:S(2)}) copy-start(f32[2048]{0:T(1024)} %param.7) | copy-start | bytes 24580
  26.1 44.0 %all-gather.9.cloned.1.call-start = ((), (), s32[]{:S(2)}) async-start(), calls=%async_computation.5 | async-start | bytes 1572864 | tf_op jit(solution)/shard_map/all_gather | solution.py:29
  42.5 45.8 %all-gather.7.cloned.1.call-start = ((), (), s32[]{:S(2)}) async-start(), calls=%async_computation.4 | async-start | bytes 1310720 | tf_op jit(solution)/shard_map/all_gather | solution.py:37
  47.2 41.2 %copy-start.3 = (bf16[256,2048]{1,0:T(8,128)(2,1)S(1)}, bf16[256,2048]{1,0:T(8,128)(2,1)}, u32[]{:S(2)}) copy-start(bf16[256,2048]{1,0:T(8,128)(2,1)} %all-gather.5.cloned.1.call-done) | copy-start | bytes 3145732
  49.0 57.5 %all-gather.11.cloned.1.call-start = ((), (), s32[]{:S(2)}) async-start(), calls=%async_computation.6 | async-start | bytes 1310720 | tf_op jit(solution)/shard_map/all_gather | solution.py:38
  88.4 2.5 %copy-start.6 = (bf16[256,2048]{1,0:T(8,128)(2,1)S(1)}, bf16[256,2048]{1,0:T(8,128)(2,1)}, u32[]{:S(2)}) copy-start(bf16[256,2048]{1,0:T(8,128)(2,1)} %all-gather.7.cloned.1.call-done) | copy-start | bytes 3145732
  94.5 12.0 %copy-start.2 = (bf16[256,2048]{1,0:T(8,128)(2,1)S(1)}, bf16[256,2048]{1,0:T(8,128)(2,1)}, u32[]{:S(2)}) copy-start(bf16[256,2048]{1,0:T(8,128)(2,1)} %all-gather.9.cloned.1.call-done) | copy-start | bytes 3145732
  106.5 1.9 copy-start.7
  106.5 1.9 copy-start.9
  108.4 1.0 copy-start.8
  114.1 17.8 %all-to-all-start = ((bf16[8,256,256]{1,0,2:T(8,128)(2,1)}), bf16[8,256,256]{1,0,2:T(8,128)(2,1)S(1)}, u32[]{:S(2)}, u32[]{:S(2)}) async-start(bf16[8,256,256]{1,0,2:T(8,128)(2,1)} %copy.12), calls=%async_computation | async-start | bytes 2097152 | tf_op jit(solution)/shard_map/all_to_all | solution.py:62
  135.0 3.8 %copy-start = (bf16[64,256]{1,0:T(8,128)(2,1)S(1)}, bf16[64,256]{1,0:T(8,128)(2,1)}, u32[]{:S(2)}) copy-start(bf16[64,256]{1,0:T(8,128)(2,1)} %param.9) | copy-start | bytes 98308
  135.0 17.2 %all-to-all-start.1 = ((bf16[16,256,128]{2,1,0:T(8,128)(2,1)}), bf16[16,256,128]{2,1,0:T(8,128)(2,1)S(1)}, u32[]{:S(2)}, u32[]{:S(2)}) async-start(bf16[16,256,128]{2,1,0:T(8,128)(2,1)} %copy.14), calls=%async_computation.1 | async-start | bytes 2097152 | tf_op jit(solution)/shard_map/all_to_all | solution.py:65
  138.7 53.7 %all-reduce.2.cloned.1.call-start = ((), (), s32[]{:S(2)}) async-start(), calls=%async_computation.7 | async-start | bytes 2097152 | tf_op jit(solution)/shard_map/psum | solution.py:69
  155.5 68.3 %reduce-scatter.2.cloned.1.call-start = ((), (), s32[]{:S(2)}) async-start(), calls=%async_computation.8 | async-start | bytes 1310720 | tf_op jit(solution)/shard_map/reduce_scatter | solution.py:71
Sparse Core Ops, SparseCore 0:
  26.2 20.9 all-gather.4
  48.7 21.2 all-gather.8
  71.6 16.6 all-gather.6
  89.8 16.6 all-gather.10
  155.6 36.7 all-reduce.1
  196.0 27.7 reduce-scatter.1
where the time goes:
time: 233 us; the launch traced here: 232 us
  waiting for transfers between devices  116 us (50%)
  blocking collectives  54.7 us (23%)
  matrix products  16.2 us (7%)
  between operations  13.7 us (6%)
  local copies, waits for them, and re-layouts  12.7 us (5%)
  other arithmetic  11.7 us (5%)
  starting transfers between devices  7.5 us (3%)
    psum x1, waiting for transfers between devices, shards(): lax.psum(partial_value.astype(jnp.bfloat16), 'col').astype(jnp.float32)  31.3 us
    reduce_scatter x1, waiting for transfers between devices, shards(): lax.psum_scatter(jnp.einsum('frc,frn->cfn', screened, middle, preferred_e...  27.9 us
    all_gather x1, blocking collectives, shards(): lax.all_gather(occ_orbitals, 'row', axis=0, tiled=True)  19.5 us
    all_gather x1, waiting for transfers between devices, shards(): lax.all_gather(own_occ, 'col', axis=0, tiled=True)  16.6 us
    all_gather x1, blocking collectives, shards(): lax.all_gather(empty_orbitals, 'row', axis=0, tiled=True)  16.4 us
    all_to_all x1, waiting for transfers between devices, shards(): lax.all_to_all(polar, 'tm', split_axis=2, concat_axis=0, tiled=True)  14.2 us
    all_gather x1, blocking collectives, shards(): lax.all_gather(columns, 'row', axis=0, tiled=True)  13.4 us
    all_gather x1, waiting for transfers between devices, shards(): lax.all_gather(own_empty, 'col', axis=0, tiled=True)  10.8 us
  transfers between devices with their start and end apart: 8, of which 7 were waited for; matrix products, arithmetic and copies ran while one was open for 9% of the time, Pallas kernels for 0%

commit v1 on v0

v1 whole, which is shorter than its diff:
```python
import functools

import jax
import jax.numpy as jnp
from jax import lax
from jax.experimental import pallas as pl
from jax.experimental.pallas import tpu as pltpu
from jax.sharding import PartitionSpec as P

NT = 16
NF = 16

damping = 0.3

ANY = pl.BlockSpec(memory_space=pl.ANY)
VMEM = pl.BlockSpec(memory_space=pltpu.VMEM)
SMEM = pl.BlockSpec(memory_space=pltpu.SMEM)


def time_tables(count_times, count_freqs):
    moments = 0.25 * (jnp.arange(count_times).astype(jnp.float32) + 0.5)
    omegas = 0.4 * (jnp.arange(count_freqs).astype(jnp.float32) + 0.5)
    cosine = (0.5 * jnp.cos(omegas[:, None] * moments[None, :])).astype(jnp.bfloat16)
    return (moments, cosine)


def swap(value, axis, bit):
    size = lax.axis_size(axis)
    return lax.ppermute(value, axis, [(i, i ^ bit) for i in range(size)])


def shift(value, axis, step):
    size = lax.axis_size(axis)
    return lax.ppermute(value, axis, [(i, (i + step) % size) for i in range(size)])


def bits_of(count):
    return [1 << b for b in reversed(range(count.bit_length() - 1))]


def ring(value, axis):
    size = lax.axis_size(axis)
    blocks = {0: value}
    ahead = behind = value
    for k in range(1, size // 2 + 1):
        ahead = shift(ahead, axis, -1)
        blocks[k] = ahead
        if k <= (size - 1) // 2:
            behind = shift(behind, axis, 1)
            blocks[size - k] = behind
    return blocks


def spread(pieces, axis, bit, slot):
    out = dict(pieces)
    for key, value in pieces.items():
        moved = list(key)
        moved[slot] ^= bit
        out[tuple(moved)] = swap(value, axis, bit)
    return out


def tile_kernel(keys, dims, cosine, factors, *refs):
    (row_keys, col_keys) = keys
    (times, freqs, half, shard_rows, part, batch) = dims
    pieces = refs[: len(row_keys) + len(col_keys)]
    out, rows, cols, scaled, polar, sem = refs[len(pieces) :]
    tm, q, p = lax.axis_index("tm"), lax.axis_index("row"), lax.axis_index("col")
    row_count = rows.shape[1] // shard_rows
    col_count = cols.shape[1] // part
    copies = []
    for (arr, kt, kc), ref in zip(row_keys, pieces[: len(row_keys)]):
        to = pl.multiple_of((p ^ kc) * shard_rows, shard_rows)
        lane = pl.multiple_of((tm ^ kt) * half, half)
        copies.append((ref, rows.at[arr, pl.ds(to, shard_rows), pl.ds(lane, half)]))
    for (arr, kts, kq), ref in zip(col_keys, pieces[len(row_keys) :]):
        to = pl.multiple_of(lax.rem(q + kq, col_count) * part, part)
        for n, kt in enumerate(kts):
            lane = pl.multiple_of((tm ^ kt) * half, half)
            copies.append(
                (ref.at[:, pl.ds(n * half, half)], cols.at[arr, pl.ds(to, part), pl.ds(lane, half)])
            )
    copies = [pltpu.make_async_copy(a, b, sem) for a, b in copies]
    for copy in copies:
        copy.start()
    for copy in copies:
        copy.wait()
    width = cols.shape[1]

    def some_times(step, carry):
        greens = []
        for arr in range(2):
            for b in range(batch):
                factor = factors[arr, pl.ds(step * batch + b, 1), :]
                scaled[arr, pl.ds(b * width, width), :] = (
                    cols[arr].astype(jnp.float32) * factor
                ).astype(jnp.bfloat16)
            greens.append(
                lax.dot_general(
                    scaled[arr],
                    rows[arr],
                    (((1,), (1,)), ((), ())),
                    preferred_element_type=jnp.float32,
                )
            )
        product = (-2.0 * greens[0] * greens[1]).astype(jnp.bfloat16)
        polar[pl.ds(step * batch, batch)] = product.reshape(batch, width, rows.shape[1])
        return carry

    lax.fori_loop(0, times // batch, some_times, 0)
    chunk = 16
    lanes = 128

    def transform(index, carry):
        start = pl.multiple_of(index * chunk, chunk)
        for lane in range(0, rows.shape[1], lanes):
            values = [
                polar[j, pl.ds(start, chunk), pl.ds(lane, lanes)].astype(jnp.float32)
                for j in range(times)
            ]
            for k in range(freqs):
                total = values[0] * cosine[k, 0]
                for j in range(1, times):
                    total = total + values[j] * cosine[k, j]
                out[k, pl.ds(start, chunk), pl.ds(lane, lanes)] = total.astype(jnp.bfloat16)
        return carry

    lax.fori_loop(0, width // chunk, transform, 0)


def columns_kernel(keys, dims, *refs):
    (tm_count, row_count, col_count, shard_rows, part) = dims
    pieces = refs[: len(keys)]
    out, own, gathered, own_rows, sem = refs[len(keys) :]
    q, p = lax.axis_index("row"), lax.axis_index("col")
    width = row_count * part
    copies = []
    for (kq, kc), ref in zip(keys, pieces):
        for t in range(tm_count):
            to = (t * col_count + (p ^ kc)) * width + lax.rem(q + kq, row_count) * part
            to = pl.multiple_of(to, part)
            copies.append((ref.at[pl.ds(t * part, part), :], gathered.at[pl.ds(to, part), :]))
        if kq == 0:
            to = pl.multiple_of((p ^ kc) * shard_rows, shard_rows)
            copies.append((ref, own_rows.at[pl.ds(to, shard_rows), :]))
    copies = [pltpu.make_async_copy(a, b, sem) for a, b in copies]
    for copy in copies:
        copy.start()
    for copy in copies:
        copy.wait()
    out[...] = gathered[...].astype(jnp.float32).T.astype(jnp.bfloat16)
    own[...] = own_rows[...].astype(jnp.float32).T.astype(jnp.bfloat16)


def first_kernel(all_columns, own, tiles, out):
    sources, freqs, width, rows = tiles.shape
    for k in range(freqs):
        weights = tiles[:, k].reshape(sources * width, rows)
        first = jnp.dot(all_columns[...], weights, preferred_element_type=jnp.float32)
        out[k] = (own[...].astype(jnp.float32) + damping * first).astype(jnp.bfloat16)


def second_kernel(dims, tiles, *refs):
    (tm_count, row_count, col_count, part, shard_rows) = dims
    middles = refs[:row_count]
    out = refs[row_count]
    sources, freqs, width, rows = tiles.shape
    q = lax.axis_index("row")
    for k in range(freqs):
        total = None
        for kq in range(row_count):
            start = pl.multiple_of(lax.rem(q + kq, row_count) * part, part)
            weights = jnp.concatenate(
                [
                    tiles[t * col_count + p, k, pl.ds(start, part), :]
                    for p in range(col_count)
                    for t in range(tm_count)
                ],
                axis=0,
            )
            term = jnp.dot(middles[kq][k], weights, preferred_element_type=jnp.float32)
            total = term if total is None else total + term
        second = total.T.astype(jnp.bfloat16)
        for p in range(col_count):
            out[p, k] = second[p * shard_rows : (p + 1) * shard_rows]


def shards(occ_orbitals, empty_orbitals, occ_rate, empty_rate, columns):
    tm_count, row_count, col_count = (lax.axis_size(a) for a in ("tm", "row", "col"))
    shard_rows, half = occ_orbitals.shape
    columns_wide = columns.shape[1]
    orbitals = tm_count * half
    part = shard_rows // tm_count
    width = row_count * part
    tile_rows = col_count * shard_rows
    tm_index, col_index = lax.axis_index("tm"), lax.axis_index("col")
    both = (occ_orbitals, empty_orbitals)
    high, low = bits_of(col_count)[:-1], bits_of(col_count)[-1:]

    col_pieces = {}
    for arr, value in enumerate(both):
        held = []
        for kt in range(tm_count):
            block = lax.dynamic_slice_in_dim(value, (tm_index ^ kt) * part, part, 0)
            held.append(swap(block, "tm", kt) if kt else block)
        groups = [((kt,), block) for kt, block in enumerate(held)]
        if tm_count > 2:
            groups = [(tuple(range(tm_count)), jnp.concatenate(held, axis=1))]
        for kts, block in groups:
            for kq, moved in ring(block, "row").items():
                col_pieces[(arr, kts, kq)] = moved
    row_pieces = {}
    for arr, value in enumerate(both):
        pieces = {(arr, 0, 0): value}
        steps = [("tm", b, 1) for b in bits_of(tm_count)], [("col", b, 2) for b in high]
        order = steps[1] + steps[0] if arr == 0 else steps[0] + steps[1]
        for axis, bit, slot in order + [("col", b, 2) for b in low]:
            pieces = spread(pieces, axis, bit, slot)
        row_pieces.update(pieces)
    column_pieces = {(kq, 0): moved for kq, moved in ring(columns, "row").items()}
    for bit in high + low:
        column_pieces = spread(column_pieces, "col", bit, 1)

    moments, cosine = time_tables(NT, NF)
    factors = jnp.exp(-jnp.stack([occ_rate, empty_rate])[:, None, :] * moments[None, :, None])
    row_keys, col_keys = list(row_pieces), list(col_pieces)
    batch = 4
    tile = pl.pallas_call(
        functools.partial(
            tile_kernel, (row_keys, col_keys), (NT, NF, half, shard_rows, part, batch)
        ),
        out_shape=jax.ShapeDtypeStruct((NF, width, tile_rows), jnp.bfloat16),
        in_specs=[SMEM, VMEM] + [ANY] * (len(row_keys) + len(col_keys)),
        out_specs=VMEM,
        scratch_shapes=[
            pltpu.VMEM((2, tile_rows, orbitals), jnp.bfloat16),
            pltpu.VMEM((2, width, orbitals), jnp.bfloat16),
            pltpu.VMEM((2, batch * width, orbitals), jnp.bfloat16),
            pltpu.VMEM((NT, width, tile_rows), jnp.bfloat16),
            pltpu.SemaphoreType.DMA,
        ],
        name="tile",
    )(
        cosine.astype(jnp.float32),
        factors,
        *[row_pieces[k] for k in row_keys],
        *[col_pieces[k] for k in col_keys],
    )

    keys = list(column_pieces)
    all_columns, own = pl.pallas_call(
        functools.partial(
            columns_kernel, keys, (tm_count, row_count, col_count, shard_rows, part)
        ),
        out_shape=(
            jax.ShapeDtypeStruct((columns_wide, tm_count * col_count * width), jnp.bfloat16),
            jax.ShapeDtypeStruct((columns_wide, tile_rows), jnp.bfloat16),
        ),
        in_specs=[ANY] * len(keys),
        out_specs=(VMEM, VMEM),
        scratch_shapes=[
            pltpu.VMEM((tm_count * col_count * width, columns_wide), jnp.bfloat16),
            pltpu.VMEM((tile_rows, columns_wide), jnp.bfloat16),
            pltpu.SemaphoreType.DMA,
        ],
        name="columns",
    )(*[column_pieces[k] for k in keys])

    local_freqs = NF // tm_count
    own_freqs = max(1, local_freqs // col_count)
    splits = max(1, col_count // local_freqs)
    columns_own = columns_wide // splits
    sent = tile.reshape(NF // own_freqs, own_freqs, width, tile_rows)
    if splits > 1:
        sent = jnp.repeat(sent, splits, axis=0)
        first_row = (col_index % splits) * columns_own
        all_columns = lax.dynamic_slice_in_dim(all_columns, first_row, columns_own, 0)
        own = lax.dynamic_slice_in_dim(own, first_row, columns_own, 0)
    tiles = lax.all_to_all(sent, ("tm", "col"), split_axis=0, concat_axis=0, tiled=True)

    middle = pl.pallas_call(
        first_kernel,
        out_shape=jax.ShapeDtypeStruct((own_freqs, columns_own, tile_rows), jnp.bfloat16),
        in_specs=[VMEM, VMEM, VMEM],
        out_specs=VMEM,
        name="first",
    )(all_columns, own, tiles)
    middles = ring(middle, "row")
    second = pl.pallas_call(
        functools.partial(second_kernel, (tm_count, row_count, col_count, part, shard_rows)),
        out_shape=jax.ShapeDtypeStruct(
            (col_count, own_freqs, shard_rows, columns_own), jnp.bfloat16
        ),
        in_specs=[VMEM] * (1 + row_count),
        out_specs=VMEM,
        name="second",
    )(tiles, *[middles[k] for k in range(row_count)])
    second = lax.all_to_all(second, "col", split_axis=0, concat_axis=0, tiled=True)
    second = second.reshape(
        col_count // splits, splits, own_freqs, shard_rows, columns_own
    ).transpose(3, 0, 2, 1, 4)
    second = second.reshape(shard_rows, local_freqs, columns_wide).astype(jnp.float32)
    return columns.astype(jnp.float32)[:, None, :] + damping * second


def solution(mesh):
    placed = (P(("col", "row"), "tm"), P(("col", "row"), "tm"), P(), P(), P(("col", "row"), None))
    return jax.shard_map(
        shards, mesh=mesh, in_specs=placed, out_specs=P(("col", "row"), "tm", None), check_vma=False
    )
```

time: 233 us -> 118 us (0.51)
  waiting for transfers between devices: 116 us -> 35.7 us
  blocking collectives: 54.7 us -> 0 us
  starting transfers between devices: 7.5 us -> 54.5 us
  Pallas kernels: 0 us -> 19.4 us
  matrix products: 16.2 us -> 0 us
  between operations: 13.7 us -> 0.6 us
  other arithmetic: 11.7 us -> 2.7 us
  local copies, waits for them, and re-layouts: 12.7 us -> 4.37 us
    all_gather x4 -> x0, blocking collectives: 54.7 us -> none  [the longest x1 19.5 us: shards(): lax.all_gather(occ_orbitals, 'row', axis=0, tiled=True)]
    ppermute x0 -> x46, starting transfers between devices: none -> 47.4 us  [the longest x18 29.7 us: shift(): lax.ppermute(value, axis, [(i, (i + step) % size) for i in range(size)])]
    all_gather x4 -> x0, waiting for transfers between devices: 42.5 us -> none  [the longest x1 16.6 us: shards(): lax.all_gather(own_occ, 'col', axis=0, tiled=True)]
    psum x1 -> x0, waiting for transfers between devices: 31.3 us -> none  [shards(): lax.psum(partial_value.astype(jnp.bfloat16), 'col').astype(jnp.float32)]
    ppermute x0 -> x46, waiting for transfers between devices: none -> 29.7 us  [the longest x18 18.1 us: shift(): lax.ppermute(value, axis, [(i, (i + step) % size) for i in range(size)])]
    reduce_scatter x1 -> x0, waiting for transfers between devices: 27.9 us -> none  [shards(): lax.psum_scatter(jnp.einsum('frc,frn->cfn', screened, middle, preferred_e...]
    pallas_call x0 -> x4, Pallas kernels: none -> 19.4 us  [the longest x1 11.9 us: shards(): pl.pallas_call(functools.partial(tile_kernel, (row_keys, col_keys), (NT,...]
    dot_general x19 -> x0, matrix products: 16.2 us -> none  [the longest x8 7.28 us: shards(): jnp.einsum('ro,co->rc', scaled_occ, occ_block, preferred_element_type=jnp...]
  transfers between devices with their start and end apart: 8 -> 48, of which waited for: 7 -> 18; matrix products, arithmetic and copies ran while one was open for 9% -> 1% of each run, Pallas kernels for 0% -> 2%
where the time goes in v1:
time: 118 us; the launch traced here: 117 us
  starting transfers between devices  54.5 us (46%)
  waiting for transfers between devices  35.7 us (30%)
  Pallas kernels  19.4 us (16%)
  local copies, waits for them, and re-layouts  4.37 us (4%)
  other arithmetic  2.7 us (2%)
    ppermute x18, starting transfers between devices, shift(): lax.ppermute(value, axis, [(i, (i + step) % size) for i in range(size)])  29.7 us
    ppermute x18, waiting for transfers between devices, shift(): lax.ppermute(value, axis, [(i, (i + step) % size) for i in range(size)])  18.1 us
    ppermute x28, starting transfers between devices, swap(): return lax.ppermute(value, axis, [(i, i ^ bit) for i in range(size)])  17.7 us
    pallas_call x1, Pallas kernels, shards(): pl.pallas_call(functools.partial(tile_kernel, (row_keys, col_keys), (NT,...  11.9 us
    ppermute x28, waiting for transfers between devices, swap(): return lax.ppermute(value, axis, [(i, i ^ bit) for i in range(size)])  11.6 us
    all_to_all x1, waiting for transfers between devices, shards(): lax.all_to_all(second, 'col', split_axis=0, concat_axis=0, tiled=True)  5.95 us
    all_to_all x1, starting transfers between devices, shards(): lax.all_to_all(sent, ('tm', 'col'), split_axis=0, concat_axis=0, tiled=True)  3.57 us
    all_to_all x1, starting transfers between devices, shards(): lax.all_to_all(second, 'col', split_axis=0, concat_axis=0, tiled=True)  3.54 us
  transfers between devices with their start and end apart: 48, of which 18 were waited for; matrix products, arithmetic and copies ran while one was open for 1% of the time, Pallas kernels for 2%

profile of v1, /device:TPU:0, one launch (start us, length us, event | category | flops | bytes accessed | tf_op | source)
XLA Modules:
  0.0 117.3 jit_solution(342024736330529947)
XLA Ops:
  0.0 0.9 constant_dynamic-slice_fusion.2
  0.9 3.0 %collective-permute-start.17 = (bf16[32,1024]{1,0:T(8,128)(2,1)S(1)}, bf16[32,1024]{1,0:T(8,128)(2,1)S(1)}, u32[]{:S(2)}, u32[]{:S(2)}) collective-permute-start(bf16[32,1024]{1,0:T(8,128)(2,1)S(1)} %get-tuple-element.11), channel_id=1, source_target_pairs={{0,16},{16,0},{1,17},{17,1},{2,18},{18,2},{3,19},{19,3},{4,20},{20... | collective-permute-start | bytes 196616 | tf_op jit(solution)/shard_map/ppermute | solution.py:29
  4.0 0.1 collective-permute-start.24
  4.1 4.1 %collective-permute-start.14 = (bf16[32,1024]{1,0:T(8,128)(2,1)S(1)}, bf16[32,1024]{1,0:T(8,128)(2,1)S(1)}, u32[]{:S(2)}, u32[]{:S(2)}) collective-permute-start(bf16[32,1024]{1,0:T(8,128)(2,1)S(1)} %get-tuple-element.12.refs_16_), channel_id=1, source_target_pairs={{0,12},{4,0},{8,4},{12,8},{1,13},{5,1},{9,5},{13,9},{2,14},{6,2},{... | collective-permute-start | bytes 196616 | tf_op jit(solution)/shard_map/ppermute | solution.py:34
  8.2 0.4 collective-permute-start.21
  8.7 1.6 %collective-permute-start.15 = (bf16[32,1024]{1,0:T(8,128)(2,1)S(1)}, bf16[32,1024]{1,0:T(8,128)(2,1)S(1)}, u32[]{:S(2)}, u32[]{:S(2)}) collective-permute-start(bf16[32,1024]{1,0:T(8,128)(2,1)S(1)} %get-tuple-element.12.refs_16_), channel_id=1, source_target_pairs={{0,4},{4,8},{8,12},{12,0},{1,5},{5,9},{9,13},{13,1},{2,6},{6,10},{... | collective-permute-start | bytes 196616 | tf_op jit(solution)/shard_map/ppermute | solution.py:34
  10.3 3.8 %collective-permute-start.18 = (bf16[32,1024]{1,0:T(8,128)(2,1)S(1)}, bf16[32,1024]{1,0:T(8,128)(2,1)S(1)}, u32[]{:S(2)}, u32[]{:S(2)}) collective-permute-start(bf16[32,1024]{1,0:T(8,128)(2,1)S(1)} %collective-permute-done.17.refs_20_), channel_id=1, source_target_pairs={{0,12},{4,0},{8,4},{12,8},{1,13},{5,1},{9,5},{13,9},{2,14},{6,2},{... | collective-permute-start | bytes 196616 | tf_op jit(solution)/shard_map/ppermute | solution.py:34
  14.1 0.9 collective-permute-start.25
  15.0 1.5 %collective-permute-start.7 = (bf16[64,1024]{1,0:T(8,128)(2,1)S(1)}, bf16[64,1024]{1,0:T(8,128)(2,1)S(1)}, u32[]{:S(2)}, u32[]{:S(2)}) collective-permute-start(bf16[64,1024]{1,0:T(8,128)(2,1)S(1)} %copy-done.2), channel_id=1, source_target_pairs={{0,16},{16,0},{1,17},{17,1},{2,18},{18,2},{3,19},{19,3},{4,20},{20... | collective-permute-start | bytes 393224 | tf_op jit(solution)/shard_map/ppermute | solution.py:29
  16.5 1.2 %collective-permute-start.16 = (bf16[32,1024]{1,0:T(8,128)(2,1)S(1)}, bf16[32,1024]{1,0:T(8,128)(2,1)S(1)}, u32[]{:S(2)}, u32[]{:S(2)}) collective-permute-start(bf16[32,1024]{1,0:T(8,128)(2,1)S(1)} %collective-permute-done.14.refs_17_), channel_id=1, source_target_pairs={{0,12},{4,0},{8,4},{12,8},{1,13},{5,1},{9,5},{13,9},{2,14},{6,2},{... | collective-permute-start | bytes 196616 | tf_op jit(solution)/shard_map/ppermute | solution.py:34
  17.7 2.0 %collective-permute-start.19 = (bf16[32,1024]{1,0:T(8,128)(2,1)S(1)}, bf16[32,1024]{1,0:T(8,128)(2,1)S(1)}, u32[]{:S(2)}, u32[]{:S(2)}) collective-permute-start(bf16[32,1024]{1,0:T(8,128)(2,1)S(1)} %collective-permute-done.17.refs_20_), channel_id=1, source_target_pairs={{0,4},{4,8},{8,12},{12,0},{1,5},{5,9},{9,13},{13,1},{2,6},{6,10},{... | collective-permute-start | bytes 196616 | tf_op jit(solution)/shard_map/ppermute | solution.py:34
  19.7 0.9 collective-permute-start.26
  20.6 0.9 collective-permute-done.16.refs_19_
  21.5 1.5 %collective-permute-start = (bf16[64,1024]{1,0:T(8,128)(2,1)S(1)}, bf16[64,1024]{1,0:T(8,128)(2,1)S(1)}, u32[]{:S(2)}, u32[]{:S(2)}) collective-permute-start(bf16[64,1024]{1,0:T(8,128)(2,1)S(1)} %copy-done.1), channel_id=1, source_target_pairs={{0,2},{1,3},{2,0},{3,1},{4,6},{5,7},{6,4},{7,5},{8,10},{9,11},{10,... | collective-permute-start | bytes 393224 | tf_op jit(solution)/shard_map/ppermute | solution.py:29
  23.0 1.4 %collective-permute-start.8 = (bf16[64,1024]{1,0:T(8,128)(2,1)S(1)}, bf16[64,1024]{1,0:T(8,128)(2,1)S(1)}, u32[]{:S(2)}, u32[]{:S(2)}) collective-permute-start(bf16[64,1024]{1,0:T(8,128)(2,1)S(1)} %copy-done.2), channel_id=1, source_target_pairs={{0,2},{1,3},{2,0},{3,1},{4,6},{5,7},{6,4},{7,5},{8,10},{9,11},{10,... | collective-permute-start | bytes 393224 | tf_op jit(solution)/shard_map/ppermute | solution.py:29
  24.4 0.5 collective-permute-start.1
  24.9 0.9 collective-permute-done.26.refs_30_
  25.8 0.5 collective-permute-start.3
  26.3 0.1 collective-permute-done.refs_1_
  26.4 1.5 %collective-permute-start.9 = (bf16[64,1024]{1,0:T(8,128)(2,1)S(1)}, bf16[64,1024]{1,0:T(8,128)(2,1)S(1)}, u32[]{:S(2)}, u32[]{:S(2)}) collective-permute-start(bf16[64,1024]{1,0:T(8,128)(2,1)S(1)} %collective-permute-done.7.refs_9_), channel_id=1, source_target_pairs={{0,2},{1,3},{2,0},{3,1},{4,6},{5,7},{6,4},{7,5},{8,10},{9,11},{10,... | collective-permute-start | bytes 393224 | tf_op jit(solution)/shard_map/ppermute | solution.py:29
  28.0 1.4 %collective-permute-done.1.refs_2_ = bf16[64,1024]{1,0:T(8,128)(2,1)S(1)} collective-permute-done((bf16[64,1024]{1,0:T(8,128)(2,1)S(1)}, bf16[64,1024]{1,0:T(8,128)(2,1)S(1)}, u32[]{:S(2)}, u32[]{:S(2)}) %collective-permute-start.1) | collective-permute-done | bytes 131104 | tf_op jit(solution)/shard_map/ppermute | solution.py:29
  29.4 1.8 %collective-permute-start.20 = (bf16[32,1024]{1,0:T(8,128)(2,1)S(1)}, bf16[32,1024]{1,0:T(8,128)(2,1)S(1)}, u32[]{:S(2)}, u32[]{:S(2)}) collective-permute-start(bf16[32,1024]{1,0:T(8,128)(2,1)S(1)} %collective-permute-done.18.refs_21_), channel_id=1, source_target_pairs={{0,12},{4,0},{8,4},{12,8},{1,13},{5,1},{9,5},{13,9},{2,14},{6,2},{... | collective-permute-start | bytes 196616 | tf_op jit(solution)/shard_map/ppermute | solution.py:34
  31.2 0.2 collective-permute-start.27
  31.4 1.3 %collective-permute-start.2 = (bf16[64,1024]{1,0:T(8,128)(2,1)S(1)}, bf16[64,1024]{1,0:T(8,128)(2,1)S(1)}, u32[]{:S(2)}, u32[]{:S(2)}) collective-permute-start(bf16[64,1024]{1,0:T(8,128)(2,1)S(1)} %collective-permute-done.refs_1_), channel_id=1, source_target_pairs={{0,16},{16,0},{1,17},{17,1},{2,18},{18,2},{3,19},{19,3},{4,20},{20... | collective-permute-start | bytes 393224 | tf_op jit(solution)/shard_map/ppermute | solution.py:29
  32.7 0.8 multiply_exponential_fusion.factors
  33.5 0.5 collective-permute-done.20.refs_23_
  34.0 1.5 %collective-permute-done.27.refs_31_ = bf16[32,1024]{1,0:T(8,128)(2,1)S(1)} collective-permute-done((bf16[32,1024]{1,0:T(8,128)(2,1)S(1)}, bf16[32,1024]{1,0:T(8,128)(2,1)S(1)}, u32[]{:S(2)}, u32[]{:S(2)}) %collective-permute-start.27) | collective-permute-done | bytes 65568 | tf_op jit(solution)/shard_map/ppermute | solution.py:34
  35.5 0.5 collective-permute-start.5
  36.0 0.4 collective-permute-done.2.refs_3_
  36.4 0.5 collective-permute-start.6
  36.9 0.7 fusion.cosine
  37.7 0.2 collective-permute-done.6.refs_7_
  38.1 0.1 copy-done.17
  38.4 0.6 copy-done.21
  39.0 11.9 %tile.1 = bf16[16,128,256]{2,1,0:T(8,128)(2,1)} custom-call(f32[16,16]{1,0:T(8,128)} %fusion.cosine, f32[2,16,2048]{2,1,0:T(8,128)} %multiply_exponential_fusion.factors, bf16[64,1024]{1,0:T(8,128)(2,1)} %refs_0_.2, bf16[64,1024]{1,0:T(8,128)(2,1)} %copy-done.9, bf16[64,1024]{1,0:T(8,128)(2,1)} %copy-done.11, bf16[64,1024]{1,0:T(8,128)(2,1)} %copy-done.16, ...), custom_call_target="tpu_custom_call" | custom-call | tf_op jit(solution)/shard_map/tile/pallas_call | solution.py:228
  51.0 3.6 %all-to-all-start = ((bf16[8,2,128,256]{3,2,1,0:T(8,128)(2,1)}), bf16[8,2,128,256]{3,2,1,0:T(8,128)(2,1)S(1)}, u32[]{:S(2)}, u32[]{:S(2)}) async-start(bf16[8,2,128,256]{3,2,1,0:T(8,128)(2,1)} %bitcast.8), calls=%async_computation | async-start | bytes 2097152 | tf_op jit(solution)/shard_map/all_to_all | solution.py:279
  54.6 2.4 %collective-permute-start.28 = (bf16[64,256]{1,0:T(8,128)(2,1)S(1)}, bf16[64,256]{1,0:T(8,128)(2,1)S(1)}, u32[]{:S(2)}, u32[]{:S(2)}) collective-permute-start(bf16[64,256]{1,0:T(8,128)(2,1)S(1)} %copy-done.22), channel_id=1, source_target_pairs={{0,12},{4,0},{8,4},{12,8},{1,13},{5,1},{9,5},{13,9},{2,14},{6,2},{... | collective-permute-start | bytes 98312 | tf_op jit(solution)/shard_map/ppermute | solution.py:34
  57.0 1.9 %collective-permute-start.31 = (bf16[64,256]{1,0:T(8,128)(2,1)S(1)}, bf16[64,256]{1,0:T(8,128)(2,1)S(1)}, u32[]{:S(2)}, u32[]{:S(2)}) collective-permute-start(bf16[64,256]{1,0:T(8,128)(2,1)S(1)} %copy-done.22), channel_id=1, source_target_pairs={{0,2},{1,3},{2,0},{3,1},{4,6},{5,7},{6,4},{7,5},{8,10},{9,11},{10,... | collective-permute-start | bytes 98312 | tf_op jit(solution)/shard_map/ppermute | solution.py:29
  58.8 3.9 %collective-permute-start.30 = (bf16[64,256]{1,0:T(8,128)(2,1)S(1)}, bf16[64,256]{1,0:T(8,128)(2,1)S(1)}, u32[]{:S(2)}, u32[]{:S(2)}) collective-permute-start(bf16[64,256]{1,0:T(8,128)(2,1)S(1)} %collective-permute-done.28.refs_1_), channel_id=1, source_target_pairs={{0,12},{4,0},{8,4},{12,8},{1,13},{5,1},{9,5},{13,9},{2,14},{6,2},{... | collective-permute-start | bytes 98312 | tf_op jit(solution)/shard_map/ppermute | solution.py:34
  62.7 1.8 %collective-permute-start.32 = (bf16[64,256]{1,0:T(8,128)(2,1)S(1)}, bf16[64,256]{1,0:T(8,128)(2,1)S(1)}, u32[]{:S(2)}, u32[]{:S(2)}) collective-permute-start(bf16[64,256]{1,0:T(8,128)(2,1)S(1)} %collective-permute-done.28.refs_1_), channel_id=1, source_target_pairs={{0,2},{1,3},{2,0},{3,1},{4,6},{5,7},{6,4},{7,5},{8,10},{9,11},{10,... | collective-permute-start | bytes 98312 | tf_op jit(solution)/shard_map/ppermute | solution.py:29
  64.5 0.2 collective-permute-start.33
  64.8 5.4 %collective-permute-done.31.refs_4_ = bf16[64,256]{1,0:T(8,128)(2,1)S(1)} collective-permute-done((bf16[64,256]{1,0:T(8,128)(2,1)S(1)}, bf16[64,256]{1,0:T(8,128)(2,1)S(1)}, u32[]{:S(2)}, u32[]{:S(2)}) %collective-permute-start.31) | collective-permute-done | bytes 32800 | tf_op jit(solution)/shard_map/ppermute | solution.py:29
  70.2 0.5 collective-permute-start.37
  70.8 0.1 collective-permute-start.39
  70.9 0.1 collective-permute-done.33.refs_6_
  71.0 0.3 collective-permute-start.38
  71.4 0.2 collective-permute-start.40
  71.6 0.3 collective-permute-start.41
  71.9 2.7 %collective-permute-done.34.refs_7_ = bf16[64,256]{1,0:T(8,128)(2,1)S(1)} collective-permute-done((bf16[64,256]{1,0:T(8,128)(2,1)S(1)}, bf16[64,256]{1,0:T(8,128)(2,1)S(1)}, u32[]{:S(2)}, u32[]{:S(2)}) %collective-permute-start.34) | collective-permute-done | bytes 32800 | tf_op jit(solution)/shard_map/ppermute | solution.py:29
  74.7 1.1 collective-permute-done.42.refs_15_
  76.0 0.6 copy-done.52
  76.6 2.1 %columns.1 = (bf16[256,1024]{1,0:T(8,128)(2,1)}, bf16[256,256]{1,0:T(8,128)(2,1)}) custom-call(bf16[64,256]{1,0:T(8,128)(2,1)} %refs_0_.3, bf16[64,256]{1,0:T(8,128)(2,1)} %copy-done.38, bf16[64,256]{1,0:T(8,128)(2,1)} %copy-done.39, bf16[64,256]{1,0:T(8,128)(2,1)} %copy-done.42, bf16[64,256]{1,0:T(8,128)(2,1)} %copy-done.40, bf16[64,256]{1,0:T(8,128)(2,1)} %copy-done.43, ...), custom_call_target="tpu_custom_call" | custom-call | tf_op jit(solution)/shard_map/columns/pallas_call | solution.py:251
  78.7 1.0 copy-done
  79.6 2.6 %first.1.refs_0_ = bf16[2,256,256]{2,1,0:T(8,128)(2,1)} custom-call(bf16[256,1024]{1,0:T(8,128)(2,1)} %get-tuple-element.7.all_columns, bf16[256,256]{1,0:T(8,128)(2,1)} %get-tuple-element.8.own, bf16[8,2,128,256]{3,2,1,0:T(8,128)(2,1)} %copy-done), custom_call_target="tpu_custom_call" | custom-call | tf_op jit(solution)/shard_map/first/pallas_call | solution.py:281
  82.2 2.3 %collective-permute-start.43 = (bf16[2,256,256]{2,1,0:T(8,128)(2,1)}, bf16[2,256,256]{2,1,0:T(8,128)(2,1)S(1)}, u32[]{:S(2)}, u32[]{:S(2)}) collective-permute-start(bf16[2,256,256]{2,1,0:T(8,128)(2,1)} %first.1.refs_0_), channel_id=1, source_target_pairs={{0,12},{4,0},{8,4},{12,8},{1,13},{5,1},{9,5},{13,9},{2,14},{6,2},{... | collective-permute-start | bytes 786440 | tf_op jit(solution)/shard_map/ppermute | solution.py:34
  84.6 7.1 %collective-permute-done.43.refs_1_ = bf16[2,256,256]{2,1,0:T(8,128)(2,1)S(1)} collective-permute-done((bf16[2,256,256]{2,1,0:T(8,128)(2,1)}, bf16[2,256,256]{2,1,0:T(8,128)(2,1)S(1)}, u32[]{:S(2)}, u32[]{:S(2)}) %collective-permute-start.43) | collective-permute-done | bytes 262176 | tf_op jit(solution)/shard_map/ppermute | solution.py:34
  91.6 4.2 %collective-permute-start.44 = (bf16[2,256,256]{2,1,0:T(8,128)(2,1)S(1)}, bf16[2,256,256]{2,1,0:T(8,128)(2,1)S(1)}, u32[]{:S(2)}, u32[]{:S(2)}) collective-permute-start(bf16[2,256,256]{2,1,0:T(8,128)(2,1)S(1)} %collective-permute-done.43.refs_1_), channel_id=1, source_target_pairs={{0,12},{4,0},{8,4},{12,8},{1,13},{5,1},{9,5},{13,9},{2,14},{6,2},{... | collective-permute-start | bytes 786440 | tf_op jit(solution)/shard_map/ppermute | solution.py:34
  95.8 2.5 %collective-permute-done.45.refs_3_ = bf16[2,256,256]{2,1,0:T(8,128)(2,1)S(1)} collective-permute-done((bf16[2,256,256]{2,1,0:T(8,128)(2,1)}, bf16[2,256,256]{2,1,0:T(8,128)(2,1)S(1)}, u32[]{:S(2)}, u32[]{:S(2)}) %collective-permute-start.45) | collective-permute-done | bytes 262176 | tf_op jit(solution)/shard_map/ppermute | solution.py:34
  98.3 4.8 %collective-permute-done.44.refs_2_ = bf16[2,256,256]{2,1,0:T(8,128)(2,1)S(1)} collective-permute-done((bf16[2,256,256]{2,1,0:T(8,128)(2,1)S(1)}, bf16[2,256,256]{2,1,0:T(8,128)(2,1)S(1)}, u32[]{:S(2)}, u32[]{:S(2)}) %collective-permute-start.44) | collective-permute-done | bytes 262176 | tf_op jit(solution)/shard_map/ppermute | solution.py:34
  103.1 0.7 copy-done.7
  103.8 2.8 %second.1 = bf16[4,2,64,256]{3,2,1,0:T(8,128)(2,1)} custom-call(bf16[8,2,128,256]{3,2,1,0:T(8,128)(2,1)} %copy-done, bf16[2,256,256]{2,1,0:T(8,128)(2,1)} %first.1.refs_0_, bf16[2,256,256]{2,1,0:T(8,128)(2,1)} %copy-done.5, bf16[2,256,256]{2,1,0:T(8,128)(2,1)} %copy-done.7, bf16[2,256,256]{2,1,0:T(8,128)(2,1)} %copy-done.6), custom_call_target="tpu_custom_call" | custom-call | tf_op jit(solution)/shard_map/second/pallas_call | solution.py:289
  106.6 3.5 %all-to-all-start.1 = ((bf16[4,2,64,256]{3,2,1,0:T(8,128)(2,1)}), bf16[4,2,64,256]{3,2,1,0:T(8,128)(2,1)S(1)}, u32[]{:S(2)}, u32[]{:S(2)}) async-start(bf16[4,2,64,256]{3,2,1,0:T(8,128)(2,1)} %second.1), calls=%async_computation.1 | async-start | bytes 524288 | tf_op jit(solution)/shard_map/all_to_all | solution.py:298
  110.2 5.9 %all-to-all-done.1 = bf16[4,2,64,256]{3,2,1,0:T(8,128)(2,1)S(1)} async-done(((bf16[4,2,64,256]{3,2,1,0:T(8,128)(2,1)}), bf16[4,2,64,256]{3,2,1,0:T(8,128)(2,1)S(1)}, u32[]{:S(2)}, u32[]{:S(2)}) %all-to-all-start.1) | async-done | bytes 262176 | tf_op jit(solution)/shard_map/all_to_all | solution.py:298
  116.2 1.1 copy_add_fusion
  (155 shorter events, 0.9 us)
Async XLA Ops:
  0.9 20.5 %copy-start.1 = (bf16[64,1024]{1,0:T(8,128)(2,1)S(1)}, bf16[64,1024]{1,0:T(8,128)(2,1)}, u32[]{:S(2)}) copy-start(bf16[64,1024]{1,0:T(8,128)(2,1)} %refs_0_.2) | copy-start | bytes 393220
  0.9 9.3 %collective-permute-start.17 = (bf16[32,1024]{1,0:T(8,128)(2,1)S(1)}, bf16[32,1024]{1,0:T(8,128)(2,1)S(1)}, u32[]{:S(2)}, u32[]{:S(2)}) collective-permute-start(bf16[32,1024]{1,0:T(8,128)(2,1)S(1)} %get-tuple-element.11), channel_id=1, source_target_pairs={{0,16},{16,0},{1,17},{17,1},{2,18},{18,2},{3,19},{19,3},{4,20},{20... | collective-permute-start | bytes 196616 | tf_op jit(solution)/shard_map/ppermute | solution.py:29
  4.0 22.3 %copy-start.54 = (f32[2048]{0:T(1024)S(1)}, f32[2048]{0:T(1024)}, u32[]{:S(2)}) copy-start(f32[2048]{0:T(1024)} %param.7) | copy-start | bytes 24580
  4.0 29.5 %copy-start.4 = (bf16[32,1024]{1,0:T(8,128)(2,1)}, bf16[32,1024]{1,0:T(8,128)(2,1)S(1)}, u32[]{:S(2)}) copy-start(bf16[32,1024]{1,0:T(8,128)(2,1)S(1)} %get-tuple-element.10.refs_24_) | copy-start | bytes 196612
  4.0 22.3 %copy-start.53 = (f32[2048]{0:T(1024)S(1)}, f32[2048]{0:T(1024)}, u32[]{:S(2)}) copy-start(f32[2048]{0:T(1024)} %param.8) | copy-start | bytes 24580
  4.0 6.3 %collective-permute-start.24 = (bf16[32,1024]{1,0:T(8,128)(2,1)S(1)}, bf16[32,1024]{1,0:T(8,128)(2,1)S(1)}, u32[]{:S(2)}, u32[]{:S(2)}) collective-permute-start(bf16[32,1024]{1,0:T(8,128)(2,1)S(1)} %get-tuple-element.9), channel_id=1, source_target_pairs={{0,16},{16,0},{1,17},{17,1},{2,18},{18,2},{3,19},{19,3},{4,20},{20... | collective-permute-start | bytes 196616 | tf_op jit(solution)/shard_map/ppermute | solution.py:29
  4.1 10.0 %collective-permute-start.14 = (bf16[32,1024]{1,0:T(8,128)(2,1)S(1)}, bf16[32,1024]{1,0:T(8,128)(2,1)S(1)}, u32[]{:S(2)}, u32[]{:S(2)}) collective-permute-start(bf16[32,1024]{1,0:T(8,128)(2,1)S(1)} %get-tuple-element.12.refs_16_), channel_id=1, source_target_pairs={{0,12},{4,0},{8,4},{12,8},{1,13},{5,1},{9,5},{13,9},{2,14},{6,2},{... | collective-permute-start | bytes 196616 | tf_op jit(solution)/shard_map/ppermute | solution.py:34
  8.2 6.8 %collective-permute-start.21 = (bf16[32,1024]{1,0:T(8,128)(2,1)S(1)}, bf16[32,1024]{1,0:T(8,128)(2,1)S(1)}, u32[]{:S(2)}, u32[]{:S(2)}) collective-permute-start(bf16[32,1024]{1,0:T(8,128)(2,1)S(1)} %get-tuple-element.10.refs_24_), channel_id=1, source_target_pairs={{0,12},{4,0},{8,4},{12,8},{1,13},{5,1},{9,5},{13,9},{2,14},{6,2},{... | collective-permute-start | bytes 196616 | tf_op jit(solution)/shard_map/ppermute | solution.py:34
  8.7 7.8 %collective-permute-start.15 = (bf16[32,1024]{1,0:T(8,128)(2,1)S(1)}, bf16[32,1024]{1,0:T(8,128)(2,1)S(1)}, u32[]{:S(2)}, u32[]{:S(2)}) collective-permute-start(bf16[32,1024]{1,0:T(8,128)(2,1)S(1)} %get-tuple-element.12.refs_16_), channel_id=1, source_target_pairs={{0,4},{4,8},{8,12},{12,0},{1,5},{5,9},{9,13},{13,1},{2,6},{6,10},{... | collective-permute-start | bytes 196616 | tf_op jit(solution)/shard_map/ppermute | solution.py:34
  10.3 27.6 %copy-start.24 = (bf16[32,1024]{1,0:T(8,128)(2,1)}, bf16[32,1024]{1,0:T(8,128)(2,1)S(1)}, u32[]{:S(2)}) copy-start(bf16[32,1024]{1,0:T(8,128)(2,1)S(1)} %collective-permute-done.17.refs_20_) | copy-start | bytes 196612
  10.3 7.4 %collective-permute-start.22 = (bf16[32,1024]{1,0:T(8,128)(2,1)S(1)}, bf16[32,1024]{1,0:T(8,128)(2,1)S(1)}, u32[]{:S(2)}, u32[]{:S(2)}) collective-permute-start(bf16[32,1024]{1,0:T(8,128)(2,1)S(1)} %get-tuple-element.10.refs_24_), channel_id=1, source_target_pairs={{0,4},{4,8},{8,12},{12,0},{1,5},{5,9},{9,13},{13,1},{2,6},{6,10},{... | collective-permute-start | bytes 196616 | tf_op jit(solution)/shard_map/ppermute | solution.py:34
  10.3 27.6 %copy-start.25 = (bf16[32,1024]{1,0:T(8,128)(2,1)}, bf16[32,1024]{1,0:T(8,128)(2,1)S(1)}, u32[]{:S(2)}) copy-start(bf16[32,1024]{1,0:T(8,128)(2,1)S(1)} %collective-permute-done.24.refs_28_) | copy-start | bytes 196612
  10.3 7.4 %collective-permute-start.18 = (bf16[32,1024]{1,0:T(8,128)(2,1)S(1)}, bf16[32,1024]{1,0:T(8,128)(2,1)S(1)}, u32[]{:S(2)}, u32[]{:S(2)}) collective-permute-start(bf16[32,1024]{1,0:T(8,128)(2,1)S(1)} %collective-permute-done.17.refs_20_), channel_id=1, source_target_pairs={{0,12},{4,0},{8,4},{12,8},{1,13},{5,1},{9,5},{13,9},{2,14},{6,2},{... | collective-permute-start | bytes 196616 | tf_op jit(solution)/shard_map/ppermute | solution.py:34
  14.1 23.8 %copy-start.26 = (bf16[32,1024]{1,0:T(8,128)(2,1)}, bf16[32,1024]{1,0:T(8,128)(2,1)S(1)}, u32[]{:S(2)}) copy-start(bf16[32,1024]{1,0:T(8,128)(2,1)S(1)} %collective-permute-done.14.refs_17_) | copy-start | bytes 196612
  14.1 5.6 %collective-permute-start.25 = (bf16[32,1024]{1,0:T(8,128)(2,1)S(1)}, bf16[32,1024]{1,0:T(8,128)(2,1)S(1)}, u32[]{:S(2)}, u32[]{:S(2)}) collective-permute-start(bf16[32,1024]{1,0:T(8,128)(2,1)S(1)} %collective-permute-done.24.refs_28_), channel_id=1, source_target_pairs={{0,12},{4,0},{8,4},{12,8},{1,13},{5,1},{9,5},{13,9},{2,14},{6,2},{... | collective-permute-start | bytes 196616 | tf_op jit(solution)/shard_map/ppermute | solution.py:34
  15.0 22.9 %copy-start.27 = (bf16[32,1024]{1,0:T(8,128)(2,1)}, bf16[32,1024]{1,0:T(8,128)(2,1)S(1)}, u32[]{:S(2)}) copy-start(bf16[32,1024]{1,0:T(8,128)(2,1)S(1)} %collective-permute-done.21.refs_25_) | copy-start | bytes 196612
  15.0 10.8 %collective-permute-start.7 = (bf16[64,1024]{1,0:T(8,128)(2,1)S(1)}, bf16[64,1024]{1,0:T(8,128)(2,1)S(1)}, u32[]{:S(2)}, u32[]{:S(2)}) collective-permute-start(bf16[64,1024]{1,0:T(8,128)(2,1)S(1)} %copy-done.2), channel_id=1, source_target_pairs={{0,16},{16,0},{1,17},{17,1},{2,18},{18,2},{3,19},{19,3},{4,20},{20... | collective-permute-start | bytes 393224 | tf_op jit(solution)/shard_map/ppermute | solution.py:29
  16.5 21.4 %copy-start.28 = (bf16[32,1024]{1,0:T(8,128)(2,1)}, bf16[32,1024]{1,0:T(8,128)(2,1)S(1)}, u32[]{:S(2)}) copy-start(bf16[32,1024]{1,0:T(8,128)(2,1)S(1)} %collective-permute-done.15.refs_18_) | copy-start | bytes 196612
  16.5 5.0 %collective-permute-start.16 = (bf16[32,1024]{1,0:T(8,128)(2,1)S(1)}, bf16[32,1024]{1,0:T(8,128)(2,1)S(1)}, u32[]{:S(2)}, u32[]{:S(2)}) collective-permute-start(bf16[32,1024]{1,0:T(8,128)(2,1)S(1)} %collective-permute-done.14.refs_17_), channel_id=1, source_target_pairs={{0,12},{4,0},{8,4},{12,8},{1,13},{5,1},{9,5},{13,9},{2,14},{6,2},{... | collective-permute-start | bytes 196616 | tf_op jit(solution)/shard_map/ppermute | solution.py:34
  17.7 20.3 %copy-start.29 = (bf16[32,1024]{1,0:T(8,128)(2,1)}, bf16[32,1024]{1,0:T(8,128)(2,1)S(1)}, u32[]{:S(2)}) copy-start(bf16[32,1024]{1,0:T(8,128)(2,1)S(1)} %collective-permute-done.22.refs_26_) | copy-start | bytes 196612
  17.7 5.3 %collective-permute-start.23 = (bf16[32,1024]{1,0:T(8,128)(2,1)S(1)}, bf16[32,1024]{1,0:T(8,128)(2,1)S(1)}, u32[]{:S(2)}, u32[]{:S(2)}) collective-permute-start(bf16[32,1024]{1,0:T(8,128)(2,1)S(1)} %collective-permute-done.21.refs_25_), channel_id=1, source_target_pairs={{0,12},{4,0},{8,4},{12,8},{1,13},{5,1},{9,5},{13,9},{2,14},{6,2},{... | collective-permute-start | bytes 196616 | tf_op jit(solution)/shard_map/ppermute | solution.py:34
  17.7 20.2 %copy-start.30 = (bf16[32,1024]{1,0:T(8,128)(2,1)}, bf16[32,1024]{1,0:T(8,128)(2,1)S(1)}, u32[]{:S(2)}) copy-start(bf16[32,1024]{1,0:T(8,128)(2,1)S(1)} %collective-permute-done.18.refs_21_) | copy-start | bytes 196612
  17.7 6.6 %collective-permute-start.19 = (bf16[32,1024]{1,0:T(8,128)(2,1)S(1)}, bf16[32,1024]{1,0:T(8,128)(2,1)S(1)}, u32[]{:S(2)}, u32[]{:S(2)}) collective-permute-start(bf16[32,1024]{1,0:T(8,128)(2,1)S(1)} %collective-permute-done.17.refs_20_), channel_id=1, source_target_pairs={{0,4},{4,8},{8,12},{12,0},{1,5},{5,9},{9,13},{13,1},{2,6},{6,10},{... | collective-permute-start | bytes 196616 | tf_op jit(solution)/shard_map/ppermute | solution.py:34
  19.7 18.2 %copy-start.31 = (bf16[32,1024]{1,0:T(8,128)(2,1)}, bf16[32,1024]{1,0:T(8,128)(2,1)S(1)}, u32[]{:S(2)}) copy-start(bf16[32,1024]{1,0:T(8,128)(2,1)S(1)} %collective-permute-done.25.refs_29_) | copy-start | bytes 196612
  19.7 6.1 %collective-permute-start.26 = (bf16[32,1024]{1,0:T(8,128)(2,1)S(1)}, bf16[32,1024]{1,0:T(8,128)(2,1)S(1)}, u32[]{:S(2)}, u32[]{:S(2)}) collective-permute-start(bf16[32,1024]{1,0:T(8,128)(2,1)S(1)} %collective-permute-done.24.refs_28_), channel_id=1, source_target_pairs={{0,4},{4,8},{8,12},{12,0},{1,5},{5,9},{9,13},{13,1},{2,6},{6,10},{... | collective-permute-start | bytes 196616 | tf_op jit(solution)/shard_map/ppermute | solution.py:34
  21.5 16.5 %copy-start.32 = (bf16[32,1024]{1,0:T(8,128)(2,1)}, bf16[32,1024]{1,0:T(8,128)(2,1)S(1)}, u32[]{:S(2)}) copy-start(bf16[32,1024]{1,0:T(8,128)(2,1)S(1)} %collective-permute-done.16.refs_19_) | copy-start | bytes 196612
  21.5 5.0 %collective-permute-start = (bf16[64,1024]{1,0:T(8,128)(2,1)S(1)}, bf16[64,1024]{1,0:T(8,128)(2,1)S(1)}, u32[]{:S(2)}, u32[]{:S(2)}) collective-permute-start(bf16[64,1024]{1,0:T(8,128)(2,1)S(1)} %copy-done.1), channel_id=1, source_target_pairs={{0,2},{1,3},{2,0},{3,1},{4,6},{5,7},{6,4},{7,5},{8,10},{9,11},{10,... | collective-permute-start | bytes 393224 | tf_op jit(solution)/shard_map/ppermute | solution.py:29
  23.0 15.0 %copy-start.33 = (bf16[32,1024]{1,0:T(8,128)(2,1)}, bf16[32,1024]{1,0:T(8,128)(2,1)S(1)}, u32[]{:S(2)}) copy-start(bf16[32,1024]{1,0:T(8,128)(2,1)S(1)} %collective-permute-done.23.refs_27_) | copy-start | bytes 196612
  23.0 5.0 %collective-permute-start.8 = (bf16[64,1024]{1,0:T(8,128)(2,1)S(1)}, bf16[64,1024]{1,0:T(8,128)(2,1)S(1)}, u32[]{:S(2)}, u32[]{:S(2)}) collective-permute-start(bf16[64,1024]{1,0:T(8,128)(2,1)S(1)} %copy-done.2), channel_id=1, source_target_pairs={{0,2},{1,3},{2,0},{3,1},{4,6},{5,7},{6,4},{7,5},{8,10},{9,11},{10,... | collective-permute-start | bytes 393224 | tf_op jit(solution)/shard_map/ppermute | solution.py:29
  24.4 13.6 %copy-start.34 = (bf16[32,1024]{1,0:T(8,128)(2,1)}, bf16[32,1024]{1,0:T(8,128)(2,1)S(1)}, u32[]{:S(2)}) copy-start(bf16[32,1024]{1,0:T(8,128)(2,1)S(1)} %collective-permute-done.19.refs_22_) | copy-start | bytes 196612
  24.4 5.0 %collective-permute-start.1 = (bf16[64,1024]{1,0:T(8,128)(2,1)S(1)}, bf16[64,1024]{1,0:T(8,128)(2,1)S(1)}, u32[]{:S(2)}, u32[]{:S(2)}) collective-permute-start(bf16[64,1024]{1,0:T(8,128)(2,1)S(1)} %copy-done.1), channel_id=1, source_target_pairs={{0,16},{16,0},{1,17},{17,1},{2,18},{18,2},{3,19},{19,3},{4,20},{20... | collective-permute-start | bytes 393224 | tf_op jit(solution)/shard_map/ppermute | solution.py:29
  25.8 5.4 %collective-permute-start.10 = (bf16[64,1024]{1,0:T(8,128)(2,1)S(1)}, bf16[64,1024]{1,0:T(8,128)(2,1)S(1)}, u32[]{:S(2)}, u32[]{:S(2)}) collective-permute-start(bf16[64,1024]{1,0:T(8,128)(2,1)S(1)} %copy-done.2), channel_id=1, source_target_pairs={{0,1},{1,0},{2,3},{3,2},{4,5},{5,4},{6,7},{7,6},{8,9},{9,8},{10,11... | collective-permute-start | bytes 393224 | tf_op jit(solution)/shard_map/ppermute | solution.py:29
  25.8 5.6 %collective-permute-start.3 = (bf16[64,1024]{1,0:T(8,128)(2,1)S(1)}, bf16[64,1024]{1,0:T(8,128)(2,1)S(1)}, u32[]{:S(2)}, u32[]{:S(2)}) collective-permute-start(bf16[64,1024]{1,0:T(8,128)(2,1)S(1)} %copy-done.1), channel_id=1, source_target_pairs={{0,1},{1,0},{2,3},{3,2},{4,5},{5,4},{6,7},{7,6},{8,9},{9,8},{10,11... | collective-permute-start | bytes 393224 | tf_op jit(solution)/shard_map/ppermute | solution.py:29
  26.4 9.0 %collective-permute-start.9 = (bf16[64,1024]{1,0:T(8,128)(2,1)S(1)}, bf16[64,1024]{1,0:T(8,128)(2,1)S(1)}, u32[]{:S(2)}, u32[]{:S(2)}) collective-permute-start(bf16[64,1024]{1,0:T(8,128)(2,1)S(1)} %collective-permute-done.7.refs_9_), channel_id=1, source_target_pairs={{0,2},{1,3},{2,0},{3,1},{4,6},{5,7},{6,4},{7,5},{8,10},{9,11},{10,... | collective-permute-start | bytes 393224 | tf_op jit(solution)/shard_map/ppermute | solution.py:29
  28.0 8.4 %collective-permute-start.11 = (bf16[64,1024]{1,0:T(8,128)(2,1)S(1)}, bf16[64,1024]{1,0:T(8,128)(2,1)S(1)}, u32[]{:S(2)}, u32[]{:S(2)}) collective-permute-start(bf16[64,1024]{1,0:T(8,128)(2,1)S(1)} %collective-permute-done.7.refs_9_), channel_id=1, source_target_pairs={{0,1},{1,0},{2,3},{3,2},{4,5},{5,4},{6,7},{7,6},{8,9},{9,8},{10,11... | collective-permute-start | bytes 393224 | tf_op jit(solution)/shard_map/ppermute | solution.py:29
  29.4 4.6 %collective-permute-start.20 = (bf16[32,1024]{1,0:T(8,128)(2,1)S(1)}, bf16[32,1024]{1,0:T(8,128)(2,1)S(1)}, u32[]{:S(2)}, u32[]{:S(2)}) collective-permute-start(bf16[32,1024]{1,0:T(8,128)(2,1)S(1)} %collective-permute-done.18.refs_21_), channel_id=1, source_target_pairs={{0,12},{4,0},{8,4},{12,8},{1,13},{5,1},{9,5},{13,9},{2,14},{6,2},{... | collective-permute-start | bytes 196616 | tf_op jit(solution)/shard_map/ppermute | solution.py:34
  31.2 4.3 %collective-permute-start.27 = (bf16[32,1024]{1,0:T(8,128)(2,1)S(1)}, bf16[32,1024]{1,0:T(8,128)(2,1)S(1)}, u32[]{:S(2)}, u32[]{:S(2)}) collective-permute-start(bf16[32,1024]{1,0:T(8,128)(2,1)S(1)} %collective-permute-done.25.refs_29_), channel_id=1, source_target_pairs={{0,12},{4,0},{8,4},{12,8},{1,13},{5,1},{9,5},{13,9},{2,14},{6,2},{... | collective-permute-start | bytes 196616 | tf_op jit(solution)/shard_map/ppermute | solution.py:34
  31.4 5.0 %collective-permute-start.2 = (bf16[64,1024]{1,0:T(8,128)(2,1)S(1)}, bf16[64,1024]{1,0:T(8,128)(2,1)S(1)}, u32[]{:S(2)}, u32[]{:S(2)}) collective-permute-start(bf16[64,1024]{1,0:T(8,128)(2,1)S(1)} %collective-permute-done.refs_1_), channel_id=1, source_target_pairs={{0,16},{16,0},{1,17},{17,1},{2,18},{18,2},{3,19},{19,3},{4,20},{20... | collective-permute-start | bytes 393224 | tf_op jit(solution)/shard_map/ppermute | solution.py:29
  34.0 3.6 %collective-permute-start.4 = (bf16[64,1024]{1,0:T(8,128)(2,1)S(1)}, bf16[64,1024]{1,0:T(8,128)(2,1)S(1)}, u32[]{:S(2)}, u32[]{:S(2)}) collective-permute-start(bf16[64,1024]{1,0:T(8,128)(2,1)S(1)} %collective-permute-done.refs_1_), channel_id=1, source_target_pairs={{0,1},{1,0},{2,3},{3,2},{4,5},{5,4},{6,7},{7,6},{8,9},{9,8},{10,11... | collective-permute-start | bytes 393224 | tf_op jit(solution)/shard_map/ppermute | solution.py:29
  35.5 2.1 %collective-permute-start.12 = (bf16[64,1024]{1,0:T(8,128)(2,1)S(1)}, bf16[64,1024]{1,0:T(8,128)(2,1)S(1)}, u32[]{:S(2)}, u32[]{:S(2)}) collective-permute-start(bf16[64,1024]{1,0:T(8,128)(2,1)S(1)} %collective-permute-done.8.refs_10_), channel_id=1, source_target_pairs={{0,1},{1,0},{2,3},{3,2},{4,5},{5,4},{6,7},{7,6},{8,9},{9,8},{10,11... | collective-permute-start | bytes 393224 | tf_op jit(solution)/shard_map/ppermute | solution.py:29
  35.5 2.1 %collective-permute-start.5 = (bf16[64,1024]{1,0:T(8,128)(2,1)S(1)}, bf16[64,1024]{1,0:T(8,128)(2,1)S(1)}, u32[]{:S(2)}, u32[]{:S(2)}) collective-permute-start(bf16[64,1024]{1,0:T(8,128)(2,1)S(1)} %collective-permute-done.1.refs_2_), channel_id=1, source_target_pairs={{0,1},{1,0},{2,3},{3,2},{4,5},{5,4},{6,7},{7,6},{8,9},{9,8},{10,11... | collective-permute-start | bytes 393224 | tf_op jit(solution)/shard_map/ppermute | solution.py:29
  36.4 1.3 %collective-permute-start.13 = (bf16[64,1024]{1,0:T(8,128)(2,1)S(1)}, bf16[64,1024]{1,0:T(8,128)(2,1)S(1)}, u32[]{:S(2)}, u32[]{:S(2)}) collective-permute-start(bf16[64,1024]{1,0:T(8,128)(2,1)S(1)} %collective-permute-done.9.refs_11_), channel_id=1, source_target_pairs={{0,1},{1,0},{2,3},{3,2},{4,5},{5,4},{6,7},{7,6},{8,9},{9,8},{10,11... | collective-permute-start | bytes 393224 | tf_op jit(solution)/shard_map/ppermute | solution.py:29
  36.4 1.5 %collective-permute-start.6 = (bf16[64,1024]{1,0:T(8,128)(2,1)S(1)}, bf16[64,1024]{1,0:T(8,128)(2,1)S(1)}, u32[]{:S(2)}, u32[]{:S(2)}) collective-permute-start(bf16[64,1024]{1,0:T(8,128)(2,1)S(1)} %collective-permute-done.2.refs_3_), channel_id=1, source_target_pairs={{0,1},{1,0},{2,3},{3,2},{4,5},{5,4},{6,7},{7,6},{8,9},{9,8},{10,11... | collective-permute-start | bytes 393224 | tf_op jit(solution)/shard_map/ppermute | solution.py:29
  51.0 27.7 %all-to-all-start = ((bf16[8,2,128,256]{3,2,1,0:T(8,128)(2,1)}), bf16[8,2,128,256]{3,2,1,0:T(8,128)(2,1)S(1)}, u32[]{:S(2)}, u32[]{:S(2)}) async-start(bf16[8,2,128,256]{3,2,1,0:T(8,128)(2,1)} %bitcast.8), calls=%async_computation | async-start | bytes 2097152 | tf_op jit(solution)/shard_map/all_to_all | solution.py:279
  54.6 4.3 %collective-permute-start.28 = (bf16[64,256]{1,0:T(8,128)(2,1)S(1)}, bf16[64,256]{1,0:T(8,128)(2,1)S(1)}, u32[]{:S(2)}, u32[]{:S(2)}) collective-permute-start(bf16[64,256]{1,0:T(8,128)(2,1)S(1)} %copy-done.22), channel_id=1, source_target_pairs={{0,12},{4,0},{8,4},{12,8},{1,13},{5,1},{9,5},{13,9},{2,14},{6,2},{... | collective-permute-start | bytes 98312 | tf_op jit(solution)/shard_map/ppermute | solution.py:34
  57.0 7.6 %collective-permute-start.29 = (bf16[64,256]{1,0:T(8,128)(2,1)S(1)}, bf16[64,256]{1,0:T(8,128)(2,1)S(1)}, u32[]{:S(2)}, u32[]{:S(2)}) collective-permute-start(bf16[64,256]{1,0:T(8,128)(2,1)S(1)} %copy-done.22), channel_id=1, source_target_pairs={{0,4},{4,8},{8,12},{12,0},{1,5},{5,9},{9,13},{13,1},{2,6},{6,10},{... | collective-permute-start | bytes 98312 | tf_op jit(solution)/shard_map/ppermute | solution.py:34
  57.0 13.2 %collective-permute-start.31 = (bf16[64,256]{1,0:T(8,128)(2,1)S(1)}, bf16[64,256]{1,0:T(8,128)(2,1)S(1)}, u32[]{:S(2)}, u32[]{:S(2)}) collective-permute-start(bf16[64,256]{1,0:T(8,128)(2,1)S(1)} %copy-done.22), channel_id=1, source_target_pairs={{0,2},{1,3},{2,0},{3,1},{4,6},{5,7},{6,4},{7,5},{8,10},{9,11},{10,... | collective-permute-start | bytes 98312 | tf_op jit(solution)/shard_map/ppermute | solution.py:29
  58.8 11.4 %collective-permute-start.35 = (bf16[64,256]{1,0:T(8,128)(2,1)S(1)}, bf16[64,256]{1,0:T(8,128)(2,1)S(1)}, u32[]{:S(2)}, u32[]{:S(2)}) collective-permute-start(bf16[64,256]{1,0:T(8,128)(2,1)S(1)} %copy-done.22), channel_id=1, source_target_pairs={{0,1},{1,0},{2,3},{3,2},{4,5},{5,4},{6,7},{7,6},{8,9},{9,8},{10,11... | collective-permute-start | bytes 98312 | tf_op jit(solution)/shard_map/ppermute | solution.py:29
  58.8 17.0 %copy-start.38 = (bf16[64,256]{1,0:T(8,128)(2,1)}, bf16[64,256]{1,0:T(8,128)(2,1)S(1)}, u32[]{:S(2)}) copy-start(bf16[64,256]{1,0:T(8,128)(2,1)S(1)} %collective-permute-done.28.refs_1_) | copy-start | bytes 98308
  58.8 11.9 %collective-permute-start.30 = (bf16[64,256]{1,0:T(8,128)(2,1)S(1)}, bf16[64,256]{1,0:T(8,128)(2,1)S(1)}, u32[]{:S(2)}, u32[]{:S(2)}) collective-permute-start(bf16[64,256]{1,0:T(8,128)(2,1)S(1)} %collective-permute-done.28.refs_1_), channel_id=1, source_target_pairs={{0,12},{4,0},{8,4},{12,8},{1,13},{5,1},{9,5},{13,9},{2,14},{6,2},{... | collective-permute-start | bytes 98312 | tf_op jit(solution)/shard_map/ppermute | solution.py:34
  62.7 8.0 %collective-permute-start.32 = (bf16[64,256]{1,0:T(8,128)(2,1)S(1)}, bf16[64,256]{1,0:T(8,128)(2,1)S(1)}, u32[]{:S(2)}, u32[]{:S(2)}) collective-permute-start(bf16[64,256]{1,0:T(8,128)(2,1)S(1)} %collective-permute-done.28.refs_1_), channel_id=1, source_target_pairs={{0,2},{1,3},{2,0},{3,1},{4,6},{5,7},{6,4},{7,5},{8,10},{9,11},{10,... | collective-permute-start | bytes 98312 | tf_op jit(solution)/shard_map/ppermute | solution.py:29
  64.5 6.5 %collective-permute-start.33 = (bf16[64,256]{1,0:T(8,128)(2,1)S(1)}, bf16[64,256]{1,0:T(8,128)(2,1)S(1)}, u32[]{:S(2)}, u32[]{:S(2)}) collective-permute-start(bf16[64,256]{1,0:T(8,128)(2,1)S(1)} %collective-permute-done.29.refs_2_), channel_id=1, source_target_pairs={{0,2},{1,3},{2,0},{3,1},{4,6},{5,7},{6,4},{7,5},{8,10},{9,11},{10,... | collective-permute-start | bytes 98312 | tf_op jit(solution)/shard_map/ppermute | solution.py:29
  70.2 1.2 %collective-permute-start.36 = (bf16[64,256]{1,0:T(8,128)(2,1)S(1)}, bf16[64,256]{1,0:T(8,128)(2,1)S(1)}, u32[]{:S(2)}, u32[]{:S(2)}) collective-permute-start(bf16[64,256]{1,0:T(8,128)(2,1)S(1)} %collective-permute-done.28.refs_1_), channel_id=1, source_target_pairs={{0,1},{1,0},{2,3},{3,2},{4,5},{5,4},{6,7},{7,6},{8,9},{9,8},{10,11... | collective-permute-start | bytes 98312 | tf_op jit(solution)/shard_map/ppermute | solution.py:29
  70.2 1.4 %collective-permute-start.37 = (bf16[64,256]{1,0:T(8,128)(2,1)S(1)}, bf16[64,256]{1,0:T(8,128)(2,1)S(1)}, u32[]{:S(2)}, u32[]{:S(2)}) collective-permute-start(bf16[64,256]{1,0:T(8,128)(2,1)S(1)} %collective-permute-done.29.refs_2_), channel_id=1, source_target_pairs={{0,1},{1,0},{2,3},{3,2},{4,5},{5,4},{6,7},{7,6},{8,9},{9,8},{10,11... | collective-permute-start | bytes 98312 | tf_op jit(solution)/shard_map/ppermute | solution.py:29
  70.7 3.9 %collective-permute-start.34 = (bf16[64,256]{1,0:T(8,128)(2,1)S(1)}, bf16[64,256]{1,0:T(8,128)(2,1)S(1)}, u32[]{:S(2)}, u32[]{:S(2)}) collective-permute-start(bf16[64,256]{1,0:T(8,128)(2,1)S(1)} %collective-permute-done.30.refs_3_), channel_id=1, source_target_pairs={{0,2},{1,3},{2,0},{3,1},{4,6},{5,7},{6,4},{7,5},{8,10},{9,11},{10,... | collective-permute-start | bytes 98312 | tf_op jit(solution)/shard_map/ppermute | solution.py:29
  70.8 3.9 %collective-permute-start.39 = (bf16[64,256]{1,0:T(8,128)(2,1)S(1)}, bf16[64,256]{1,0:T(8,128)(2,1)S(1)}, u32[]{:S(2)}, u32[]{:S(2)}) collective-permute-start(bf16[64,256]{1,0:T(8,128)(2,1)S(1)} %collective-permute-done.31.refs_4_), channel_id=1, source_target_pairs={{0,1},{1,0},{2,3},{3,2},{4,5},{5,4},{6,7},{7,6},{8,9},{9,8},{10,11... | collective-permute-start | bytes 98312 | tf_op jit(solution)/shard_map/ppermute | solution.py:29
  71.0 3.6 %collective-permute-start.38 = (bf16[64,256]{1,0:T(8,128)(2,1)S(1)}, bf16[64,256]{1,0:T(8,128)(2,1)S(1)}, u32[]{:S(2)}, u32[]{:S(2)}) collective-permute-start(bf16[64,256]{1,0:T(8,128)(2,1)S(1)} %collective-permute-done.30.refs_3_), channel_id=1, source_target_pairs={{0,1},{1,0},{2,3},{3,2},{4,5},{5,4},{6,7},{7,6},{8,9},{9,8},{10,11... | collective-permute-start | bytes 98312 | tf_op jit(solution)/shard_map/ppermute | solution.py:29
  71.4 3.3 %collective-permute-start.40 = (bf16[64,256]{1,0:T(8,128)(2,1)S(1)}, bf16[64,256]{1,0:T(8,128)(2,1)S(1)}, u32[]{:S(2)}, u32[]{:S(2)}) collective-permute-start(bf16[64,256]{1,0:T(8,128)(2,1)S(1)} %collective-permute-done.32.refs_5_), channel_id=1, source_target_pairs={{0,1},{1,0},{2,3},{3,2},{4,5},{5,4},{6,7},{7,6},{8,9},{9,8},{10,11... | collective-permute-start | bytes 98312 | tf_op jit(solution)/shard_map/ppermute | solution.py:29
  71.6 3.1 %collective-permute-start.41 = (bf16[64,256]{1,0:T(8,128)(2,1)S(1)}, bf16[64,256]{1,0:T(8,128)(2,1)S(1)}, u32[]{:S(2)}, u32[]{:S(2)}) collective-permute-start(bf16[64,256]{1,0:T(8,128)(2,1)S(1)} %collective-permute-done.33.refs_6_), channel_id=1, source_target_pairs={{0,1},{1,0},{2,3},{3,2},{4,5},{5,4},{6,7},{7,6},{8,9},{9,8},{10,11... | collective-permute-start | bytes 98312 | tf_op jit(solution)/shard_map/ppermute | solution.py:29
  74.6 1.2 %collective-permute-start.42 = (bf16[64,256]{1,0:T(8,128)(2,1)S(1)}, bf16[64,256]{1,0:T(8,128)(2,1)S(1)}, u32[]{:S(2)}, u32[]{:S(2)}) collective-permute-start(bf16[64,256]{1,0:T(8,128)(2,1)S(1)} %collective-permute-done.34.refs_7_), channel_id=1, source_target_pairs={{0,1},{1,0},{2,3},{3,2},{4,5},{5,4},{6,7},{7,6},{8,9},{9,8},{10,11... | collective-permute-start | bytes 98312 | tf_op jit(solution)/shard_map/ppermute | solution.py:29
  82.2 9.4 %collective-permute-start.43 = (bf16[2,256,256]{2,1,0:T(8,128)(2,1)}, bf16[2,256,256]{2,1,0:T(8,128)(2,1)S(1)}, u32[]{:S(2)}, u32[]{:S(2)}) collective-permute-start(bf16[2,256,256]{2,1,0:T(8,128)(2,1)} %first.1.refs_0_), channel_id=1, source_target_pairs={{0,12},{4,0},{8,4},{12,8},{1,13},{5,1},{9,5},{13,9},{2,14},{6,2},{... | collective-permute-start | bytes 786440 | tf_op jit(solution)/shard_map/ppermute | solution.py:34
  84.6 13.7 %collective-permute-start.45 = (bf16[2,256,256]{2,1,0:T(8,128)(2,1)}, bf16[2,256,256]{2,1,0:T(8,128)(2,1)S(1)}, u32[]{:S(2)}, u32[]{:S(2)}) collective-permute-start(bf16[2,256,256]{2,1,0:T(8,128)(2,1)} %first.1.refs_0_), channel_id=1, source_target_pairs={{0,4},{4,8},{8,12},{12,0},{1,5},{5,9},{9,13},{13,1},{2,6},{6,10},{... | collective-permute-start | bytes 786440 | tf_op jit(solution)/shard_map/ppermute | solution.py:34
  91.6 11.5 %collective-permute-start.44 = (bf16[2,256,256]{2,1,0:T(8,128)(2,1)S(1)}, bf16[2,256,256]{2,1,0:T(8,128)(2,1)S(1)}, u32[]{:S(2)}, u32[]{:S(2)}) collective-permute-start(bf16[2,256,256]{2,1,0:T(8,128)(2,1)S(1)} %collective-permute-done.43.refs_1_), channel_id=1, source_target_pairs={{0,12},{4,0},{8,4},{12,8},{1,13},{5,1},{9,5},{13,9},{2,14},{6,2},{... | collective-permute-start | bytes 786440 | tf_op jit(solution)/shard_map/ppermute | solution.py:34
  106.6 9.5 %all-to-all-start.1 = ((bf16[4,2,64,256]{3,2,1,0:T(8,128)(2,1)}), bf16[4,2,64,256]{3,2,1,0:T(8,128)(2,1)S(1)}, u32[]{:S(2)}, u32[]{:S(2)}) async-start(bf16[4,2,64,256]{3,2,1,0:T(8,128)(2,1)} %second.1), calls=%async_computation.1 | async-start | bytes 524288 | tf_op jit(solution)/shard_map/all_to_all | solution.py:298
  (39 other events, 170.1 us)

commit v2 on v1

v2 whole, which is shorter than its diff:
```python
import functools

import jax
import jax.numpy as jnp
import numpy as np
from jax import lax
from jax.experimental import pallas as pl
from jax.experimental.pallas import tpu as pltpu
from jax.sharding import PartitionSpec as P

NT = 16
NF = 16

damping = 0.3

FULL = pltpu.CompilerParams(vmem_limit_bytes=67043328)
HBM = pl.BlockSpec(memory_space=pltpu.HBM)
VMEM = pl.BlockSpec(memory_space=pltpu.VMEM)
SMEM = pl.BlockSpec(memory_space=pltpu.SMEM)


def time_tables(count_times, count_freqs):
    moments = np.float32(0.25) * (np.arange(count_times, dtype=np.float32) + np.float32(0.5))
    omegas = np.float32(0.4) * (np.arange(count_freqs, dtype=np.float32) + np.float32(0.5))
    cosine = np.float32(0.5) * np.cos(omegas[:, None] * moments[None, :])
    return (moments, cosine.astype(jnp.bfloat16))


def swap(value, axis, bit):
    size = lax.axis_size(axis)
    return lax.ppermute(value, axis, [(i, i ^ bit) for i in range(size)])


def shift(value, axis, step):
    size = lax.axis_size(axis)
    return lax.ppermute(value, axis, [(i, (i + step) % size) for i in range(size)])


def bits_of(count):
    return [1 << b for b in reversed(range(count.bit_length() - 1))]


def spread(pieces, axis, bit, slot):
    out = dict(pieces)
    for key, value in pieces.items():
        moved = list(key)
        moved[slot] ^= bit
        out[tuple(moved)] = swap(value, axis, bit)
    return out


def run_copies(copies, sem):
    copies = [pltpu.make_async_copy(a, b, sem) for a, b in copies]
    for copy in copies:
        copy.start()
    for copy in copies:
        copy.wait()


def tile_kernel(row_keys, groups, dims, mix, factors, *refs):
    (times, freqs, half, shard_rows, places) = dims
    row_pieces = refs[: len(row_keys)]
    pieces = refs[len(row_pieces) :][: places * len(groups)]
    out, rows, cols, scaled, spectral, sems, out_sem = refs[len(row_pieces) + len(pieces) :]
    tm, p = lax.axis_index("tm"), lax.axis_index("col")
    part = cols.shape[2]
    copies = []
    for n in range(places):
        for i, kts in enumerate(groups):
            ref = pieces[n * len(groups) + i]
            for m, (kt, arr) in enumerate((kt, arr) for kt in kts for arr in range(2)):
                lane = pl.multiple_of((tm ^ kt) * half, half)
                to = cols.at[arr, n, :, pl.ds(lane, half)]
                copies.append((ref.at[:, pl.ds(m * half, half)], to))
    for (arr, kt, kc), ref in zip(row_keys, row_pieces):
        to = pl.multiple_of((p ^ kc) * shard_rows, shard_rows)
        lane = pl.multiple_of((tm ^ kt) * half, half)
        copies.append((ref, rows.at[arr, pl.ds(to, shard_rows), pl.ds(lane, half)]))
    run_copies(copies, sems)
    block = mix.shape[0] // freqs
    span = block * times

    for n in range(places):
        greens = []
        slot = n % scaled.shape[0]
        for arr in range(2):
            for g in range(part // block):
                values = cols[arr, n, pl.ds(g * block, block), :].astype(jnp.float32)
                for j in range(times):
                    factor = factors[arr, pl.ds(j, 1), :]
                    scaled[slot, arr, pl.ds(g * span + j * block, block), :] = (values * factor).astype(
                        jnp.bfloat16
                    )
            greens.append(
                lax.dot_general(
                    scaled[slot, arr],
                    rows[arr],
                    (((1,), (1,)), ((), ())),
                    preferred_element_type=jnp.float32,
                )
            )
        polar = (-2.0 * greens[0] * greens[1]).astype(jnp.bfloat16)
        for g in range(part // block):
            total = jnp.dot(
                mix[...], polar[g * span : (g + 1) * span], preferred_element_type=jnp.float32
            )
            spectral[n, :, pl.ds(g * block, block), :] = total.astype(jnp.bfloat16).reshape(
                freqs, block, total.shape[1]
            )
        pltpu.make_async_copy(spectral.at[n], out.at[:, n], out_sem.at[n]).start()
    for n in range(places):
        pltpu.make_async_copy(spectral.at[n], out.at[:, n], out_sem.at[n]).wait()


def pick_kernel(lanes, *refs):
    pieces, out, sem = refs[:-2], refs[-2], refs[-1]
    run_copies(
        [(ref.at[:, pl.ds(lanes, out.shape[2])], out.at[n]) for n, ref in enumerate(pieces)], sem
    )


def columns_kernel(keys, dims, *refs):
    (tm_count, row_count, col_count, shard_rows, part) = dims
    pieces = refs[: len(keys)]
    out, own, gathered, own_rows, sem = refs[len(keys) :]
    p = lax.axis_index("col")
    width = row_count * part
    copies = []
    wide = own.shape[0]
    for kc, ref in zip(keys, pieces):
        for kq in range(row_count):
            for t in range(tm_count):
                source = ref.at[kq, :, pl.ds(t * wide, wide)]
                to = pl.multiple_of((t * col_count + (p ^ kc)) * width + kq * part, part)
                copies.append((source, gathered.at[pl.ds(to, part), :]))
                if kq == 0:
                    to = pl.multiple_of((p ^ kc) * shard_rows + t * part, part)
                    copies.append((source, own_rows.at[pl.ds(to, part), :]))
    run_copies(copies, sem)
    out[...] = gathered[...].astype(jnp.float32).T.astype(jnp.bfloat16)
    own[...] = own_rows[...].astype(jnp.float32).T.astype(jnp.bfloat16)


def first_kernel(all_columns, own, tiles, out):
    sources, freqs, width, rows = tiles.shape
    for k in range(freqs):
        weights = tiles[:, k].reshape(sources * width, rows)
        first = jnp.dot(all_columns[...], weights, preferred_element_type=jnp.float32)
        out[k] = (own[...].astype(jnp.float32) + damping * first).astype(jnp.bfloat16)


def second_kernel(dims, tiles, *refs):
    (tm_count, row_count, col_count, part, shard_rows) = dims
    middles = refs[:row_count]
    out = refs[row_count]
    _, freqs, _, _ = tiles.shape
    for k in range(freqs):
        total = None
        for kq in range(row_count):
            weights = jnp.concatenate(
                [
                    tiles[t * col_count + p, k, pl.ds(kq * part, part), :]
                    for p in range(col_count)
                    for t in range(tm_count)
                ],
                axis=0,
            )
            term = jnp.dot(middles[kq][k], weights, preferred_element_type=jnp.float32)
            total = term if total is None else total + term
        second = total.T.astype(jnp.bfloat16)
        for p in range(col_count):
            out[p, k] = second[p * shard_rows : (p + 1) * shard_rows]


def shards(occ_orbitals, empty_orbitals, occ_rate, empty_rate, columns):
    tm_count, row_count, col_count = (lax.axis_size(a) for a in ("tm", "row", "col"))
    shard_rows, half = occ_orbitals.shape
    columns_wide = columns.shape[1]
    orbitals = tm_count * half
    part = shard_rows // tm_count
    width = row_count * part
    tile_rows = col_count * shard_rows
    tm_index, col_index = lax.axis_index("tm"), lax.axis_index("col")
    both = (occ_orbitals, empty_orbitals)
    high, low = bits_of(col_count)[:-1], bits_of(col_count)[-1:]

    rows_of = [{(arr, 0, 0): value} for arr, value in enumerate(both)]
    own = jnp.concatenate(
        [lax.dynamic_slice_in_dim(value, tm_index * part, part, 0) for value in both]
        + [columns[t * part : (t + 1) * part] for t in range(tm_count)],
        axis=1,
    )
    for bit in bits_of(tm_count):
        rows_of = [spread(pieces, "tm", bit, 1) for pieces in rows_of]
    near = [{k: v for k, v in pieces.items() if k[1] == 0} for pieces in rows_of]
    far = [{k: v for k, v in pieces.items() if k[1] != 0} for pieces in rows_of]
    for bit in high:
        near = [spread(pieces, "col", bit, 2) for pieces in near]
    got = [
        lax.dynamic_slice_in_dim(far[arr][(arr, kt, 0)], tm_index * part, part, 0)
        for kt in range(1, tm_count)
        for arr in range(2)
    ]
    streams, late = (0,), tuple(range(1, tm_count))
    cols_of = {(0, streams): own, (0, late): jnp.concatenate(got, axis=1)}

    def ring_step(group, source, target, step):
        cols_of[(target, group)] = shift(cols_of[(source, group)], "row", step)

    behind = (row_count - 1) // 2
    ahead = row_count // 2
    ring_step(streams, 0, 1, -1)
    if behind:
        ring_step(streams, 0, row_count - 1, 1)
    for bit in high:
        far = [spread(pieces, "col", bit, 2) for pieces in far]
    if behind:
        ring_step(late, 0, row_count - 1, 1)
    ring_step(late, 0, 1, -1)
    for k in range(2, ahead + 1):
        ring_step(streams, k - 1, k, -1)
    for k in range(2, behind + 1):
        ring_step(streams, row_count - k + 1, row_count - k, 1)
    for bit in low:
        near = [spread(pieces, "col", bit, 2) for pieces in near]
    for k in range(2, ahead + 1):
        ring_step(late, k - 1, k, -1)
    for k in range(2, behind + 1):
        ring_step(late, row_count - k + 1, row_count - k, 1)
    for bit in low:
        far = [spread(pieces, "col", bit, 2) for pieces in far]
    row_pieces = {**near[0], **near[1], **far[0], **far[1]}
    row_keys = list(row_pieces)

    picked = pl.pallas_call(
        functools.partial(pick_kernel, 2 * half),
        out_shape=jax.ShapeDtypeStruct((row_count, part, tm_count * columns_wide), jnp.bfloat16),
        in_specs=[HBM] * row_count,
        out_specs=VMEM,
        scratch_shapes=[pltpu.SemaphoreType.DMA],
        compiler_params=FULL,
        name="pick",
    )(*[cols_of[(kq, streams)] for kq in range(row_count)])
    column_pieces = {(0,): picked}
    for bit in high:
        column_pieces = spread(column_pieces, "col", bit, 0)
    for bit in low:
        column_pieces = spread(column_pieces, "col", bit, 0)

    moments, cosine = time_tables(NT, NF)
    factors = jnp.exp(-jnp.stack([occ_rate, empty_rate])[:, None, :] * moments[None, :, None])
    block = min(16, part)
    mix = jnp.asarray(np.kron(cosine.astype(np.float32), np.eye(block)).astype(jnp.bfloat16))
    groups = [streams, late]
    pieces = [cols_of[(place, kts)] for place in range(row_count) for kts in groups]
    tile = pl.pallas_call(
        functools.partial(
            tile_kernel, row_keys, groups, (NT, NF, half, shard_rows, row_count)
        ),
        out_shape=jax.ShapeDtypeStruct((NF, row_count, part, tile_rows), jnp.bfloat16),
        in_specs=[VMEM, VMEM] + [HBM] * (len(row_keys) + len(pieces)),
        out_specs=HBM,
        scratch_shapes=[
            pltpu.VMEM((2, tile_rows, orbitals), jnp.bfloat16),
            pltpu.VMEM((2, row_count, part, orbitals), jnp.bfloat16),
            pltpu.VMEM((2, 2, NT * part, orbitals), jnp.bfloat16),
            pltpu.VMEM((row_count, NF, part, tile_rows), jnp.bfloat16),
            pltpu.SemaphoreType.DMA,
            pltpu.SemaphoreType.DMA((row_count,)),
        ],
        compiler_params=FULL,
        name="tile",
    )(mix, factors, *[row_pieces[k] for k in row_keys], *pieces)

    keys = [key[0] for key in column_pieces]
    all_columns, own_columns = pl.pallas_call(
        functools.partial(columns_kernel, keys, (tm_count, row_count, col_count, shard_rows, part)),
        out_shape=(
            jax.ShapeDtypeStruct((columns_wide, tm_count * col_count * width), jnp.bfloat16),
            jax.ShapeDtypeStruct((columns_wide, tile_rows), jnp.bfloat16),
        ),
        in_specs=[HBM] * len(keys),
        out_specs=(VMEM, VMEM),
        scratch_shapes=[
            pltpu.VMEM((tm_count * col_count * width, columns_wide), jnp.bfloat16),
            pltpu.VMEM((tile_rows, columns_wide), jnp.bfloat16),
            pltpu.SemaphoreType.DMA,
        ],
        compiler_params=FULL,
        name="columns",
    )(*column_pieces.values())

    local_freqs = NF // tm_count
    own_freqs = max(1, local_freqs // col_count)
    splits = max(1, col_count // local_freqs)
    columns_own = columns_wide // splits
    sent = tile.reshape(NF // own_freqs, own_freqs, width, tile_rows)
    if splits > 1:
        sent = jnp.repeat(sent, splits, axis=0)
        first_row = (col_index % splits) * columns_own
        all_columns = lax.dynamic_slice_in_dim(all_columns, first_row, columns_own, 0)
        own_columns = lax.dynamic_slice_in_dim(own_columns, first_row, columns_own, 0)
    tiles = lax.all_to_all(sent, ("tm", "col"), split_axis=0, concat_axis=0, tiled=True)

    middle = pl.pallas_call(
        first_kernel,
        out_shape=jax.ShapeDtypeStruct((own_freqs, columns_own, tile_rows), jnp.bfloat16),
        in_specs=[VMEM, VMEM, VMEM],
        out_specs=VMEM,
        name="first",
    )(all_columns, own_columns, tiles)
    middles = {0: middle}
    middles[1] = shift(middle, "row", -1)
    for k in range(1, behind + 1):
        middles[row_count - k] = shift(middles[(row_count - k + 1) % row_count], "row", 1)
    for k in range(2, ahead + 1):
        middles[k] = shift(middles[k - 1], "row", -1)
    second = pl.pallas_call(
        functools.partial(second_kernel, (tm_count, row_count, col_count, part, shard_rows)),
        out_shape=jax.ShapeDtypeStruct(
            (col_count, own_freqs, shard_rows, columns_own), jnp.bfloat16
        ),
        in_specs=[VMEM] * (1 + row_count),
        out_specs=VMEM,
        name="second",
    )(tiles, *[middles[k] for k in range(row_count)])
    second = lax.all_to_all(second, "col", split_axis=0, concat_axis=0, tiled=True)
    second = second.reshape(
        col_count // splits, splits, own_freqs, shard_rows, columns_own
    ).transpose(3, 0, 2, 1, 4)
    second = second.reshape(shard_rows, local_freqs, columns_wide).astype(jnp.float32)
    return columns.astype(jnp.float32)[:, None, :] + damping * second


def solution(mesh):
    placed = (P(("col", "row"), "tm"), P(("col", "row"), "tm"), P(), P(), P(("col", "row"), None))
    return jax.shard_map(
        shards, mesh=mesh, in_specs=placed, out_specs=P(("col", "row"), "tm", None), check_vma=False
    )
```

time: 118 us -> 113 us (0.958)
  starting transfers between devices: 54.5 us -> 39.3 us
  waiting for transfers between devices: 35.7 us -> 48.2 us
  Pallas kernels: 19.4 us -> 17.9 us
    ppermute x28 -> x17, waiting for transfers between devices: 11.6 us -> 20.9 us  [swap(): return lax.ppermute(value, axis, [(i, i ^ bit) for i in range(size)])]
    ppermute x28 -> x17, starting transfers between devices: 17.7 us -> 9.42 us  [swap(): return lax.ppermute(value, axis, [(i, i ^ bit) for i in range(size)])]
    ppermute x18 -> x9, starting transfers between devices: 29.7 us -> 22.1 us  [shift(): lax.ppermute(value, axis, [(i, (i + step) % size) for i in range(size)])]
    ppermute x18 -> x9, waiting for transfers between devices: 18.1 us -> 21.4 us  [shift(): lax.ppermute(value, axis, [(i, (i + step) % size) for i in range(size)])]
    pallas_call x1 -> x2, Pallas kernels: 11.9 us -> 10.4 us  [the longest x1 8.98 us: shards(): pl.pallas_call(functools.partial(tile_kernel, row_keys, groups, (NT, NF,...]
    unnamed x110 -> x58, local copies, waits for them, and re-layouts: 3.45 us -> 3.3 us
  transfers between devices with their start and end apart: 48 -> 28, of which waited for: 18 -> 13; matrix products, arithmetic and copies ran while one was open for 1% -> 2% of each run, Pallas kernels for 2% -> 3%
where the time goes in v2:
time: 113 us
  waiting for transfers between devices  48.2 us (43%)
  starting transfers between devices  39.3 us (35%)
  Pallas kernels  17.9 us (16%)
  local copies, waits for them, and re-layouts  4.94 us (4%)
  other arithmetic  2.01 us (2%)
    ppermute x9, starting transfers between devices, shift(): lax.ppermute(value, axis, [(i, (i + step) % size) for i in range(size)])  22.1 us
    ppermute x9, waiting for transfers between devices, shift(): lax.ppermute(value, axis, [(i, (i + step) % size) for i in range(size)])  21.4 us
    ppermute x17, waiting for transfers between devices, swap(): return lax.ppermute(value, axis, [(i, i ^ bit) for i in range(size)])  20.9 us
    ppermute x17, starting transfers between devices, swap(): return lax.ppermute(value, axis, [(i, i ^ bit) for i in range(size)])  9.42 us
    pallas_call x1, Pallas kernels, shards(): pl.pallas_call(functools.partial(tile_kernel, row_keys, groups, (NT, NF,...  8.98 us
    all_to_all x1, waiting for transfers between devices, shards(): lax.all_to_all(second, 'col', split_axis=0, concat_axis=0, tiled=True)  5.95 us
    all_to_all x1, starting transfers between devices, shards(): lax.all_to_all(sent, ('tm', 'col'), split_axis=0, concat_axis=0, tiled=True)  4.26 us
    all_to_all x1, starting transfers between devices, shards(): lax.all_to_all(second, 'col', split_axis=0, concat_axis=0, tiled=True)  3.54 us
  transfers between devices with their start and end apart: 28, of which 13 were waited for; matrix products, arithmetic and copies ran while one was open for 2% of the time, Pallas kernels for 3%

profile of v2, /device:TPU:0, one launch (start us, length us, event | category | flops | bytes accessed | tf_op | source)
XLA Modules:
  0.0 112.7 jit_solution(8977728248101585232)
XLA Ops:
  0.0 3.0 %collective-permute-start = (bf16[64,1024]{1,0:T(8,128)(2,1)}, bf16[64,1024]{1,0:T(8,128)(2,1)S(1)}, u32[]{:S(2)}, u32[]{:S(2)}) collective-permute-start(bf16[64,1024]{1,0:T(8,128)(2,1)} %refs_0_.1), channel_id=1, source_target_pairs={{0,2},{1,3},{2,0},{3,1},{4,6},{5,7},{6,4},{7,5},{8,10},{9,11},{10,... | collective-permute-start | bytes 393224 | tf_op jit(solution)/shard_map/ppermute | solution.py:31
  3.0 0.0 collective-permute-start.1
  3.0 1.5 %collective-permute-start.6 = (bf16[64,1024]{1,0:T(8,128)(2,1)}, bf16[64,1024]{1,0:T(8,128)(2,1)S(1)}, u32[]{:S(2)}, u32[]{:S(2)}) collective-permute-start(bf16[64,1024]{1,0:T(8,128)(2,1)} %refs_0_.1), channel_id=1, source_target_pairs={{0,16},{16,0},{1,17},{17,1},{2,18},{18,2},{3,19},{19,3},{4,20},{20... | collective-permute-start | bytes 393224 | tf_op jit(solution)/shard_map/ppermute | solution.py:31
  4.5 0.5 collective-permute-start.3
  5.0 0.1 collective-permute-start.10
  5.1 0.7 fusion
  5.8 0.9 constant_dynamic-slice_fusion.2
  6.7 0.0 copy-start.7
  6.8 5.2 %collective-permute-done.10.refs_12_ = bf16[64,1024]{1,0:T(8,128)(2,1)S(1)} collective-permute-done((bf16[64,1024]{1,0:T(8,128)(2,1)}, bf16[64,1024]{1,0:T(8,128)(2,1)S(1)}, u32[]{:S(2)}, u32[]{:S(2)}) %collective-permute-start.10) | collective-permute-done | bytes 131104 | tf_op jit(solution)/shard_map/ppermute | solution.py:31
  11.9 0.0 collective-permute-start.4
  12.0 0.0 collective-permute-done.6.refs_8_
  12.0 3.7 %collective-permute-start.14 = (bf16[32,2560]{1,0:T(8,128)(2,1)S(1)}, bf16[32,2560]{1,0:T(8,128)(2,1)S(1)}, u32[]{:S(2)}, u32[]{:S(2)}) collective-permute-start(bf16[32,2560]{1,0:T(8,128)(2,1)S(1)} %pad_maximum_fusion.refs_16_.refs_0_), channel_id=1, source_target_pairs={{0,12},{4,0},{8,4},{12,8},{1,13},{5,1},{9,5},{13,9},{2,14},{6,2},{... | collective-permute-start | bytes 491528 | tf_op jit(solution)/shard_map/ppermute | solution.py:36
  15.7 0.1 collective-permute-start.18
  15.7 0.0 collective-permute-done.1.refs_2_
  15.7 0.3 collective-permute-start.2
  16.0 0.0 collective-permute-done.3.refs_5_
  16.0 0.3 collective-permute-start.5
  16.4 3.8 %collective-permute-start.15 = (bf16[32,2048]{1,0:T(8,128)(2,1)S(1)}, bf16[32,2048]{1,0:T(8,128)(2,1)S(1)}, u32[]{:S(2)}, u32[]{:S(2)}) collective-permute-start(bf16[32,2048]{1,0:T(8,128)(2,1)S(1)} %pad_maximum_fusion.1.refs_17_), channel_id=1, source_target_pairs={{0,12},{4,0},{8,4},{12,8},{1,13},{5,1},{9,5},{13,9},{2,14},{6,2},{... | collective-permute-start | bytes 393224 | tf_op jit(solution)/shard_map/ppermute | solution.py:36
  20.2 0.1 collective-permute-done.14.refs_18_.refs_1_
  20.3 0.5 collective-permute-start.7
  20.8 3.9 %collective-permute-done.18.refs_22_.refs_3_ = bf16[32,2560]{1,0:T(8,128)(2,1)S(1)} collective-permute-done((bf16[32,2560]{1,0:T(8,128)(2,1)S(1)}, bf16[32,2560]{1,0:T(8,128)(2,1)S(1)}, u32[]{:S(2)}, u32[]{:S(2)}) %collective-permute-start.18) | collective-permute-done | bytes 163872 | tf_op jit(solution)/shard_map/ppermute | solution.py:36
  24.6 0.0 collective-permute-start.8
  24.7 0.6 collective-permute-start.11
  25.2 0.0 collective-permute-done.5.refs_7_
  25.2 0.2 collective-permute-start.12
  25.5 0.0 collective-permute-done.7.refs_9_
  25.5 1.7 %collective-permute-start.19 = (bf16[32,2048]{1,0:T(8,128)(2,1)S(1)}, bf16[32,2048]{1,0:T(8,128)(2,1)S(1)}, u32[]{:S(2)}, u32[]{:S(2)}) collective-permute-start(bf16[32,2048]{1,0:T(8,128)(2,1)S(1)} %pad_maximum_fusion.1.refs_17_), channel_id=1, source_target_pairs={{0,4},{4,8},{8,12},{12,0},{1,5},{5,9},{9,13},{13,1},{2,6},{6,10},{... | collective-permute-start | bytes 393224 | tf_op jit(solution)/shard_map/ppermute | solution.py:36
  27.2 0.0 collective-permute-done.8.refs_10_
  27.2 2.8 %collective-permute-start.16 = (bf16[32,2560]{1,0:T(8,128)(2,1)S(1)}, bf16[32,2560]{1,0:T(8,128)(2,1)S(1)}, u32[]{:S(2)}, u32[]{:S(2)}) collective-permute-start(bf16[32,2560]{1,0:T(8,128)(2,1)S(1)} %collective-permute-done.14.refs_18_.refs_1_), channel_id=1, source_target_pairs={{0,12},{4,0},{8,4},{12,8},{1,13},{5,1},{9,5},{13,9},{2,14},{6,2},{... | collective-permute-start | bytes 491528 | tf_op jit(solution)/shard_map/ppermute | solution.py:36
  30.0 0.5 collective-permute-done.11.refs_13_
  30.6 0.0 collective-permute-start.9
  30.6 0.0 collective-permute-done.12.refs_14_
  30.6 0.5 collective-permute-start.13
  31.1 0.0 collective-permute-done.15.refs_19_
  31.1 1.8 %collective-permute-start.17 = (bf16[32,2048]{1,0:T(8,128)(2,1)S(1)}, bf16[32,2048]{1,0:T(8,128)(2,1)}, u32[]{:S(2)}, u32[]{:S(2)}) collective-permute-start(bf16[32,2048]{1,0:T(8,128)(2,1)S(1)} %collective-permute-done.15.refs_19_), channel_id=1, source_target_pairs={{0,12},{4,0},{8,4},{12,8},{1,13},{5,1},{9,5},{13,9},{2,14},{6,2},{... | collective-permute-start | bytes 393224 | tf_op jit(solution)/shard_map/ppermute | solution.py:36
  32.9 0.8 multiply_exponential_fusion.factors
  33.7 0.6 collective-permute-done.19.refs_23_
  34.3 2.4 %collective-permute-done.16.refs_20_.refs_2_ = bf16[32,2560]{1,0:T(8,128)(2,1)S(1)} collective-permute-done((bf16[32,2560]{1,0:T(8,128)(2,1)S(1)}, bf16[32,2560]{1,0:T(8,128)(2,1)S(1)}, u32[]{:S(2)}, u32[]{:S(2)}) %collective-permute-start.16) | collective-permute-done | bytes 163872 | tf_op jit(solution)/shard_map/ppermute | solution.py:36
  36.7 0.6 copy-done.3
  37.4 0.0 collective-permute-done.13.refs_15_
  37.5 0.5 copy-done.22
  38.0 0.6 copy-done.23
  38.7 0.5 collective-permute-done.17.refs_21_
  39.2 9.0 %tile.1 = bf16[16,4,32,256]{3,2,1,0:T(8,128)(2,1)} custom-call(bf16[256,256]{1,0:T(8,128)(2,1)} %constant.19.clone.mix, f32[2,16,2048]{2,1,0:T(8,128)} %multiply_exponential_fusion.factors, bf16[64,1024]{1,0:T(8,128)(2,1)} %refs_0_.1, bf16[64,1024]{1,0:T(8,128)(2,1)} %copy-done.11, bf16[64,1024]{1,0:T(8,128)(2,1)} %copy-done.12, ...), custom_call_target="tpu_custom_call" | custom-call | tf_op jit(solution)/shard_map/tile/pallas_call | solution.py:256
  48.2 4.3 %all-to-all-start = ((bf16[8,2,128,256]{3,2,1,0:T(8,128)(2,1)}), bf16[8,2,128,256]{3,2,1,0:T(8,128)(2,1)}, u32[]{:S(2)}, u32[]{:S(2)}) async-start(bf16[8,2,128,256]{3,2,1,0:T(8,128)(2,1)} %bitcast.8), calls=%async_computation | async-start | bytes 2097152 | tf_op jit(solution)/shard_map/all_to_all | solution.py:303
  52.4 1.5 %pick.1.refs_0_ = bf16[4,32,512]{2,1,0:T(8,128)(2,1)} custom-call(bf16[32,2560]{1,0:T(8,128)(2,1)} %copy-done, bf16[32,2560]{1,0:T(8,128)(2,1)} %copy-done.1, bf16[32,2560]{1,0:T(8,128)(2,1)} %copy-done.3, bf16[32,2560]{1,0:T(8,128)(2,1)} %copy-done.2), custom_call_target="tpu_custom_call" | custom-call | tf_op jit(solution)/shard_map/pick/pallas_call | solution.py:235
  53.9 2.0 %collective-permute-start.20 = (bf16[4,32,512]{2,1,0:T(8,128)(2,1)}, bf16[4,32,512]{2,1,0:T(8,128)(2,1)S(1)}, u32[]{:S(2)}, u32[]{:S(2)}) collective-permute-start(bf16[4,32,512]{2,1,0:T(8,128)(2,1)} %pick.1.refs_0_), channel_id=1, source_target_pairs={{0,2},{1,3},{2,0},{3,1},{4,6},{5,7},{6,4},{7,5},{8,10},{9,11},{10,... | collective-permute-start | bytes 393224 | tf_op jit(solution)/shard_map/ppermute | solution.py:31
  55.9 13.7 %collective-permute-done.20.refs_1_ = bf16[4,32,512]{2,1,0:T(8,128)(2,1)S(1)} collective-permute-done((bf16[4,32,512]{2,1,0:T(8,128)(2,1)}, bf16[4,32,512]{2,1,0:T(8,128)(2,1)S(1)}, u32[]{:S(2)}, u32[]{:S(2)}) %collective-permute-start.20) | collective-permute-done | bytes 131104 | tf_op jit(solution)/shard_map/ppermute | solution.py:31
  69.5 0.6 copy-done.25
  70.2 0.0 collective-permute-start.22
  70.2 0.0 collective-permute-done.21.refs_2_
  70.2 1.5 %collective-permute-done.22.refs_3_ = bf16[4,32,512]{2,1,0:T(8,128)(2,1)} collective-permute-done((bf16[4,32,512]{2,1,0:T(8,128)(2,1)S(1)}, bf16[4,32,512]{2,1,0:T(8,128)(2,1)}, u32[]{:S(2)}, u32[]{:S(2)}) %collective-permute-start.22) | collective-permute-done | bytes 131104 | tf_op jit(solution)/shard_map/ppermute | solution.py:31
  71.7 2.1 %columns.1 = (bf16[256,1024]{1,0:T(8,128)(2,1)}, bf16[256,256]{1,0:T(8,128)(2,1)}) custom-call(bf16[4,32,512]{2,1,0:T(8,128)(2,1)} %pick.1.refs_0_, bf16[4,32,512]{2,1,0:T(8,128)(2,1)} %copy-done.25, bf16[4,32,512]{2,1,0:T(8,128)(2,1)} %collective-permute-done.21.refs_2_, bf16[4,32,512]{2,1,0:T(8,128)(2,1)} %collective-permute-done.22.refs_3_), custom_call_target="tpu_custom_call" | custom-call | tf_op jit(solution)/shard_map/columns/pallas_call | solution.py:276
  73.7 2.6 %first.1.refs_0_ = bf16[2,256,256]{2,1,0:T(8,128)(2,1)} custom-call(bf16[256,1024]{1,0:T(8,128)(2,1)} %get-tuple-element.7.all_columns, bf16[256,256]{1,0:T(8,128)(2,1)} %get-tuple-element.8.own, bf16[8,2,128,256]{3,2,1,0:T(8,128)(2,1)} %all-to-all-done.tiles), custom_call_target="tpu_custom_call" | custom-call | tf_op jit(solution)/shard_map/first/pallas_call | solution.py:305
  76.4 4.1 %collective-permute-start.23 = (bf16[2,256,256]{2,1,0:T(8,128)(2,1)}, bf16[2,256,256]{2,1,0:T(8,128)(2,1)S(1)}, u32[]{:S(2)}, u32[]{:S(2)}) collective-permute-start(bf16[2,256,256]{2,1,0:T(8,128)(2,1)} %first.1.refs_0_), channel_id=1, source_target_pairs={{0,12},{4,0},{8,4},{12,8},{1,13},{5,1},{9,5},{13,9},{2,14},{6,2},{... | collective-permute-start | bytes 786440 | tf_op jit(solution)/shard_map/ppermute | solution.py:36
  80.5 7.1 %collective-permute-done.23.refs_1_ = bf16[2,256,256]{2,1,0:T(8,128)(2,1)S(1)} collective-permute-done((bf16[2,256,256]{2,1,0:T(8,128)(2,1)}, bf16[2,256,256]{2,1,0:T(8,128)(2,1)S(1)}, u32[]{:S(2)}, u32[]{:S(2)}) %collective-permute-start.23) | collective-permute-done | bytes 262176 | tf_op jit(solution)/shard_map/ppermute | solution.py:36
  87.5 4.2 %collective-permute-start.24 = (bf16[2,256,256]{2,1,0:T(8,128)(2,1)S(1)}, bf16[2,256,256]{2,1,0:T(8,128)(2,1)S(1)}, u32[]{:S(2)}, u32[]{:S(2)}) collective-permute-start(bf16[2,256,256]{2,1,0:T(8,128)(2,1)S(1)} %collective-permute-done.23.refs_1_), channel_id=1, source_target_pairs={{0,12},{4,0},{8,4},{12,8},{1,13},{5,1},{9,5},{13,9},{2,14},{6,2},{... | collective-permute-start | bytes 786440 | tf_op jit(solution)/shard_map/ppermute | solution.py:36
  91.7 1.8 %collective-permute-done.25.refs_3_ = bf16[2,256,256]{2,1,0:T(8,128)(2,1)S(1)} collective-permute-done((bf16[2,256,256]{2,1,0:T(8,128)(2,1)}, bf16[2,256,256]{2,1,0:T(8,128)(2,1)S(1)}, u32[]{:S(2)}, u32[]{:S(2)}) %collective-permute-start.25) | collective-permute-done | bytes 262176 | tf_op jit(solution)/shard_map/ppermute | solution.py:36
  93.5 5.1 %collective-permute-done.24.refs_2_ = bf16[2,256,256]{2,1,0:T(8,128)(2,1)S(1)} collective-permute-done((bf16[2,256,256]{2,1,0:T(8,128)(2,1)S(1)}, bf16[2,256,256]{2,1,0:T(8,128)(2,1)S(1)}, u32[]{:S(2)}, u32[]{:S(2)}) %collective-permute-start.24) | collective-permute-done | bytes 262176 | tf_op jit(solution)/shard_map/ppermute | solution.py:36
  98.6 0.7 copy-done.10
  99.3 2.7 %second.1 = bf16[4,2,64,256]{3,2,1,0:T(8,128)(2,1)} custom-call(bf16[8,2,128,256]{3,2,1,0:T(8,128)(2,1)} %all-to-all-done.tiles, bf16[2,256,256]{2,1,0:T(8,128)(2,1)} %first.1.refs_0_, bf16[2,256,256]{2,1,0:T(8,128)(2,1)} %copy-done.8, bf16[2,256,256]{2,1,0:T(8,128)(2,1)} %copy-done.10, bf16[2,256,256]{2,1,0:T(8,128)(2,1)} %copy-done.9), custom_call_target="tpu_custom_call" | custom-call | tf_op jit(solution)/shard_map/second/pallas_call | solution.py:318
  102.0 3.5 %all-to-all-start.1 = ((bf16[4,2,64,256]{3,2,1,0:T(8,128)(2,1)}), bf16[4,2,64,256]{3,2,1,0:T(8,128)(2,1)S(1)}, u32[]{:S(2)}, u32[]{:S(2)}) async-start(bf16[4,2,64,256]{3,2,1,0:T(8,128)(2,1)} %second.1), calls=%async_computation.1 | async-start | bytes 524288 | tf_op jit(solution)/shard_map/all_to_all | solution.py:327
  105.6 5.9 %all-to-all-done.1 = bf16[4,2,64,256]{3,2,1,0:T(8,128)(2,1)S(1)} async-done(((bf16[4,2,64,256]{3,2,1,0:T(8,128)(2,1)}), bf16[4,2,64,256]{3,2,1,0:T(8,128)(2,1)S(1)}, u32[]{:S(2)}, u32[]{:S(2)}) %all-to-all-start.1) | async-done | bytes 262176 | tf_op jit(solution)/shard_map/all_to_all | solution.py:327
  111.6 1.1 copy_add_fusion
  (66 shorter events, 0.2 us)
Async XLA Ops:
  0.0 15.6 %collective-permute-start = (bf16[64,1024]{1,0:T(8,128)(2,1)}, bf16[64,1024]{1,0:T(8,128)(2,1)S(1)}, u32[]{:S(2)}, u32[]{:S(2)}) collective-permute-start(bf16[64,1024]{1,0:T(8,128)(2,1)} %refs_0_.1), channel_id=1, source_target_pairs={{0,2},{1,3},{2,0},{3,1},{4,6},{5,7},{6,4},{7,5},{8,10},{9,11},{10,... | collective-permute-start | bytes 393224 | tf_op jit(solution)/shard_map/ppermute | solution.py:31
  3.0 12.7 %collective-permute-start.1 = (bf16[64,1024]{1,0:T(8,128)(2,1)}, bf16[64,1024]{1,0:T(8,128)(2,1)S(1)}, u32[]{:S(2)}, u32[]{:S(2)}) collective-permute-start(bf16[64,1024]{1,0:T(8,128)(2,1)} %refs_0_.1), channel_id=1, source_target_pairs={{0,1},{1,0},{2,3},{3,2},{4,5},{5,4},{6,7},{7,6},{8,9},{9,8},{10,11... | collective-permute-start | bytes 393224 | tf_op jit(solution)/shard_map/ppermute | solution.py:31
  3.0 9.0 %collective-permute-start.6 = (bf16[64,1024]{1,0:T(8,128)(2,1)}, bf16[64,1024]{1,0:T(8,128)(2,1)S(1)}, u32[]{:S(2)}, u32[]{:S(2)}) collective-permute-start(bf16[64,1024]{1,0:T(8,128)(2,1)} %refs_0_.1), channel_id=1, source_target_pairs={{0,16},{16,0},{1,17},{17,1},{2,18},{18,2},{3,19},{19,3},{4,20},{20... | collective-permute-start | bytes 393224 | tf_op jit(solution)/shard_map/ppermute | solution.py:31
  4.5 11.5 %collective-permute-start.3 = (bf16[64,1024]{1,0:T(8,128)(2,1)}, bf16[64,1024]{1,0:T(8,128)(2,1)S(1)}, u32[]{:S(2)}, u32[]{:S(2)}) collective-permute-start(bf16[64,1024]{1,0:T(8,128)(2,1)} %refs_4_.1), channel_id=1, source_target_pairs={{0,2},{1,3},{2,0},{3,1},{4,6},{5,7},{6,4},{7,5},{8,10},{9,11},{10,... | collective-permute-start | bytes 393224 | tf_op jit(solution)/shard_map/ppermute | solution.py:31
  5.0 6.9 %collective-permute-start.10 = (bf16[64,1024]{1,0:T(8,128)(2,1)}, bf16[64,1024]{1,0:T(8,128)(2,1)S(1)}, u32[]{:S(2)}, u32[]{:S(2)}) collective-permute-start(bf16[64,1024]{1,0:T(8,128)(2,1)} %refs_4_.1), channel_id=1, source_target_pairs={{0,16},{16,0},{1,17},{17,1},{2,18},{18,2},{3,19},{19,3},{4,20},{20... | collective-permute-start | bytes 393224 | tf_op jit(solution)/shard_map/ppermute | solution.py:31
  6.7 5.2 %copy-start.7 = (bf16[64,1024]{1,0:T(8,128)(2,1)S(1)}, bf16[64,1024]{1,0:T(8,128)(2,1)}, u32[]{:S(2)}) copy-start(bf16[64,1024]{1,0:T(8,128)(2,1)} %refs_4_.1) | copy-start | bytes 393220
  6.8 9.6 %copy-start = (bf16[32,2560]{1,0:T(8,128)(2,1)}, bf16[32,2560]{1,0:T(8,128)(2,1)S(1)}, u32[]{:S(2)}) copy-start(bf16[32,2560]{1,0:T(8,128)(2,1)S(1)} %pad_maximum_fusion.refs_16_.refs_0_) | copy-start | bytes 491524
  11.9 13.3 %copy-start.6 = (bf16[64,1024]{1,0:T(8,128)(2,1)}, bf16[64,1024]{1,0:T(8,128)(2,1)S(1)}, u32[]{:S(2)}) copy-start(bf16[64,1024]{1,0:T(8,128)(2,1)S(1)} %collective-permute-done.10.refs_12_) | copy-start | bytes 393220
  11.9 4.4 %collective-permute-start.4 = (bf16[64,1024]{1,0:T(8,128)(2,1)S(1)}, bf16[64,1024]{1,0:T(8,128)(2,1)S(1)}, u32[]{:S(2)}, u32[]{:S(2)}) collective-permute-start(bf16[64,1024]{1,0:T(8,128)(2,1)S(1)} %copy-done.7), channel_id=1, source_target_pairs={{0,1},{1,0},{2,3},{3,2},{4,5},{5,4},{6,7},{7,6},{8,9},{9,8},{10,11... | collective-permute-start | bytes 393224 | tf_op jit(solution)/shard_map/ppermute | solution.py:31
  12.0 12.7 %copy-start.5 = (bf16[64,1024]{1,0:T(8,128)(2,1)}, bf16[64,1024]{1,0:T(8,128)(2,1)S(1)}, u32[]{:S(2)}) copy-start(bf16[64,1024]{1,0:T(8,128)(2,1)S(1)} %collective-permute-done.6.refs_8_) | copy-start | bytes 393220
  12.0 8.3 %collective-permute-start.14 = (bf16[32,2560]{1,0:T(8,128)(2,1)S(1)}, bf16[32,2560]{1,0:T(8,128)(2,1)S(1)}, u32[]{:S(2)}, u32[]{:S(2)}) collective-permute-start(bf16[32,2560]{1,0:T(8,128)(2,1)S(1)} %pad_maximum_fusion.refs_16_.refs_0_), channel_id=1, source_target_pairs={{0,12},{4,0},{8,4},{12,8},{1,13},{5,1},{9,5},{13,9},{2,14},{6,2},{... | collective-permute-start | bytes 491528 | tf_op jit(solution)/shard_map/ppermute | solution.py:36
  15.6 21.7 %copy-start.11 = (bf16[64,1024]{1,0:T(8,128)(2,1)}, bf16[64,1024]{1,0:T(8,128)(2,1)S(1)}, u32[]{:S(2)}) copy-start(bf16[64,1024]{1,0:T(8,128)(2,1)S(1)} %collective-permute-done.refs_1_) | copy-start | bytes 393220
  15.7 9.0 %collective-permute-start.18 = (bf16[32,2560]{1,0:T(8,128)(2,1)S(1)}, bf16[32,2560]{1,0:T(8,128)(2,1)S(1)}, u32[]{:S(2)}, u32[]{:S(2)}) collective-permute-start(bf16[32,2560]{1,0:T(8,128)(2,1)S(1)} %pad_maximum_fusion.refs_16_.refs_0_), channel_id=1, source_target_pairs={{0,4},{4,8},{8,12},{12,0},{1,5},{5,9},{9,13},{13,1},{2,6},{6,10},{... | collective-permute-start | bytes 491528 | tf_op jit(solution)/shard_map/ppermute | solution.py:36
  15.7 21.7 %copy-start.12 = (bf16[64,1024]{1,0:T(8,128)(2,1)}, bf16[64,1024]{1,0:T(8,128)(2,1)S(1)}, u32[]{:S(2)}) copy-start(bf16[64,1024]{1,0:T(8,128)(2,1)S(1)} %collective-permute-done.1.refs_2_) | copy-start | bytes 393220
  15.7 8.9 %collective-permute-start.2 = (bf16[64,1024]{1,0:T(8,128)(2,1)S(1)}, bf16[64,1024]{1,0:T(8,128)(2,1)S(1)}, u32[]{:S(2)}, u32[]{:S(2)}) collective-permute-start(bf16[64,1024]{1,0:T(8,128)(2,1)S(1)} %collective-permute-done.refs_1_), channel_id=1, source_target_pairs={{0,1},{1,0},{2,3},{3,2},{4,5},{5,4},{6,7},{7,6},{8,9},{9,8},{10,11... | collective-permute-start | bytes 393224 | tf_op jit(solution)/shard_map/ppermute | solution.py:31
  16.0 21.4 %copy-start.13 = (bf16[64,1024]{1,0:T(8,128)(2,1)}, bf16[64,1024]{1,0:T(8,128)(2,1)S(1)}, u32[]{:S(2)}) copy-start(bf16[64,1024]{1,0:T(8,128)(2,1)S(1)} %collective-permute-done.3.refs_5_) | copy-start | bytes 393220
  16.0 9.2 %collective-permute-start.5 = (bf16[64,1024]{1,0:T(8,128)(2,1)S(1)}, bf16[64,1024]{1,0:T(8,128)(2,1)S(1)}, u32[]{:S(2)}, u32[]{:S(2)}) collective-permute-start(bf16[64,1024]{1,0:T(8,128)(2,1)S(1)} %collective-permute-done.3.refs_5_), channel_id=1, source_target_pairs={{0,1},{1,0},{2,3},{3,2},{4,5},{5,4},{6,7},{7,6},{8,9},{9,8},{10,11... | collective-permute-start | bytes 393224 | tf_op jit(solution)/shard_map/ppermute | solution.py:31
  16.3 9.1 %copy-start.26 = (f32[2048]{0:T(1024)S(1)}, f32[2048]{0:T(1024)}, u32[]{:S(2)}) copy-start(f32[2048]{0:T(1024)} %param.10) | copy-start | bytes 24580
  16.3 9.1 %copy-start.27 = (f32[2048]{0:T(1024)S(1)}, f32[2048]{0:T(1024)}, u32[]{:S(2)}) copy-start(f32[2048]{0:T(1024)} %param.9) | copy-start | bytes 24580
  16.4 21.1 %copy-start.4 = (bf16[32,2048]{1,0:T(8,128)(2,1)}, bf16[32,2048]{1,0:T(8,128)(2,1)S(1)}, u32[]{:S(2)}) copy-start(bf16[32,2048]{1,0:T(8,128)(2,1)S(1)} %pad_maximum_fusion.1.refs_17_) | copy-start | bytes 393220
  16.4 10.8 %copy-start.14 = (bf16[64,1024]{1,0:T(8,128)(2,1)}, bf16[64,1024]{1,0:T(8,128)(2,1)S(1)}, u32[]{:S(2)}) copy-start(bf16[64,1024]{1,0:T(8,128)(2,1)S(1)} %collective-permute-done.4.refs_6_) | copy-start | bytes 393220
  16.4 14.7 %collective-permute-start.15 = (bf16[32,2048]{1,0:T(8,128)(2,1)S(1)}, bf16[32,2048]{1,0:T(8,128)(2,1)S(1)}, u32[]{:S(2)}, u32[]{:S(2)}) collective-permute-start(bf16[32,2048]{1,0:T(8,128)(2,1)S(1)} %pad_maximum_fusion.1.refs_17_), channel_id=1, source_target_pairs={{0,12},{4,0},{8,4},{12,8},{1,13},{5,1},{9,5},{13,9},{2,14},{6,2},{... | collective-permute-start | bytes 393224 | tf_op jit(solution)/shard_map/ppermute | solution.py:36
  20.3 6.9 %copy-start.1 = (bf16[32,2560]{1,0:T(8,128)(2,1)}, bf16[32,2560]{1,0:T(8,128)(2,1)S(1)}, u32[]{:S(2)}) copy-start(bf16[32,2560]{1,0:T(8,128)(2,1)S(1)} %collective-permute-done.14.refs_18_.refs_1_) | copy-start | bytes 491524
  20.3 5.2 %collective-permute-start.7 = (bf16[64,1024]{1,0:T(8,128)(2,1)S(1)}, bf16[64,1024]{1,0:T(8,128)(2,1)S(1)}, u32[]{:S(2)}, u32[]{:S(2)}) collective-permute-start(bf16[64,1024]{1,0:T(8,128)(2,1)S(1)} %collective-permute-done.6.refs_8_), channel_id=1, source_target_pairs={{0,2},{1,3},{2,0},{3,1},{4,6},{5,7},{6,4},{7,5},{8,10},{9,11},{10,... | collective-permute-start | bytes 393224 | tf_op jit(solution)/shard_map/ppermute | solution.py:31
  24.6 12.1 %copy-start.2 = (bf16[32,2560]{1,0:T(8,128)(2,1)}, bf16[32,2560]{1,0:T(8,128)(2,1)S(1)}, u32[]{:S(2)}) copy-start(bf16[32,2560]{1,0:T(8,128)(2,1)S(1)} %collective-permute-done.18.refs_22_.refs_3_) | copy-start | bytes 491524
  24.6 2.6 %collective-permute-start.8 = (bf16[64,1024]{1,0:T(8,128)(2,1)S(1)}, bf16[64,1024]{1,0:T(8,128)(2,1)}, u32[]{:S(2)}, u32[]{:S(2)}) collective-permute-start(bf16[64,1024]{1,0:T(8,128)(2,1)S(1)} %collective-permute-done.6.refs_8_), channel_id=1, source_target_pairs={{0,1},{1,0},{2,3},{3,2},{4,5},{5,4},{6,7},{7,6},{8,9},{9,8},{10,11... | collective-permute-start | bytes 393224 | tf_op jit(solution)/shard_map/ppermute | solution.py:31
  24.7 12.8 %copy-start.15 = (bf16[64,1024]{1,0:T(8,128)(2,1)}, bf16[64,1024]{1,0:T(8,128)(2,1)S(1)}, u32[]{:S(2)}) copy-start(bf16[64,1024]{1,0:T(8,128)(2,1)S(1)} %collective-permute-done.2.refs_3_) | copy-start | bytes 393220
  24.7 5.9 %collective-permute-start.11 = (bf16[64,1024]{1,0:T(8,128)(2,1)S(1)}, bf16[64,1024]{1,0:T(8,128)(2,1)S(1)}, u32[]{:S(2)}, u32[]{:S(2)}) collective-permute-start(bf16[64,1024]{1,0:T(8,128)(2,1)S(1)} %collective-permute-done.10.refs_12_), channel_id=1, source_target_pairs={{0,2},{1,3},{2,0},{3,1},{4,6},{5,7},{6,4},{7,5},{8,10},{9,11},{10,... | collective-permute-start | bytes 393224 | tf_op jit(solution)/shard_map/ppermute | solution.py:31
  25.2 12.2 %copy-start.16 = (bf16[64,1024]{1,0:T(8,128)(2,1)}, bf16[64,1024]{1,0:T(8,128)(2,1)S(1)}, u32[]{:S(2)}) copy-start(bf16[64,1024]{1,0:T(8,128)(2,1)S(1)} %collective-permute-done.5.refs_7_) | copy-start | bytes 393220
  25.2 5.3 %collective-permute-start.12 = (bf16[64,1024]{1,0:T(8,128)(2,1)S(1)}, bf16[64,1024]{1,0:T(8,128)(2,1)S(1)}, u32[]{:S(2)}, u32[]{:S(2)}) collective-permute-start(bf16[64,1024]{1,0:T(8,128)(2,1)S(1)} %collective-permute-done.10.refs_12_), channel_id=1, source_target_pairs={{0,1},{1,0},{2,3},{3,2},{4,5},{5,4},{6,7},{7,6},{8,9},{9,8},{10,11... | collective-permute-start | bytes 393224 | tf_op jit(solution)/shard_map/ppermute | solution.py:31
  25.5 7.4 %copy-start.28 = (f32[16]{0:T(128)S(1)}, f32[16]{0:T(128)}, u32[]{:S(2)}) copy-start(f32[16]{0:T(128)} %constant.20) | copy-start | bytes 196
  25.5 11.9 %copy-start.18 = (bf16[64,1024]{1,0:T(8,128)(2,1)}, bf16[64,1024]{1,0:T(8,128)(2,1)S(1)}, u32[]{:S(2)}) copy-start(bf16[64,1024]{1,0:T(8,128)(2,1)S(1)} %collective-permute-done.7.refs_9_) | copy-start | bytes 393220
  25.5 8.8 %collective-permute-start.19 = (bf16[32,2048]{1,0:T(8,128)(2,1)S(1)}, bf16[32,2048]{1,0:T(8,128)(2,1)S(1)}, u32[]{:S(2)}, u32[]{:S(2)}) collective-permute-start(bf16[32,2048]{1,0:T(8,128)(2,1)S(1)} %pad_maximum_fusion.1.refs_17_), channel_id=1, source_target_pairs={{0,4},{4,8},{8,12},{12,0},{1,5},{5,9},{9,13},{13,1},{2,6},{6,10},{... | collective-permute-start | bytes 393224 | tf_op jit(solution)/shard_map/ppermute | solution.py:36
  27.2 9.5 %collective-permute-start.16 = (bf16[32,2560]{1,0:T(8,128)(2,1)S(1)}, bf16[32,2560]{1,0:T(8,128)(2,1)S(1)}, u32[]{:S(2)}, u32[]{:S(2)}) collective-permute-start(bf16[32,2560]{1,0:T(8,128)(2,1)S(1)} %collective-permute-done.14.refs_18_.refs_1_), channel_id=1, source_target_pairs={{0,12},{4,0},{8,4},{12,8},{1,13},{5,1},{9,5},{13,9},{2,14},{6,2},{... | collective-permute-start | bytes 491528 | tf_op jit(solution)/shard_map/ppermute | solution.py:36
  30.6 6.9 %copy-start.19 = (bf16[64,1024]{1,0:T(8,128)(2,1)}, bf16[64,1024]{1,0:T(8,128)(2,1)S(1)}, u32[]{:S(2)}) copy-start(bf16[64,1024]{1,0:T(8,128)(2,1)S(1)} %collective-permute-done.11.refs_13_) | copy-start | bytes 393220
  30.6 6.2 %collective-permute-start.9 = (bf16[64,1024]{1,0:T(8,128)(2,1)S(1)}, bf16[64,1024]{1,0:T(8,128)(2,1)S(1)}, u32[]{:S(2)}, u32[]{:S(2)}) collective-permute-start(bf16[64,1024]{1,0:T(8,128)(2,1)S(1)} %collective-permute-done.7.refs_9_), channel_id=1, source_target_pairs={{0,1},{1,0},{2,3},{3,2},{4,5},{5,4},{6,7},{7,6},{8,9},{9,8},{10,11... | collective-permute-start | bytes 393224 | tf_op jit(solution)/shard_map/ppermute | solution.py:31
  30.6 6.9 %copy-start.20 = (bf16[64,1024]{1,0:T(8,128)(2,1)}, bf16[64,1024]{1,0:T(8,128)(2,1)S(1)}, u32[]{:S(2)}) copy-start(bf16[64,1024]{1,0:T(8,128)(2,1)S(1)} %collective-permute-done.12.refs_14_) | copy-start | bytes 393220
  30.6 6.8 %collective-permute-start.13 = (bf16[64,1024]{1,0:T(8,128)(2,1)S(1)}, bf16[64,1024]{1,0:T(8,128)(2,1)S(1)}, u32[]{:S(2)}, u32[]{:S(2)}) collective-permute-start(bf16[64,1024]{1,0:T(8,128)(2,1)S(1)} %collective-permute-done.11.refs_13_), channel_id=1, source_target_pairs={{0,1},{1,0},{2,3},{3,2},{4,5},{5,4},{6,7},{7,6},{8,9},{9,8},{10,11... | collective-permute-start | bytes 393224 | tf_op jit(solution)/shard_map/ppermute | solution.py:31
  31.1 6.4 %copy-start.17 = (bf16[32,2048]{1,0:T(8,128)(2,1)}, bf16[32,2048]{1,0:T(8,128)(2,1)S(1)}, u32[]{:S(2)}) copy-start(bf16[32,2048]{1,0:T(8,128)(2,1)S(1)} %collective-permute-done.15.refs_19_) | copy-start | bytes 393220
  31.1 8.1 %collective-permute-start.17 = (bf16[32,2048]{1,0:T(8,128)(2,1)S(1)}, bf16[32,2048]{1,0:T(8,128)(2,1)}, u32[]{:S(2)}, u32[]{:S(2)}) collective-permute-start(bf16[32,2048]{1,0:T(8,128)(2,1)S(1)} %collective-permute-done.15.refs_19_), channel_id=1, source_target_pairs={{0,12},{4,0},{8,4},{12,8},{1,13},{5,1},{9,5},{13,9},{2,14},{6,2},{... | collective-permute-start | bytes 393224 | tf_op jit(solution)/shard_map/ppermute | solution.py:36
  34.3 3.2 %copy-start.21 = (bf16[32,2048]{1,0:T(8,128)(2,1)}, bf16[32,2048]{1,0:T(8,128)(2,1)S(1)}, u32[]{:S(2)}) copy-start(bf16[32,2048]{1,0:T(8,128)(2,1)S(1)} %collective-permute-done.19.refs_23_) | copy-start | bytes 393220
  36.7 0.7 copy-start.3
  37.4 0.6 copy-start.22
  38.0 0.7 copy-start.23
  48.2 25.6 %all-to-all-start = ((bf16[8,2,128,256]{3,2,1,0:T(8,128)(2,1)}), bf16[8,2,128,256]{3,2,1,0:T(8,128)(2,1)}, u32[]{:S(2)}, u32[]{:S(2)}) async-start(bf16[8,2,128,256]{3,2,1,0:T(8,128)(2,1)} %bitcast.8), calls=%async_computation | async-start | bytes 2097152 | tf_op jit(solution)/shard_map/all_to_all | solution.py:303
  53.9 15.6 %collective-permute-start.20 = (bf16[4,32,512]{2,1,0:T(8,128)(2,1)}, bf16[4,32,512]{2,1,0:T(8,128)(2,1)S(1)}, u32[]{:S(2)}, u32[]{:S(2)}) collective-permute-start(bf16[4,32,512]{2,1,0:T(8,128)(2,1)} %pick.1.refs_0_), channel_id=1, source_target_pairs={{0,2},{1,3},{2,0},{3,1},{4,6},{5,7},{6,4},{7,5},{8,10},{9,11},{10,... | collective-permute-start | bytes 393224 | tf_op jit(solution)/shard_map/ppermute | solution.py:31
  55.8 14.3 %collective-permute-start.21 = (bf16[4,32,512]{2,1,0:T(8,128)(2,1)}, bf16[4,32,512]{2,1,0:T(8,128)(2,1)}, u32[]{:S(2)}, u32[]{:S(2)}) collective-permute-start(bf16[4,32,512]{2,1,0:T(8,128)(2,1)} %pick.1.refs_0_), channel_id=1, source_target_pairs={{0,1},{1,0},{2,3},{3,2},{4,5},{5,4},{6,7},{7,6},{8,9},{9,8},{10,11... | collective-permute-start | bytes 393224 | tf_op jit(solution)/shard_map/ppermute | solution.py:31
  69.5 0.7 copy-start.25
  70.2 1.5 %collective-permute-start.22 = (bf16[4,32,512]{2,1,0:T(8,128)(2,1)S(1)}, bf16[4,32,512]{2,1,0:T(8,128)(2,1)}, u32[]{:S(2)}, u32[]{:S(2)}) collective-permute-start(bf16[4,32,512]{2,1,0:T(8,128)(2,1)S(1)} %collective-permute-done.20.refs_1_), channel_id=1, source_target_pairs={{0,1},{1,0},{2,3},{3,2},{4,5},{5,4},{6,7},{7,6},{8,9},{9,8},{10,11... | collective-permute-start | bytes 393224 | tf_op jit(solution)/shard_map/ppermute | solution.py:31
  76.4 11.1 %collective-permute-start.23 = (bf16[2,256,256]{2,1,0:T(8,128)(2,1)}, bf16[2,256,256]{2,1,0:T(8,128)(2,1)S(1)}, u32[]{:S(2)}, u32[]{:S(2)}) collective-permute-start(bf16[2,256,256]{2,1,0:T(8,128)(2,1)} %first.1.refs_0_), channel_id=1, source_target_pairs={{0,12},{4,0},{8,4},{12,8},{1,13},{5,1},{9,5},{13,9},{2,14},{6,2},{... | collective-permute-start | bytes 786440 | tf_op jit(solution)/shard_map/ppermute | solution.py:36
  80.5 13.0 %collective-permute-start.25 = (bf16[2,256,256]{2,1,0:T(8,128)(2,1)}, bf16[2,256,256]{2,1,0:T(8,128)(2,1)S(1)}, u32[]{:S(2)}, u32[]{:S(2)}) collective-permute-start(bf16[2,256,256]{2,1,0:T(8,128)(2,1)} %first.1.refs_0_), channel_id=1, source_target_pairs={{0,4},{4,8},{8,12},{12,0},{1,5},{5,9},{9,13},{13,1},{2,6},{6,10},{... | collective-permute-start | bytes 786440 | tf_op jit(solution)/shard_map/ppermute | solution.py:36
  87.5 11.0 %copy-start.8 = (bf16[2,256,256]{2,1,0:T(8,128)(2,1)}, bf16[2,256,256]{2,1,0:T(8,128)(2,1)S(1)}, u32[]{:S(2)}) copy-start(bf16[2,256,256]{2,1,0:T(8,128)(2,1)S(1)} %collective-permute-done.23.refs_1_) | copy-start | bytes 786436
  87.5 11.0 %collective-permute-start.24 = (bf16[2,256,256]{2,1,0:T(8,128)(2,1)S(1)}, bf16[2,256,256]{2,1,0:T(8,128)(2,1)S(1)}, u32[]{:S(2)}, u32[]{:S(2)}) collective-permute-start(bf16[2,256,256]{2,1,0:T(8,128)(2,1)S(1)} %collective-permute-done.23.refs_1_), channel_id=1, source_target_pairs={{0,12},{4,0},{8,4},{12,8},{1,13},{5,1},{9,5},{13,9},{2,14},{6,2},{... | collective-permute-start | bytes 786440 | tf_op jit(solution)/shard_map/ppermute | solution.py:36
  93.5 5.1 %copy-start.9 = (bf16[2,256,256]{2,1,0:T(8,128)(2,1)}, bf16[2,256,256]{2,1,0:T(8,128)(2,1)S(1)}, u32[]{:S(2)}) copy-start(bf16[2,256,256]{2,1,0:T(8,128)(2,1)S(1)} %collective-permute-done.25.refs_3_) | copy-start | bytes 786436
  98.6 0.7 copy-start.10
  102.0 3.5 %copy-start.24 = (bf16[64,256]{1,0:T(8,128)(2,1)S(1)}, bf16[64,256]{1,0:T(8,128)(2,1)}, u32[]{:S(2)}) copy-start(bf16[64,256]{1,0:T(8,128)(2,1)} %param.11) | copy-start | bytes 98308
  102.0 9.5 %all-to-all-start.1 = ((bf16[4,2,64,256]{3,2,1,0:T(8,128)(2,1)}), bf16[4,2,64,256]{3,2,1,0:T(8,128)(2,1)S(1)}, u32[]{:S(2)}, u32[]{:S(2)}) async-start(bf16[4,2,64,256]{3,2,1,0:T(8,128)(2,1)} %second.1), calls=%async_computation.1 | async-start | bytes 524288 | tf_op jit(solution)/shard_map/all_to_all | solution.py:327

commit v3 on v2

v3 whole, which is shorter than its diff:
```python
import functools

import jax
import jax.numpy as jnp
import numpy as np
from jax import lax
from jax.experimental import pallas as pl
from jax.experimental.pallas import tpu as pltpu
from jax.sharding import PartitionSpec as P

NT = 16
NF = 16

damping = 0.3

FULL = pltpu.CompilerParams(vmem_limit_bytes=67043328)
HBM = pl.BlockSpec(memory_space=pltpu.HBM)
VMEM = pl.BlockSpec(memory_space=pltpu.VMEM)
SMEM = pl.BlockSpec(memory_space=pltpu.SMEM)


def time_tables(count_times, count_freqs):
    moments = np.float32(0.25) * (np.arange(count_times, dtype=np.float32) + np.float32(0.5))
    omegas = np.float32(0.4) * (np.arange(count_freqs, dtype=np.float32) + np.float32(0.5))
    cosine = np.float32(0.5) * np.cos(omegas[:, None] * moments[None, :])
    return (moments, cosine.astype(jnp.bfloat16))


def swap(value, axis, bit):
    size = lax.axis_size(axis)
    return lax.ppermute(value, axis, [(i, i ^ bit) for i in range(size)])


def shift(value, axis, step):
    size = lax.axis_size(axis)
    return lax.ppermute(value, axis, [(i, (i + step) % size) for i in range(size)])


def bits_of(count):
    return [1 << b for b in reversed(range(count.bit_length() - 1))]


def spread(pieces, axis, bit, slot):
    out = dict(pieces)
    for key, value in pieces.items():
        moved = list(key)
        moved[slot] ^= bit
        out[tuple(moved)] = swap(value, axis, bit)
    return out


def run_copies(copies, sem):
    copies = [pltpu.make_async_copy(a, b, sem) for a, b in copies]
    for copy in copies:
        copy.start()
    for copy in copies:
        copy.wait()


def copies_of(pairs, sem):
    copies = [pltpu.make_async_copy(a, b, sem) for a, b in pairs]
    for copy in copies:
        copy.start()
    return copies


def wait_for(copies):
    for copy in copies:
        copy.wait()


def tile_kernel(row_keys, groups, dims, mix, occ_rate, empty_rate, *refs):
    (times, freqs, half, shard_rows, places, col_count, own_freqs, splits) = dims
    row_pieces = refs[: len(row_keys)]
    pieces = refs[len(row_pieces) :][: places * len(groups)]
    rest = refs[len(row_pieces) + len(pieces) :]
    outs, (rows, cols, scaled, greens, factors, spectral, sems, out_sem) = rest[:-8], rest[-8:]
    tm, p = lax.axis_index("tm"), lax.axis_index("col")
    part = cols.shape[2]
    local_freqs = freqs // (len(outs) // col_count)
    pairs = [[], []]
    for n in range(places):
        for i, kts in enumerate(groups):
            ref = pieces[n * len(groups) + i]
            for m, (kt, arr) in enumerate((kt, arr) for kt in kts for arr in range(2)):
                lane = pl.multiple_of((tm ^ kt) * half, half)
                to = cols.at[arr, n, :, pl.ds(lane, half)]
                pairs[arr].append((ref.at[:, pl.ds(m * half, half)], to))
    for (arr, kt, kc), ref in zip(row_keys, row_pieces):
        to = pl.multiple_of((p ^ kc) * shard_rows, shard_rows)
        lane = pl.multiple_of((tm ^ kt) * half, half)
        pairs[arr].append((ref, rows.at[arr, pl.ds(to, shard_rows), pl.ds(lane, half)]))
    arriving = [copies_of(pairs[arr], sems.at[arr]) for arr in range(2)]
    steps = lax.broadcasted_iota(jnp.int32, factors.shape[1:], 0).astype(jnp.float32)
    for arr, rate in enumerate((occ_rate, empty_rate)):
        factors[arr] = jnp.exp(-rate[...] * (0.25 * (steps + 0.5)))
    block = mix.shape[0] // freqs
    span = block * times

    def green(arr, n):
        slot = (arr * places + n) % scaled.shape[0]
        for g in range(part // block):
            values = cols[arr, n, pl.ds(g * block, block), :].astype(jnp.float32)
            for j in range(times):
                factor = factors[arr, pl.ds(j, 1), :]
                scaled[slot, pl.ds(g * span + j * block, block), :] = (values * factor).astype(
                    jnp.bfloat16
                )
        return lax.dot_general(
            scaled[slot], rows[arr], (((1,), (1,)), ((), ())), preferred_element_type=jnp.float32
        )

    wait_for(arriving[0])
    for n in range(places):
        greens[n] = -2.0 * green(0, n)
    wait_for(arriving[1])
    for n in range(places):
        polar = (greens[n] * green(1, n)).astype(jnp.bfloat16)
        for g in range(part // block):
            total = jnp.dot(
                mix[...], polar[g * span : (g + 1) * span], preferred_element_type=jnp.float32
            )
            spectral[n, :, pl.ds(g * block, block), :] = total.astype(jnp.bfloat16).reshape(
                freqs, block, total.shape[1]
            )
        if len(outs) <= 8 or n == places - 1:
            done = slice(n, n + 1) if len(outs) <= 8 else slice(0, places)
            leaving = leaving if n else []
            for r, ref in enumerate(outs):
                to_tm, to_col = tm ^ (r // col_count), p ^ (r % col_count)
                start = to_tm * local_freqs + (to_col // splits) * own_freqs
                pairs = [
                    (spectral.at[m, pl.ds(start, own_freqs)], ref.at[:, m])
                    for m in range(places)[done]
                ]
                leaving += copies_of(pairs, out_sem)
        else:
            leaving = []
    wait_for(leaving)


def pack_kernel(dims, occ, empty, columns, own, other, sem):
    (part, half, tm_count) = dims
    tm = lax.axis_index("tm")
    wide = columns.shape[1]
    pairs = []
    for arr, ref in enumerate((occ, empty)):
        for kt in range(tm_count):
            source = ref.at[pl.ds(pl.multiple_of((tm ^ kt) * part, part), part), :]
            lanes = pl.ds(arr * half, half)
            pairs.append((source, other.at[kt - 1, :, lanes] if kt else own.at[:, lanes]))
    for t in range(tm_count):
        lanes = pl.ds(2 * half + t * wide, wide)
        pairs.append((columns.at[pl.ds(t * part, part), :], own.at[:, lanes]))
    wait_for(copies_of(pairs, sem))


def pick_kernel(lanes, *refs):
    pieces, out, sem = refs[:-2], refs[-2], refs[-1]
    run_copies(
        [(ref.at[:, pl.ds(lanes, out.shape[2])], out.at[n]) for n, ref in enumerate(pieces)], sem
    )


def columns_kernel(keys, dims, *refs):
    (tm_count, row_count, col_count, shard_rows, part) = dims
    pieces = refs[: len(keys)]
    out, own, gathered, own_rows, sem = refs[len(keys) :]
    p = lax.axis_index("col")
    width = row_count * part
    copies = []
    wide = own.shape[0]
    for kc, ref in zip(keys, pieces):
        for kq in range(row_count):
            for t in range(tm_count):
                source = ref.at[kq, :, pl.ds(t * wide, wide)]
                to = pl.multiple_of((t * col_count + (p ^ kc)) * width + kq * part, part)
                copies.append((source, gathered.at[pl.ds(to, part), :]))
                if kq == 0:
                    to = pl.multiple_of((p ^ kc) * shard_rows + t * part, part)
                    copies.append((source, own_rows.at[pl.ds(to, part), :]))
    run_copies(copies, sem)
    out[...] = gathered[...].astype(jnp.float32).T.astype(jnp.bfloat16)
    own[...] = own_rows[...].astype(jnp.float32).T.astype(jnp.bfloat16)


def source_of(r, col_count):
    tm, p = lax.axis_index("tm"), lax.axis_index("col")
    return (tm ^ (r // col_count)) * col_count + (p ^ (r % col_count))


def first_kernel(col_count, all_columns, own, *refs):
    columns_v, own_v, tiles_v, middle_v, sems = refs[-5:]
    (freqs, sources, places, part, rows) = tiles_v.shape
    tiles, outs = refs[:sources], refs[sources : sources + freqs]
    arriving = [copies_of([(all_columns, columns_v), (own, own_v)], sems.at[freqs])]
    arriving += [
        copies_of(
            [
                (ref.at[k], tiles_v.at[k, source_of(r, col_count)])
                for r, ref in enumerate(tiles)
            ],
            sems.at[k],
        )
        for k in range(freqs)
    ]
    wait_for(arriving[0])
    leaving = []
    for k in range(freqs):
        wait_for(arriving[1 + k])
        weights = tiles_v[k].reshape(sources * places * part, rows)
        first = jnp.dot(columns_v[...], weights, preferred_element_type=jnp.float32)
        middle_v[k] = (own_v[...].astype(jnp.float32) + damping * first).astype(jnp.bfloat16)
        leaving += copies_of([(middle_v.at[k], outs[k])], sems.at[freqs + 1])
    wait_for(leaving)


def weights_of(tiles_v, k, index, dims):
    (tm_count, col_count) = dims
    return jnp.concatenate(
        [tiles_v[t * col_count + p, k, index] for p in range(col_count) for t in range(tm_count)],
        axis=0,
    )


def near_kernel(dims, *refs):
    (tm_count, col_count, places) = dims
    sources, count = tm_count * col_count, len(places)
    (out, tiles_v, middles_v, total_v, sems) = refs[-5:]
    tiles, middles = refs[:sources], refs[sources:-5]
    freqs = total_v.shape[0]
    arriving = copies_of(
        [
            (ref.at[:, place], tiles_v.at[source_of(r, col_count), :, n])
            for n, place in enumerate(places)
            for r, ref in enumerate(tiles)
        ],
        sems.at[0],
    )
    arriving += copies_of(
        [(ref, middles_v.at[i // freqs, i % freqs]) for i, ref in enumerate(middles)], sems.at[0]
    )
    wait_for(arriving)
    for k in range(freqs):
        total = None
        for n in range(count):
            weights = weights_of(tiles_v, k, n, dims[:2])
            term = jnp.dot(middles_v[n, k], weights, preferred_element_type=jnp.float32)
            total = term if total is None else total + term
        total_v[k] = total
    wait_for(copies_of([(total_v, out)], sems.at[1]))


def far_kernel(dims, *refs):
    (tm_count, col_count, place, top, shard_rows, other) = dims
    sources = tm_count * col_count
    tiles, total, rest = refs[:sources], refs[sources], refs[sources + 1 :]
    middles, outs = rest[: -5 - top], rest[-5 - top : -5]
    (tiles_v, total_v, middle_v, second_v, sems) = rest[-5:]
    p = lax.axis_index("col")
    freqs = total_v.shape[0]
    span = top * shard_rows
    part_of = p // top
    lane = pl.multiple_of((1 - part_of if other else part_of) * span, span)
    pairs = [
        (ref.at[:, place, :, pl.ds(lane, span)], tiles_v.at[source_of(r, col_count), :, 0])
        for r, ref in enumerate(tiles)
    ]
    pairs += [(total.at[:, :, pl.ds(lane, span)], total_v)]
    pairs += [(ref, middle_v.at[k]) for k, ref in enumerate(middles)]
    wait_for(copies_of(pairs, sems.at[0]))
    for k in range(freqs):
        weights = weights_of(tiles_v, k, 0, dims[:2])
        term = jnp.dot(middle_v[k], weights, preferred_element_type=jnp.float32)
        second = (total_v[k] + term).T.astype(jnp.bfloat16)
        for i in range(top):
            second_v[i, k] = second[i * shard_rows : (i + 1) * shard_rows]
    slot = lax.rem(p, top)
    wait_for(copies_of([(second_v.at[slot ^ d], ref) for d, ref in enumerate(outs)], sems.at[1]))


def final_kernel(keys, splits, columns, *refs):
    pieces, (out, held, columns_v, out_v, sems) = refs[: len(keys)], refs[len(keys) :]
    p = lax.axis_index("col")
    pairs = [(ref, held.at[p ^ k]) for k, ref in zip(keys, pieces)] + [(columns, columns_v)]
    wait_for(copies_of(pairs, sems.at[0]))
    (count, freqs, shard_rows, wide) = held.shape
    step = max(16, shard_rows // 2)
    leaving = []
    for start in range(0, shard_rows, step):
        rows = slice(start, start + step)
        base = columns_v[rows].astype(jnp.float32)
        for source in range(count):
            lane = (source % splits) * wide
            for k in range(freqs):
                value = base[:, lane : lane + wide] + damping * held[source, k, rows].astype(
                    jnp.float32
                )
                out_v[rows, (source // splits) * freqs + k, lane : lane + wide] = value
        leaving += copies_of([(out_v.at[rows], out.at[rows])], sems.at[1])
    wait_for(leaving)


def shards(occ_orbitals, empty_orbitals, occ_rate, empty_rate, columns):
    tm_count, row_count, col_count = (lax.axis_size(a) for a in ("tm", "row", "col"))
    shard_rows, half = occ_orbitals.shape
    columns_wide = columns.shape[1]
    orbitals = tm_count * half
    part = shard_rows // tm_count
    width = row_count * part
    tile_rows = col_count * shard_rows
    col_index = lax.axis_index("col")
    both = (occ_orbitals, empty_orbitals)
    sources = tm_count * col_count
    local_freqs = NF // tm_count
    own_freqs = max(1, local_freqs // col_count)
    splits = max(1, col_count // local_freqs)
    columns_own = columns_wide // splits
    high, low = bits_of(col_count)[:-1], bits_of(col_count)[-1:]

    rows_of = [{(arr, 0, 0): value} for arr, value in enumerate(both)]
    own, other = pl.pallas_call(
        functools.partial(pack_kernel, (part, half, tm_count)),
        out_shape=(
            jax.ShapeDtypeStruct((part, 2 * half + tm_count * columns_wide), jnp.bfloat16),
            jax.ShapeDtypeStruct((tm_count - 1, part, 2 * half), jnp.bfloat16),
        ),
        in_specs=[HBM] * 3,
        out_specs=(VMEM, VMEM),
        scratch_shapes=[pltpu.SemaphoreType.DMA],
        compiler_params=FULL,
        name="pack",
    )(occ_orbitals, empty_orbitals, columns)
    got = [
        swap(other[kt - 1], "tm", kt) if tm_count > 2 else swap(other.reshape(part, -1), "tm", kt)
        for kt in range(1, tm_count)
    ]
    for bit in bits_of(tm_count):
        rows_of = [spread(pieces, "tm", bit, 1) for pieces in rows_of]
    near = [{k: v for k, v in pieces.items() if k[1] == 0} for pieces in rows_of]
    far = [{k: v for k, v in pieces.items() if k[1] != 0} for pieces in rows_of]
    for bit in high:
        near = [spread(pieces, "col", bit, 2) for pieces in near]
    streams, late = (0,), tuple(range(1, tm_count))
    cols_of = {(0, streams): own, (0, late): jnp.concatenate(got, axis=1) if len(got) > 1 else got[0]}

    def ring_step(group, source, target, step):
        cols_of[(target, group)] = shift(cols_of[(source, group)], "row", step)

    behind = (row_count - 1) // 2
    ahead = row_count // 2
    ring_step(streams, 0, 1, -1)
    if behind:
        ring_step(streams, 0, row_count - 1, 1)
    for bit in high:
        far = [spread(pieces, "col", bit, 2) for pieces in far]
    if behind:
        ring_step(late, 0, row_count - 1, 1)
    ring_step(late, 0, 1, -1)
    for k in range(2, ahead + 1):
        ring_step(streams, k - 1, k, -1)
    for k in range(2, behind + 1):
        ring_step(streams, row_count - k + 1, row_count - k, 1)
    for bit in low:
        near = [spread(pieces, "col", bit, 2) for pieces in near]
    for k in range(2, ahead + 1):
        ring_step(late, k - 1, k, -1)
    for k in range(2, behind + 1):
        ring_step(late, row_count - k + 1, row_count - k, 1)
    for bit in low:
        far = [spread(pieces, "col", bit, 2) for pieces in far]
    row_pieces = {**near[0], **near[1], **far[0], **far[1]}
    row_keys = list(row_pieces)

    picked = pl.pallas_call(
        functools.partial(pick_kernel, 2 * half),
        out_shape=jax.ShapeDtypeStruct((row_count, part, tm_count * columns_wide), jnp.bfloat16),
        in_specs=[HBM] * row_count,
        out_specs=VMEM,
        scratch_shapes=[pltpu.SemaphoreType.DMA],
        compiler_params=FULL,
        name="pick",
    )(*[cols_of[(kq, streams)] for kq in range(row_count)])
    column_pieces = {(0,): picked}
    for bit in high:
        column_pieces = spread(column_pieces, "col", bit, 0)
    for bit in low:
        column_pieces = spread(column_pieces, "col", bit, 0)

    cosine = time_tables(NT, NF)[1]
    rates = [rate.reshape(1, -1) for rate in (occ_rate, empty_rate)]
    block = min(16, part)
    mix = jnp.asarray(np.kron(cosine.astype(np.float32), np.eye(block)).astype(jnp.bfloat16))
    groups = [streams, late]
    pieces = [cols_of[(place, kts)] for place in range(row_count) for kts in groups]
    sent = pl.pallas_call(
        functools.partial(
            tile_kernel,
            row_keys,
            groups,
            (NT, NF, half, shard_rows, row_count, col_count, own_freqs, splits),
        ),
        out_shape=[
            jax.ShapeDtypeStruct((own_freqs, row_count, part, tile_rows), jnp.bfloat16)
        ]
        * sources,
        in_specs=[VMEM] * 3 + [HBM] * (len(row_keys) + len(pieces)),
        out_specs=[HBM] * sources,
        scratch_shapes=[
            pltpu.VMEM((2, tile_rows, orbitals), jnp.bfloat16),
            pltpu.VMEM((2, row_count, part, orbitals), jnp.bfloat16),
            pltpu.VMEM((2, NT * part, orbitals), jnp.bfloat16),
            pltpu.VMEM((row_count, NT * part, tile_rows), jnp.float32),
            pltpu.VMEM((2, NT, orbitals), jnp.float32),
            pltpu.VMEM((row_count, NF, part, tile_rows), jnp.bfloat16),
            pltpu.SemaphoreType.DMA((2,)),
            pltpu.SemaphoreType.DMA,
        ],
        compiler_params=FULL,
        name="tile",
    )(mix, *rates, *[row_pieces[k] for k in row_keys], *pieces)

    keys = [key[0] for key in column_pieces]
    all_columns, own_columns = pl.pallas_call(
        functools.partial(columns_kernel, keys, (tm_count, row_count, col_count, shard_rows, part)),
        out_shape=(
            jax.ShapeDtypeStruct((columns_wide, tm_count * col_count * width), jnp.bfloat16),
            jax.ShapeDtypeStruct((columns_wide, tile_rows), jnp.bfloat16),
        ),
        in_specs=[HBM] * len(keys),
        out_specs=(VMEM, VMEM),
        scratch_shapes=[
            pltpu.VMEM((tm_count * col_count * width, columns_wide), jnp.bfloat16),
            pltpu.VMEM((tile_rows, columns_wide), jnp.bfloat16),
            pltpu.SemaphoreType.DMA,
        ],
        compiler_params=FULL,
        name="columns",
    )(*column_pieces.values())

    if splits > 1:
        first_row = (col_index % splits) * columns_own
        all_columns = lax.dynamic_slice_in_dim(all_columns, first_row, columns_own, 0)
        own_columns = lax.dynamic_slice_in_dim(own_columns, first_row, columns_own, 0)
    far_first = sorted(range(1, sources), key=lambda r: -(r >= col_count) - (r % col_count > 1))
    tiles = [sent[0]] * sources
    for r in far_first:
        pairs = [(i, i ^ r) for i in range(sources)]
        tiles[r] = lax.ppermute(sent[r], ("tm", "col"), pairs)

    first_shape = (own_freqs, columns_own, tile_rows)
    middle = pl.pallas_call(
        functools.partial(first_kernel, col_count),
        out_shape=[jax.ShapeDtypeStruct(first_shape[1:], jnp.bfloat16)] * own_freqs,
        in_specs=[HBM] * (2 + sources),
        out_specs=[HBM] * own_freqs,
        scratch_shapes=[
            pltpu.VMEM((columns_own, sources * width), jnp.bfloat16),
            pltpu.VMEM((columns_own, tile_rows), jnp.bfloat16),
            pltpu.VMEM((own_freqs, sources, row_count, part, tile_rows), jnp.bfloat16),
            pltpu.VMEM(first_shape, jnp.bfloat16),
            pltpu.SemaphoreType.DMA((own_freqs + 2,)),
        ],
        compiler_params=FULL,
        name="first",
    )(all_columns, own_columns, *tiles)
    middles = {(0, k): value for k, value in enumerate(middle)}

    def middle_step(source, target, step):
        for k in range(own_freqs):
            middles[(target, k)] = shift(middles[(source, k)], "row", step)

    middle_step(0, 1, -1)
    for k in range(1, behind + 1):
        middle_step((row_count - k + 1) % row_count, row_count - k, 1)
    for k in range(2, ahead + 1):
        middle_step(k - 1, k, -1)
    own_range = range(own_freqs)
    last = ahead
    places = [k for k in range(row_count) if k != last]
    total = pl.pallas_call(
        functools.partial(near_kernel, (tm_count, col_count, places)),
        out_shape=jax.ShapeDtypeStruct(first_shape, jnp.float32),
        in_specs=[HBM] * (sources + len(places) * own_freqs),
        out_specs=HBM,
        scratch_shapes=[
            pltpu.VMEM((sources, own_freqs, len(places), part, tile_rows), jnp.bfloat16),
            pltpu.VMEM((len(places),) + first_shape, jnp.bfloat16),
            pltpu.VMEM(first_shape, jnp.float32),
            pltpu.SemaphoreType.DMA((2,)),
        ],
        compiler_params=FULL,
        name="near",
    )(*tiles, *[middles[(place, k)] for place in places for k in own_range])
    top = col_count // 2
    span = top * shard_rows
    seconds = []
    for other in (True, False):
        seconds.append(
            pl.pallas_call(
                functools.partial(far_kernel, (tm_count, col_count, last, top, shard_rows, other)),
                out_shape=[jax.ShapeDtypeStruct((own_freqs, shard_rows, columns_own), jnp.bfloat16)]
                * top,
                in_specs=[HBM] * (sources + 1 + own_freqs),
                out_specs=[HBM] * top,
                scratch_shapes=[
                    pltpu.VMEM((sources, own_freqs, 1, part, span), jnp.bfloat16),
                    pltpu.VMEM((own_freqs, columns_own, span), jnp.float32),
                    pltpu.VMEM(first_shape, jnp.bfloat16),
                    pltpu.VMEM((top, own_freqs, shard_rows, columns_own), jnp.bfloat16),
                    pltpu.SemaphoreType.DMA((2,)),
                ],
                compiler_params=FULL,
            )(*tiles, total, *[middles[(last, k)] for k in own_range])
        )
    parts = {0: seconds[1][0]}
    for group, start in ((seconds[0], top), (seconds[1], 0)):
        for d, value in enumerate(group):
            if start + d:
                parts[start + d] = swap(value, "col", start + d)
    return pl.pallas_call(
        functools.partial(final_kernel, list(parts), splits),
        out_shape=jax.ShapeDtypeStruct((shard_rows, local_freqs, columns_wide), jnp.float32),
        in_specs=[HBM] * (1 + len(parts)),
        out_specs=HBM,
        scratch_shapes=[
            pltpu.VMEM((col_count, own_freqs, shard_rows, columns_own), jnp.bfloat16),
            pltpu.VMEM((shard_rows, columns_wide), jnp.bfloat16),
            pltpu.VMEM((shard_rows, local_freqs, columns_wide), jnp.float32),
            pltpu.SemaphoreType.DMA((2,)),
        ],
        compiler_params=FULL,
        name="final",
    )(columns, *parts.values())


def solution(mesh):
    placed = (P(("col", "row"), "tm"), P(("col", "row"), "tm"), P(), P(), P(("col", "row"), None))
    return jax.shard_map(
        shards, mesh=mesh, in_specs=placed, out_specs=P(("col", "row"), "tm", None), check_vma=False
    )
```

time: 113 us -> 102 us (0.903)
  waiting for transfers between devices: 48.2 us -> 28.2 us
  Pallas kernels: 17.9 us -> 27.4 us
  starting transfers between devices: 39.3 us -> 44.8 us
  local copies, waits for them, and re-layouts: 4.94 us -> 1.33 us
  other arithmetic: 2.01 us -> 0 us
    ppermute x17 -> x21, waiting for transfers between devices: 20.9 us -> 7.25 us  [swap(): return lax.ppermute(value, axis, [(i, i ^ bit) for i in range(size)])]
    ppermute x9 -> x12, waiting for transfers between devices: 21.4 us -> 11.7 us  [shift(): lax.ppermute(value, axis, [(i, (i + step) % size) for i in range(size)])]
    ppermute x0 -> x7, waiting for transfers between devices: none -> 9.22 us  [shards(): tiles[r] = lax.ppermute(sent[r], ('tm', 'col'), pairs)]
    all_to_all x2 -> x0, starting transfers between devices: 7.79 us -> none  [the longest x1 4.26 us: shards(): lax.all_to_all(sent, ('tm', 'col'), split_axis=0, concat_axis=0, tiled=True)]
    pallas_call x2 -> x6, Pallas kernels: 5.36 us -> 13.1 us  [the longest x2 4.25 us: shards(): pl.pallas_call(functools.partial(far_kernel, (tm_count, col_count, last,...]
    ppermute x0 -> x7, starting transfers between devices: none -> 6.51 us  [shards(): tiles[r] = lax.ppermute(sent[r], ('tm', 'col'), pairs)]
    all_to_all x2 -> x0, waiting for transfers between devices: 5.95 us -> none  [the longest x1 5.95 us: shards(): lax.all_to_all(second, 'col', split_axis=0, concat_axis=0, tiled=True)]
    ppermute x17 -> x21, starting transfers between devices: 9.42 us -> 13.7 us  [swap(): return lax.ppermute(value, axis, [(i, i ^ bit) for i in range(size)])]
  transfers between devices with their start and end apart: 28 -> 40, of which waited for: 13 -> 16; matrix products, arithmetic and copies ran while one was open for 2% -> 0% of each run, Pallas kernels for 3% -> 20%
where the time goes in v3:
time: 102 us
  starting transfers between devices  44.8 us (44%)
  waiting for transfers between devices  28.2 us (28%)
  Pallas kernels  27.4 us (27%)
  local copies, waits for them, and re-layouts  1.33 us (1%)
    ppermute x12, starting transfers between devices, shift(): lax.ppermute(value, axis, [(i, (i + step) % size) for i in range(size)])  24.6 us
    ppermute x21, starting transfers between devices, swap(): return lax.ppermute(value, axis, [(i, i ^ bit) for i in range(size)])  13.7 us
    ppermute x12, waiting for transfers between devices, shift(): lax.ppermute(value, axis, [(i, (i + step) % size) for i in range(size)])  11.7 us
    pallas_call x1, Pallas kernels, shards(): pl.pallas_call(functools.partial(tile_kernel, row_keys, groups, (NT, NF,...  10.7 us
    ppermute x7, waiting for transfers between devices, shards(): tiles[r] = lax.ppermute(sent[r], ('tm', 'col'), pairs)  9.22 us
    ppermute x21, waiting for transfers between devices, swap(): return lax.ppermute(value, axis, [(i, i ^ bit) for i in range(size)])  7.25 us
    ppermute x7, starting transfers between devices, shards(): tiles[r] = lax.ppermute(sent[r], ('tm', 'col'), pairs)  6.51 us
    pallas_call x2, Pallas kernels, shards(): pl.pallas_call(functools.partial(far_kernel, (tm_count, col_count, last,...  4.25 us
  transfers between devices with their start and end apart: 40, of which 16 were waited for; matrix products, arithmetic and copies ran while one was open for 0% of the time, Pallas kernels for 20%

profile of v3, /device:TPU:0, one launch (start us, length us, event | category | flops | bytes accessed | tf_op | source)
XLA Modules:
  0.0 101.8 jit_solution(7289413921230510365)
XLA Ops:
  0.0 3.0 %collective-permute-start.6 = (bf16[64,1024]{1,0:T(8,128)(2,1)}, bf16[64,1024]{1,0:T(8,128)(2,1)}, u32[]{:S(2)}, u32[]{:S(2)}) collective-permute-start(bf16[64,1024]{1,0:T(8,128)(2,1)} %refs_0_.1), channel_id=1, source_target_pairs={{0,16},{16,0},{1,17},{17,1},{2,18},{18,2},{3,19},{19,3},{4,20},{20... | collective-permute-start | bytes 393224 | tf_op jit(solution)/shard_map/ppermute | solution.py:31
  3.0 1.5 %collective-permute-start = (bf16[64,1024]{1,0:T(8,128)(2,1)}, bf16[64,1024]{1,0:T(8,128)(2,1)}, u32[]{:S(2)}, u32[]{:S(2)}) collective-permute-start(bf16[64,1024]{1,0:T(8,128)(2,1)} %refs_0_.1), channel_id=1, source_target_pairs={{0,2},{1,3},{2,0},{3,1},{4,6},{5,7},{6,4},{7,5},{8,10},{9,11},{10,... | collective-permute-start | bytes 393224 | tf_op jit(solution)/shard_map/ppermute | solution.py:31
  4.5 0.5 collective-permute-start.10
  5.0 0.0 collective-permute-start.4
  5.0 1.7 %collective-permute-done.6.refs_8_ = bf16[64,1024]{1,0:T(8,128)(2,1)} collective-permute-done((bf16[64,1024]{1,0:T(8,128)(2,1)}, bf16[64,1024]{1,0:T(8,128)(2,1)}, u32[]{:S(2)}, u32[]{:S(2)}) %collective-permute-start.6) | collective-permute-done | bytes 131104 | tf_op jit(solution)/shard_map/ppermute | solution.py:31
  6.8 2.2 %collective-permute-start.3 = (bf16[64,1024]{1,0:T(8,128)(2,1)}, bf16[64,1024]{1,0:T(8,128)(2,1)}, u32[]{:S(2)}, u32[]{:S(2)}) collective-permute-start(bf16[64,1024]{1,0:T(8,128)(2,1)} %refs_4_.1), channel_id=1, source_target_pairs={{0,2},{1,3},{2,0},{3,1},{4,6},{5,7},{6,4},{7,5},{8,10},{9,11},{10,... | collective-permute-start | bytes 393224 | tf_op jit(solution)/shard_map/ppermute | solution.py:31
  9.0 1.7 %pack.1 = (bf16[32,2560]{1,0:T(8,128)(2,1)}, bf16[1,32,2048]{2,1,0:T(8,128)(2,1)}) custom-call(bf16[64,1024]{1,0:T(8,128)(2,1)} %refs_0_.1, bf16[64,1024]{1,0:T(8,128)(2,1)} %refs_4_.1, bf16[64,256]{1,0:T(8,128)(2,1)} %columns.5), custom_call_target="tpu_custom_call" | custom-call | tf_op jit(solution)/shard_map/pack/pallas_call | solution.py:322
  10.6 0.0 collective-permute-done.1.refs_2_
  10.6 2.3 %collective-permute-start.14 = (bf16[32,2048]{1,0:T(8,128)(2,1)}, bf16[32,2048]{1,0:T(8,128)(2,1)}, u32[]{:S(2)}, u32[]{:S(2)}) collective-permute-start(bf16[32,2048]{1,0:T(8,128)(2,1)} %bitcast.5), channel_id=1, source_target_pairs={{0,16},{16,0},{1,17},{17,1},{2,18},{18,2},{3,19},{19,3},{4,20},{20... | collective-permute-start | bytes 393224 | tf_op jit(solution)/shard_map/ppermute | solution.py:31
  12.9 3.6 %collective-permute-start.15 = (bf16[32,2560]{1,0:T(8,128)(2,1)}, bf16[32,2560]{1,0:T(8,128)(2,1)S(1)}, u32[]{:S(2)}, u32[]{:S(2)}) collective-permute-start(bf16[32,2560]{1,0:T(8,128)(2,1)} %get-tuple-element.23.refs_16_.refs_0_), channel_id=1, source_target_pairs={{0,12},{4,0},{8,4},{12,8},{1,13},{5,1},{9,5},{13,9},{2,14},{6,2},{... | collective-permute-start | bytes 491528 | tf_op jit(solution)/shard_map/ppermute | solution.py:36
  16.5 0.0 collective-permute-done.10.refs_12_
  16.5 0.0 collective-permute-start.19
  16.5 0.0 collective-permute-done.4.refs_6_
  16.5 0.1 collective-permute-start.8
  16.6 0.1 collective-permute-start.7
  16.7 0.5 collective-permute-start.2
  17.2 2.5 %collective-permute-done.15.refs_18_.refs_1_ = bf16[32,2560]{1,0:T(8,128)(2,1)S(1)} collective-permute-done((bf16[32,2560]{1,0:T(8,128)(2,1)}, bf16[32,2560]{1,0:T(8,128)(2,1)S(1)}, u32[]{:S(2)}, u32[]{:S(2)}) %collective-permute-start.15) | collective-permute-done | bytes 163872 | tf_op jit(solution)/shard_map/ppermute | solution.py:36
  19.7 0.7 copy-done
  20.4 4.2 %collective-permute-start.17 = (bf16[32,2560]{1,0:T(8,128)(2,1)S(1)}, bf16[32,2560]{1,0:T(8,128)(2,1)S(1)}, u32[]{:S(2)}, u32[]{:S(2)}) collective-permute-start(bf16[32,2560]{1,0:T(8,128)(2,1)S(1)} %collective-permute-done.15.refs_18_.refs_1_), channel_id=1, source_target_pairs={{0,12},{4,0},{8,4},{12,8},{1,13},{5,1},{9,5},{13,9},{2,14},{6,2},{... | collective-permute-start | bytes 491528 | tf_op jit(solution)/shard_map/ppermute | solution.py:36
  24.6 0.5 collective-permute-done.19.refs_22_.refs_3_
  25.2 0.1 collective-permute-start.11
  25.3 1.3 %collective-permute-start.16 = (bf16[32,2048]{1,0:T(8,128)(2,1)}, bf16[32,2048]{1,0:T(8,128)(2,1)}, u32[]{:S(2)}, u32[]{:S(2)}) collective-permute-start(bf16[32,2048]{1,0:T(8,128)(2,1)} %collective-permute-done.14.refs_17_), channel_id=1, source_target_pairs={{0,12},{4,0},{8,4},{12,8},{1,13},{5,1},{9,5},{13,9},{2,14},{6,2},{... | collective-permute-start | bytes 393224 | tf_op jit(solution)/shard_map/ppermute | solution.py:36
  26.6 0.1 collective-permute-done.12.refs_14_
  26.7 0.8 collective-permute-start.20
  27.5 3.9 %collective-permute-done.11.refs_13_ = bf16[64,1024]{1,0:T(8,128)(2,1)} collective-permute-done((bf16[64,1024]{1,0:T(8,128)(2,1)}, bf16[64,1024]{1,0:T(8,128)(2,1)}, u32[]{:S(2)}, u32[]{:S(2)}) %collective-permute-start.11) | collective-permute-done | bytes 131104 | tf_op jit(solution)/shard_map/ppermute | solution.py:31
  31.4 0.1 collective-permute-done.16.refs_19_
  31.5 0.4 collective-permute-start.13
  31.9 0.6 copy-done.2
  32.6 3.8 %collective-permute-start.18 = (bf16[32,2048]{1,0:T(8,128)(2,1)}, bf16[32,2048]{1,0:T(8,128)(2,1)}, u32[]{:S(2)}, u32[]{:S(2)}) collective-permute-start(bf16[32,2048]{1,0:T(8,128)(2,1)} %collective-permute-done.16.refs_19_), channel_id=1, source_target_pairs={{0,12},{4,0},{8,4},{12,8},{1,13},{5,1},{9,5},{13,9},{2,14},{6,2},{... | collective-permute-start | bytes 393224 | tf_op jit(solution)/shard_map/ppermute | solution.py:36
  36.3 1.5 %pick.1.refs_0_ = bf16[4,32,512]{2,1,0:T(8,128)(2,1)} custom-call(bf16[32,2560]{1,0:T(8,128)(2,1)} %get-tuple-element.23.refs_16_.refs_0_, bf16[32,2560]{1,0:T(8,128)(2,1)} %copy-done, bf16[32,2560]{1,0:T(8,128)(2,1)} %copy-done.2, bf16[32,2560]{1,0:T(8,128)(2,1)} %copy-done.1), custom_call_target="tpu_custom_call" | custom-call | tf_op jit(solution)/shard_map/pick/pallas_call | solution.py:375
  37.8 0.4 collective-permute-start.28
  38.2 0.2 collective-permute-start.29
  38.4 1.7 %collective-permute-done.18.refs_21_ = bf16[32,2048]{1,0:T(8,128)(2,1)} collective-permute-done((bf16[32,2048]{1,0:T(8,128)(2,1)}, bf16[32,2048]{1,0:T(8,128)(2,1)}, u32[]{:S(2)}, u32[]{:S(2)}) %collective-permute-start.18) | collective-permute-done | bytes 131104 | tf_op jit(solution)/shard_map/ppermute | solution.py:36
  40.1 10.7 %tile.1 = (bf16[2,4,32,256]{3,2,1,0:T(8,128)(2,1)}, bf16[2,4,32,256]{3,2,1,0:T(8,128)(2,1)}, bf16[2,4,32,256]{3,2,1,0:T(8,128)(2,1)}, bf16[2,4,32,256]{3,2,1,0:T...) custom-call(bf16[256,256]{1,0:T(8,128)(2,1)} %constant.2.clone.mix, ...), custom_call_target="tpu_custom_call" | custom-call | tf_op jit(solution)/shard_map/tile/pallas_call | solution.py:396
  50.8 0.1 collective-permute-start.21
  50.9 2.9 %collective-permute-start.22 = (bf16[2,4,32,256]{3,2,1,0:T(8,128)(2,1)}, bf16[2,4,32,256]{3,2,1,0:T(8,128)(2,1)}, u32[]{:S(2)}, u32[]{:S(2)}) collective-permute-start(bf16[2,4,32,256]{3,2,1,0:T(8,128)(2,1)} %get-tuple-element.27), channel_id=1, source_target_pairs={{0,2},{1,3},{2,0},{3,1},{16,18},{17,19},{18,16},{19,17},{4,6},{5,7... | collective-permute-start | bytes 393224 | tf_op jit(solution)/shard_map/ppermute | solution.py:449
  53.8 0.2 collective-permute-start.30
  53.9 0.1 collective-permute-start.23
  54.0 1.7 %collective-permute-start.25 = (bf16[2,4,32,256]{3,2,1,0:T(8,128)(2,1)}, bf16[2,4,32,256]{3,2,1,0:T(8,128)(2,1)}, u32[]{:S(2)}, u32[]{:S(2)}) collective-permute-start(bf16[2,4,32,256]{3,2,1,0:T(8,128)(2,1)} %get-tuple-element.30), channel_id=1, source_target_pairs={{0,17},{1,16},{2,19},{3,18},{16,1},{17,0},{18,3},{19,2},{4,21},{5,... | collective-permute-start | bytes 393224 | tf_op jit(solution)/shard_map/ppermute | solution.py:449
  55.7 2.8 %collective-permute-done.22.refs_2_ = bf16[2,4,32,256]{3,2,1,0:T(8,128)(2,1)} collective-permute-done((bf16[2,4,32,256]{3,2,1,0:T(8,128)(2,1)}, bf16[2,4,32,256]{3,2,1,0:T(8,128)(2,1)}, u32[]{:S(2)}, u32[]{:S(2)}) %collective-permute-start.22) | collective-permute-done | bytes 131104 | tf_op jit(solution)/shard_map/ppermute | solution.py:449
  58.4 1.3 %collective-permute-start.26 = (bf16[2,4,32,256]{3,2,1,0:T(8,128)(2,1)}, bf16[2,4,32,256]{3,2,1,0:T(8,128)(2,1)}, u32[]{:S(2)}, u32[]{:S(2)}) collective-permute-start(bf16[2,4,32,256]{3,2,1,0:T(8,128)(2,1)} %get-tuple-element.31), channel_id=1, source_target_pairs={{0,18},{1,19},{2,16},{3,17},{16,2},{17,3},{18,0},{19,1},{4,22},{5,... | collective-permute-start | bytes 393224 | tf_op jit(solution)/shard_map/ppermute | solution.py:449
  59.8 0.5 collective-permute-start.27
  60.3 2.1 %columns.4 = (bf16[256,1024]{1,0:T(8,128)(2,1)}, bf16[256,256]{1,0:T(8,128)(2,1)}) custom-call(bf16[4,32,512]{2,1,0:T(8,128)(2,1)} %pick.1.refs_0_, bf16[4,32,512]{2,1,0:T(8,128)(2,1)} %collective-permute-done.28.refs_1_, bf16[4,32,512]{2,1,0:T(8,128)(2,1)} %collective-permute-done.29.refs_2_, bf16[4,32,512]{2,1,0:T(8,128)(2,1)} %collective-permute-done.30.refs_3_), custom_call_target="tpu_custom_call" | custom-call | tf_op jit(solution)/shard_map/columns/pallas_call | solution.py:424
  62.4 5.3 %collective-permute-done.26.refs_6_ = bf16[2,4,32,256]{3,2,1,0:T(8,128)(2,1)} collective-permute-done((bf16[2,4,32,256]{3,2,1,0:T(8,128)(2,1)}, bf16[2,4,32,256]{3,2,1,0:T(8,128)(2,1)}, u32[]{:S(2)}, u32[]{:S(2)}) %collective-permute-start.26) | collective-permute-done | bytes 131104 | tf_op jit(solution)/shard_map/ppermute | solution.py:449
  67.7 1.2 %collective-permute-done.27.refs_7_ = bf16[2,4,32,256]{3,2,1,0:T(8,128)(2,1)} collective-permute-done((bf16[2,4,32,256]{3,2,1,0:T(8,128)(2,1)}, bf16[2,4,32,256]{3,2,1,0:T(8,128)(2,1)}, u32[]{:S(2)}, u32[]{:S(2)}) %collective-permute-start.27) | collective-permute-done | bytes 131104 | tf_op jit(solution)/shard_map/ppermute | solution.py:449
  68.8 2.7 %first.1 = (bf16[256,256]{1,0:T(8,128)(2,1)}, bf16[256,256]{1,0:T(8,128)(2,1)}) custom-call(bf16[256,1024]{1,0:T(8,128)(2,1)} %get-tuple-element.33.all_columns, bf16[256,256]{1,0:T(8,128)(2,1)} %get-tuple-element.34.own, bf16[2,4,32,256]{3,2,1,0:T(8,128)(2,1)} %get-tuple-element.25.refs_0_, bf16[2,4,32,256]{3,2,1,0:T(8,128)(2,1)} %collective-permute-done.21.refs_1_, ...), custom_call_target="tpu_custom_call" | custom-call | tf_op jit(solution)/shard_map/first/pallas_call | solution.py:452
  71.5 2.1 %collective-permute-start.31 = (bf16[256,256]{1,0:T(8,128)(2,1)}, bf16[256,256]{1,0:T(8,128)(2,1)}, u32[]{:S(2)}, u32[]{:S(2)}) collective-permute-start(bf16[256,256]{1,0:T(8,128)(2,1)} %get-tuple-element.35.refs_8_), channel_id=1, source_target_pairs={{0,12},{4,0},{8,4},{12,8},{1,13},{5,1},{9,5},{13,9},{2,14},{6,2},{... | collective-permute-start | bytes 393224 | tf_op jit(solution)/shard_map/ppermute | solution.py:36
  73.7 0.1 collective-permute-start.32
  73.7 2.0 %collective-permute-start.33 = (bf16[256,256]{1,0:T(8,128)(2,1)}, bf16[256,256]{1,0:T(8,128)(2,1)}, u32[]{:S(2)}, u32[]{:S(2)}) collective-permute-start(bf16[256,256]{1,0:T(8,128)(2,1)} %get-tuple-element.35.refs_8_), channel_id=1, source_target_pairs={{0,4},{4,8},{8,12},{12,0},{1,5},{5,9},{9,13},{13,1},{2,6},{6,10},{... | collective-permute-start | bytes 393224 | tf_op jit(solution)/shard_map/ppermute | solution.py:36
  75.7 0.0 collective-permute-start.34
  75.7 2.6 %collective-permute-done.31.refs_10_ = bf16[256,256]{1,0:T(8,128)(2,1)} collective-permute-done((bf16[256,256]{1,0:T(8,128)(2,1)}, bf16[256,256]{1,0:T(8,128)(2,1)}, u32[]{:S(2)}, u32[]{:S(2)}) %collective-permute-start.31) | collective-permute-done | bytes 131104 | tf_op jit(solution)/shard_map/ppermute | solution.py:36
  78.3 4.0 %collective-permute-start.35 = (bf16[256,256]{1,0:T(8,128)(2,1)}, bf16[256,256]{1,0:T(8,128)(2,1)}, u32[]{:S(2)}, u32[]{:S(2)}) collective-permute-start(bf16[256,256]{1,0:T(8,128)(2,1)} %collective-permute-done.31.refs_10_), channel_id=1, source_target_pairs={{0,12},{4,0},{8,4},{12,8},{1,13},{5,1},{9,5},{13,9},{2,14},{6,2},{... | collective-permute-start | bytes 393224 | tf_op jit(solution)/shard_map/ppermute | solution.py:36
  82.2 2.8 %collective-permute-start.36 = (bf16[256,256]{1,0:T(8,128)(2,1)}, bf16[256,256]{1,0:T(8,128)(2,1)}, u32[]{:S(2)}, u32[]{:S(2)}) collective-permute-start(bf16[256,256]{1,0:T(8,128)(2,1)} %collective-permute-done.32.refs_11_), channel_id=1, source_target_pairs={{0,12},{4,0},{8,4},{12,8},{1,13},{5,1},{9,5},{13,9},{2,14},{6,2},{... | collective-permute-start | bytes 393224 | tf_op jit(solution)/shard_map/ppermute | solution.py:36
  85.0 1.8 %collective-permute-done.34.refs_13_ = bf16[256,256]{1,0:T(8,128)(2,1)} collective-permute-done((bf16[256,256]{1,0:T(8,128)(2,1)}, bf16[256,256]{1,0:T(8,128)(2,1)}, u32[]{:S(2)}, u32[]{:S(2)}) %collective-permute-start.34) | collective-permute-done | bytes 131104 | tf_op jit(solution)/shard_map/ppermute | solution.py:36
  86.8 2.6 %near.1.refs_8_ = f32[2,256,256]{2,1,0:T(8,128)} custom-call(bf16[2,4,32,256]{3,2,1,0:T(8,128)(2,1)} %get-tuple-element.25.refs_0_, bf16[2,4,32,256]{3,2,1,0:T(8,128)(2,1)} %collective-permute-done.21.refs_1_, bf16[2,4,32,256]{3,2,1,0:T(8,128)(2,1)} %collective-permute-done.22.refs_2_, bf16[2,4,32,256]{3,2,1,0:T(8,128)(2,1)} %collective-permute-done.23.refs_3_, ...), custom_call_target="tpu_custom_call" | custom-call | tf_op jit(solution)/shard_map/near/pallas_call | solution.py:481
  89.5 0.1 collective-permute-done.35.refs_9_
  89.6 2.4 %collective-permute-done.36.refs_10_ = bf16[256,256]{1,0:T(8,128)(2,1)} collective-permute-done((bf16[256,256]{1,0:T(8,128)(2,1)}, bf16[256,256]{1,0:T(8,128)(2,1)}, u32[]{:S(2)}, u32[]{:S(2)}) %collective-permute-start.36) | collective-permute-done | bytes 131104 | tf_op jit(solution)/shard_map/ppermute | solution.py:36
  92.0 2.1 %shard_map.65 = (bf16[2,64,256]{2,1,0:T(8,128)(2,1)}, bf16[2,64,256]{2,1,0:T(8,128)(2,1)}) custom-call(bf16[2,4,32,256]{3,2,1,0:T(8,128)(2,1)} %get-tuple-element.25.refs_0_, bf16[2,4,32,256]{3,2,1,0:T(8,128)(2,1)} %collective-permute-done.21.refs_1_, bf16[2,4,32,256]{3,2,1,0:T(8,128)(2,1)} %collective-permute-done.22.refs_2_, ...), custom_call_target="tpu_custom_call" | custom-call | tf_op jit(solution)/shard_map/pallas_call | solution.py:500
  94.1 1.2 %collective-permute-start.37 = (bf16[2,64,256]{2,1,0:T(8,128)(2,1)}, bf16[2,64,256]{2,1,0:T(8,128)(2,1)}, u32[]{:S(2)}, u32[]{:S(2)}) collective-permute-start(bf16[2,64,256]{2,1,0:T(8,128)(2,1)} %get-tuple-element.38), channel_id=1, source_target_pairs={{0,2},{1,3},{2,0},{3,1},{4,6},{5,7},{6,4},{7,5},{8,10},{9,11},{10,... | collective-permute-start | bytes 196616 | tf_op jit(solution)/shard_map/ppermute | solution.py:31
  95.3 2.1 %shard_map.64 = (bf16[2,64,256]{2,1,0:T(8,128)(2,1)}, bf16[2,64,256]{2,1,0:T(8,128)(2,1)}) custom-call(bf16[2,4,32,256]{3,2,1,0:T(8,128)(2,1)} %get-tuple-element.25.refs_0_, bf16[2,4,32,256]{3,2,1,0:T(8,128)(2,1)} %collective-permute-done.21.refs_1_, bf16[2,4,32,256]{3,2,1,0:T(8,128)(2,1)} %collective-permute-done.22.refs_2_, ...), custom_call_target="tpu_custom_call" | custom-call | tf_op jit(solution)/shard_map/pallas_call | solution.py:500
  97.4 1.1 %collective-permute-start.39 = (bf16[2,64,256]{2,1,0:T(8,128)(2,1)}, bf16[2,64,256]{2,1,0:T(8,128)(2,1)}, u32[]{:S(2)}, u32[]{:S(2)}) collective-permute-start(bf16[2,64,256]{2,1,0:T(8,128)(2,1)} %get-tuple-element.40), channel_id=1, source_target_pairs={{0,1},{1,0},{2,3},{3,2},{4,5},{5,4},{6,7},{7,6},{8,9},{9,8},{10,11... | collective-permute-start | bytes 196616 | tf_op jit(solution)/shard_map/ppermute | solution.py:31
  98.5 0.4 collective-permute-done.37.refs_1_
  98.9 1.0 %collective-permute-done.38.refs_2_ = bf16[2,64,256]{2,1,0:T(8,128)(2,1)} collective-permute-done((bf16[2,64,256]{2,1,0:T(8,128)(2,1)}, bf16[2,64,256]{2,1,0:T(8,128)(2,1)}, u32[]{:S(2)}, u32[]{:S(2)}) %collective-permute-start.38) | collective-permute-done | bytes 65568 | tf_op jit(solution)/shard_map/ppermute | solution.py:31
  100.0 1.8 %final.1 = f32[64,8,256]{2,1,0:T(8,128)} custom-call(bf16[64,256]{1,0:T(8,128)(2,1)} %columns.5, bf16[2,64,256]{2,1,0:T(8,128)(2,1)} %get-tuple-element.37.refs_0_, bf16[2,64,256]{2,1,0:T(8,128)(2,1)} %collective-permute-done.37.refs_1_, bf16[2,64,256]{2,1,0:T(8,128)(2,1)} %collective-permute-done.38.refs_2_, bf16[2,64,256]{2,1,0:T(8,128)(2,1)} %collective-permute-done.39.refs_3_), custom_call_target="tpu_custom_call" | custom-call | tf_op jit(solution)/shard_map/final/pallas_call | solution.py:521
  (37 shorter events, 0.1 us)
Async XLA Ops:
  0.0 6.8 %collective-permute-start.6 = (bf16[64,1024]{1,0:T(8,128)(2,1)}, bf16[64,1024]{1,0:T(8,128)(2,1)}, u32[]{:S(2)}, u32[]{:S(2)}) collective-permute-start(bf16[64,1024]{1,0:T(8,128)(2,1)} %refs_0_.1), channel_id=1, source_target_pairs={{0,16},{16,0},{1,17},{17,1},{2,18},{18,2},{3,19},{19,3},{4,20},{20... | collective-permute-start | bytes 393224 | tf_op jit(solution)/shard_map/ppermute | solution.py:31
  3.0 7.7 %collective-permute-start.1 = (bf16[64,1024]{1,0:T(8,128)(2,1)}, bf16[64,1024]{1,0:T(8,128)(2,1)}, u32[]{:S(2)}, u32[]{:S(2)}) collective-permute-start(bf16[64,1024]{1,0:T(8,128)(2,1)} %refs_0_.1), channel_id=1, source_target_pairs={{0,1},{1,0},{2,3},{3,2},{4,5},{5,4},{6,7},{7,6},{8,9},{9,8},{10,11... | collective-permute-start | bytes 393224 | tf_op jit(solution)/shard_map/ppermute | solution.py:31
  3.0 9.9 %collective-permute-start = (bf16[64,1024]{1,0:T(8,128)(2,1)}, bf16[64,1024]{1,0:T(8,128)(2,1)}, u32[]{:S(2)}, u32[]{:S(2)}) collective-permute-start(bf16[64,1024]{1,0:T(8,128)(2,1)} %refs_0_.1), channel_id=1, source_target_pairs={{0,2},{1,3},{2,0},{3,1},{4,6},{5,7},{6,4},{7,5},{8,10},{9,11},{10,... | collective-permute-start | bytes 393224 | tf_op jit(solution)/shard_map/ppermute | solution.py:31
  4.5 12.0 %collective-permute-start.10 = (bf16[64,1024]{1,0:T(8,128)(2,1)}, bf16[64,1024]{1,0:T(8,128)(2,1)}, u32[]{:S(2)}, u32[]{:S(2)}) collective-permute-start(bf16[64,1024]{1,0:T(8,128)(2,1)} %refs_4_.1), channel_id=1, source_target_pairs={{0,16},{16,0},{1,17},{17,1},{2,18},{18,2},{3,19},{19,3},{4,20},{20... | collective-permute-start | bytes 393224 | tf_op jit(solution)/shard_map/ppermute | solution.py:31
  5.0 11.5 %collective-permute-start.4 = (bf16[64,1024]{1,0:T(8,128)(2,1)}, bf16[64,1024]{1,0:T(8,128)(2,1)}, u32[]{:S(2)}, u32[]{:S(2)}) collective-permute-start(bf16[64,1024]{1,0:T(8,128)(2,1)} %refs_4_.1), channel_id=1, source_target_pairs={{0,1},{1,0},{2,3},{3,2},{4,5},{5,4},{6,7},{7,6},{8,9},{9,8},{10,11... | collective-permute-start | bytes 393224 | tf_op jit(solution)/shard_map/ppermute | solution.py:31
  6.8 9.8 %collective-permute-start.3 = (bf16[64,1024]{1,0:T(8,128)(2,1)}, bf16[64,1024]{1,0:T(8,128)(2,1)}, u32[]{:S(2)}, u32[]{:S(2)}) collective-permute-start(bf16[64,1024]{1,0:T(8,128)(2,1)} %refs_4_.1), channel_id=1, source_target_pairs={{0,2},{1,3},{2,0},{3,1},{4,6},{5,7},{6,4},{7,5},{8,10},{9,11},{10,... | collective-permute-start | bytes 393224 | tf_op jit(solution)/shard_map/ppermute | solution.py:31
  10.6 6.1 %collective-permute-start.14 = (bf16[32,2048]{1,0:T(8,128)(2,1)}, bf16[32,2048]{1,0:T(8,128)(2,1)}, u32[]{:S(2)}, u32[]{:S(2)}) collective-permute-start(bf16[32,2048]{1,0:T(8,128)(2,1)} %bitcast.5), channel_id=1, source_target_pairs={{0,16},{16,0},{1,17},{17,1},{2,18},{18,2},{3,19},{19,3},{4,20},{20... | collective-permute-start | bytes 393224 | tf_op jit(solution)/shard_map/ppermute | solution.py:31
  12.9 6.8 %collective-permute-start.15 = (bf16[32,2560]{1,0:T(8,128)(2,1)}, bf16[32,2560]{1,0:T(8,128)(2,1)S(1)}, u32[]{:S(2)}, u32[]{:S(2)}) collective-permute-start(bf16[32,2560]{1,0:T(8,128)(2,1)} %get-tuple-element.23.refs_16_.refs_0_), channel_id=1, source_target_pairs={{0,12},{4,0},{8,4},{12,8},{1,13},{5,1},{9,5},{13,9},{2,14},{6,2},{... | collective-permute-start | bytes 491528 | tf_op jit(solution)/shard_map/ppermute | solution.py:36
  16.5 8.6 %collective-permute-start.19 = (bf16[32,2560]{1,0:T(8,128)(2,1)}, bf16[32,2560]{1,0:T(8,128)(2,1)S(1)}, u32[]{:S(2)}, u32[]{:S(2)}) collective-permute-start(bf16[32,2560]{1,0:T(8,128)(2,1)} %get-tuple-element.23.refs_16_.refs_0_), channel_id=1, source_target_pairs={{0,4},{4,8},{8,12},{12,0},{1,5},{5,9},{9,13},{13,1},{2,6},{6,10},{... | collective-permute-start | bytes 491528 | tf_op jit(solution)/shard_map/ppermute | solution.py:36
  16.5 8.6 %collective-permute-start.8 = (bf16[64,1024]{1,0:T(8,128)(2,1)}, bf16[64,1024]{1,0:T(8,128)(2,1)S(1)}, u32[]{:S(2)}, u32[]{:S(2)}) collective-permute-start(bf16[64,1024]{1,0:T(8,128)(2,1)} %collective-permute-done.6.refs_8_), channel_id=1, source_target_pairs={{0,1},{1,0},{2,3},{3,2},{4,5},{5,4},{6,7},{7,6},{8,9},{9,8},{10,11... | collective-permute-start | bytes 393224 | tf_op jit(solution)/shard_map/ppermute | solution.py:31
  16.6 8.6 %collective-permute-start.7 = (bf16[64,1024]{1,0:T(8,128)(2,1)}, bf16[64,1024]{1,0:T(8,128)(2,1)}, u32[]{:S(2)}, u32[]{:S(2)}) collective-permute-start(bf16[64,1024]{1,0:T(8,128)(2,1)} %collective-permute-done.6.refs_8_), channel_id=1, source_target_pairs={{0,2},{1,3},{2,0},{3,1},{4,6},{5,7},{6,4},{7,5},{8,10},{9,11},{10,... | collective-permute-start | bytes 393224 | tf_op jit(solution)/shard_map/ppermute | solution.py:31
  16.7 9.9 %collective-permute-start.2 = (bf16[64,1024]{1,0:T(8,128)(2,1)}, bf16[64,1024]{1,0:T(8,128)(2,1)S(1)}, u32[]{:S(2)}, u32[]{:S(2)}) collective-permute-start(bf16[64,1024]{1,0:T(8,128)(2,1)} %collective-permute-done.refs_1_), channel_id=1, source_target_pairs={{0,1},{1,0},{2,3},{3,2},{4,5},{5,4},{6,7},{7,6},{8,9},{9,8},{10,11... | collective-permute-start | bytes 393224 | tf_op jit(solution)/shard_map/ppermute | solution.py:31
  19.7 0.7 copy-start
  20.4 11.5 %collective-permute-start.17 = (bf16[32,2560]{1,0:T(8,128)(2,1)S(1)}, bf16[32,2560]{1,0:T(8,128)(2,1)S(1)}, u32[]{:S(2)}, u32[]{:S(2)}) collective-permute-start(bf16[32,2560]{1,0:T(8,128)(2,1)S(1)} %collective-permute-done.15.refs_18_.refs_1_), channel_id=1, source_target_pairs={{0,12},{4,0},{8,4},{12,8},{1,13},{5,1},{9,5},{13,9},{2,14},{6,2},{... | collective-permute-start | bytes 491528 | tf_op jit(solution)/shard_map/ppermute | solution.py:36
  25.2 6.8 %copy-start.1 = (bf16[32,2560]{1,0:T(8,128)(2,1)}, bf16[32,2560]{1,0:T(8,128)(2,1)S(1)}, u32[]{:S(2)}) copy-start(bf16[32,2560]{1,0:T(8,128)(2,1)S(1)} %collective-permute-done.19.refs_22_.refs_3_) | copy-start | bytes 491524
  25.2 1.6 %collective-permute-start.12 = (bf16[64,1024]{1,0:T(8,128)(2,1)}, bf16[64,1024]{1,0:T(8,128)(2,1)S(1)}, u32[]{:S(2)}, u32[]{:S(2)}) collective-permute-start(bf16[64,1024]{1,0:T(8,128)(2,1)} %collective-permute-done.10.refs_12_), channel_id=1, source_target_pairs={{0,1},{1,0},{2,3},{3,2},{4,5},{5,4},{6,7},{7,6},{8,9},{9,8},{10,11... | collective-permute-start | bytes 393224 | tf_op jit(solution)/shard_map/ppermute | solution.py:31
  25.2 6.7 %copy-start.3 = (bf16[64,1024]{1,0:T(8,128)(2,1)}, bf16[64,1024]{1,0:T(8,128)(2,1)S(1)}, u32[]{:S(2)}) copy-start(bf16[64,1024]{1,0:T(8,128)(2,1)S(1)} %collective-permute-done.8.refs_10_) | copy-start | bytes 393220
  25.2 6.2 %collective-permute-start.11 = (bf16[64,1024]{1,0:T(8,128)(2,1)}, bf16[64,1024]{1,0:T(8,128)(2,1)}, u32[]{:S(2)}, u32[]{:S(2)}) collective-permute-start(bf16[64,1024]{1,0:T(8,128)(2,1)} %collective-permute-done.10.refs_12_), channel_id=1, source_target_pairs={{0,2},{1,3},{2,0},{3,1},{4,6},{5,7},{6,4},{7,5},{8,10},{9,11},{10,... | collective-permute-start | bytes 393224 | tf_op jit(solution)/shard_map/ppermute | solution.py:31
  25.3 6.2 %collective-permute-start.16 = (bf16[32,2048]{1,0:T(8,128)(2,1)}, bf16[32,2048]{1,0:T(8,128)(2,1)}, u32[]{:S(2)}, u32[]{:S(2)}) collective-permute-start(bf16[32,2048]{1,0:T(8,128)(2,1)} %collective-permute-done.14.refs_17_), channel_id=1, source_target_pairs={{0,12},{4,0},{8,4},{12,8},{1,13},{5,1},{9,5},{13,9},{2,14},{6,2},{... | collective-permute-start | bytes 393224 | tf_op jit(solution)/shard_map/ppermute | solution.py:36
  26.6 5.3 %copy-start.4 = (bf16[64,1024]{1,0:T(8,128)(2,1)}, bf16[64,1024]{1,0:T(8,128)(2,1)S(1)}, u32[]{:S(2)}) copy-start(bf16[64,1024]{1,0:T(8,128)(2,1)S(1)} %collective-permute-done.2.refs_3_) | copy-start | bytes 393220
  26.6 11.2 %collective-permute-start.5 = (bf16[64,1024]{1,0:T(8,128)(2,1)}, bf16[64,1024]{1,0:T(8,128)(2,1)}, u32[]{:S(2)}, u32[]{:S(2)}) collective-permute-start(bf16[64,1024]{1,0:T(8,128)(2,1)} %collective-permute-done.3.refs_5_), channel_id=1, source_target_pairs={{0,1},{1,0},{2,3},{3,2},{4,5},{5,4},{6,7},{7,6},{8,9},{9,8},{10,11... | collective-permute-start | bytes 393224 | tf_op jit(solution)/shard_map/ppermute | solution.py:31
  26.7 5.2 %copy-start.5 = (bf16[64,1024]{1,0:T(8,128)(2,1)}, bf16[64,1024]{1,0:T(8,128)(2,1)S(1)}, u32[]{:S(2)}) copy-start(bf16[64,1024]{1,0:T(8,128)(2,1)S(1)} %collective-permute-done.12.refs_14_) | copy-start | bytes 393220
  26.7 11.5 %collective-permute-start.20 = (bf16[32,2048]{1,0:T(8,128)(2,1)}, bf16[32,2048]{1,0:T(8,128)(2,1)}, u32[]{:S(2)}, u32[]{:S(2)}) collective-permute-start(bf16[32,2048]{1,0:T(8,128)(2,1)} %collective-permute-done.14.refs_17_), channel_id=1, source_target_pairs={{0,4},{4,8},{8,12},{12,0},{1,5},{5,9},{9,13},{13,1},{2,6},{6,10},{... | collective-permute-start | bytes 393224 | tf_op jit(solution)/shard_map/ppermute | solution.py:36
  31.4 7.0 %collective-permute-start.9 = (bf16[64,1024]{1,0:T(8,128)(2,1)}, bf16[64,1024]{1,0:T(8,128)(2,1)}, u32[]{:S(2)}, u32[]{:S(2)}) collective-permute-start(bf16[64,1024]{1,0:T(8,128)(2,1)} %collective-permute-done.7.refs_9_), channel_id=1, source_target_pairs={{0,1},{1,0},{2,3},{3,2},{4,5},{5,4},{6,7},{7,6},{8,9},{9,8},{10,11... | collective-permute-start | bytes 393224 | tf_op jit(solution)/shard_map/ppermute | solution.py:31
  31.5 7.0 %collective-permute-start.13 = (bf16[64,1024]{1,0:T(8,128)(2,1)}, bf16[64,1024]{1,0:T(8,128)(2,1)}, u32[]{:S(2)}, u32[]{:S(2)}) collective-permute-start(bf16[64,1024]{1,0:T(8,128)(2,1)} %collective-permute-done.11.refs_13_), channel_id=1, source_target_pairs={{0,1},{1,0},{2,3},{3,2},{4,5},{5,4},{6,7},{7,6},{8,9},{9,8},{10,11... | collective-permute-start | bytes 393224 | tf_op jit(solution)/shard_map/ppermute | solution.py:31
  31.9 0.7 copy-start.2
  32.6 7.5 %collective-permute-start.18 = (bf16[32,2048]{1,0:T(8,128)(2,1)}, bf16[32,2048]{1,0:T(8,128)(2,1)}, u32[]{:S(2)}, u32[]{:S(2)}) collective-permute-start(bf16[32,2048]{1,0:T(8,128)(2,1)} %collective-permute-done.16.refs_19_), channel_id=1, source_target_pairs={{0,12},{4,0},{8,4},{12,8},{1,13},{5,1},{9,5},{13,9},{2,14},{6,2},{... | collective-permute-start | bytes 393224 | tf_op jit(solution)/shard_map/ppermute | solution.py:36
  37.8 15.9 %collective-permute-start.28 = (bf16[4,32,512]{2,1,0:T(8,128)(2,1)}, bf16[4,32,512]{2,1,0:T(8,128)(2,1)}, u32[]{:S(2)}, u32[]{:S(2)}) collective-permute-start(bf16[4,32,512]{2,1,0:T(8,128)(2,1)} %pick.1.refs_0_), channel_id=1, source_target_pairs={{0,2},{1,3},{2,0},{3,1},{4,6},{5,7},{6,4},{7,5},{8,10},{9,11},{10,... | collective-permute-start | bytes 393224 | tf_op jit(solution)/shard_map/ppermute | solution.py:31
  38.2 15.8 %collective-permute-start.29 = (bf16[4,32,512]{2,1,0:T(8,128)(2,1)}, bf16[4,32,512]{2,1,0:T(8,128)(2,1)}, u32[]{:S(2)}, u32[]{:S(2)}) collective-permute-start(bf16[4,32,512]{2,1,0:T(8,128)(2,1)} %pick.1.refs_0_), channel_id=1, source_target_pairs={{0,1},{1,0},{2,3},{3,2},{4,5},{5,4},{6,7},{7,6},{8,9},{9,8},{10,11... | collective-permute-start | bytes 393224 | tf_op jit(solution)/shard_map/ppermute | solution.py:31
  50.8 3.1 %collective-permute-start.21 = (bf16[2,4,32,256]{3,2,1,0:T(8,128)(2,1)}, bf16[2,4,32,256]{3,2,1,0:T(8,128)(2,1)}, u32[]{:S(2)}, u32[]{:S(2)}) collective-permute-start(bf16[2,4,32,256]{3,2,1,0:T(8,128)(2,1)} %get-tuple-element.26), channel_id=1, source_target_pairs={{0,1},{1,0},{2,3},{3,2},{16,17},{17,16},{18,19},{19,18},{4,5},{5,4... | collective-permute-start | bytes 393224 | tf_op jit(solution)/shard_map/ppermute | solution.py:449
  50.9 7.5 %collective-permute-start.22 = (bf16[2,4,32,256]{3,2,1,0:T(8,128)(2,1)}, bf16[2,4,32,256]{3,2,1,0:T(8,128)(2,1)}, u32[]{:S(2)}, u32[]{:S(2)}) collective-permute-start(bf16[2,4,32,256]{3,2,1,0:T(8,128)(2,1)} %get-tuple-element.27), channel_id=1, source_target_pairs={{0,2},{1,3},{2,0},{3,1},{16,18},{17,19},{18,16},{19,17},{4,6},{5,7... | collective-permute-start | bytes 393224 | tf_op jit(solution)/shard_map/ppermute | solution.py:449
  53.8 6.0 %collective-permute-start.30 = (bf16[4,32,512]{2,1,0:T(8,128)(2,1)}, bf16[4,32,512]{2,1,0:T(8,128)(2,1)}, u32[]{:S(2)}, u32[]{:S(2)}) collective-permute-start(bf16[4,32,512]{2,1,0:T(8,128)(2,1)} %collective-permute-done.28.refs_1_), channel_id=1, source_target_pairs={{0,1},{1,0},{2,3},{3,2},{4,5},{5,4},{6,7},{7,6},{8,9},{9,8},{10,11... | collective-permute-start | bytes 393224 | tf_op jit(solution)/shard_map/ppermute | solution.py:31
  53.9 8.4 %collective-permute-start.23 = (bf16[2,4,32,256]{3,2,1,0:T(8,128)(2,1)}, bf16[2,4,32,256]{3,2,1,0:T(8,128)(2,1)}, u32[]{:S(2)}, u32[]{:S(2)}) collective-permute-start(bf16[2,4,32,256]{3,2,1,0:T(8,128)(2,1)} %get-tuple-element.28), channel_id=1, source_target_pairs={{0,3},{1,2},{2,1},{3,0},{16,19},{17,18},{18,17},{19,16},{4,7},{5,6... | collective-permute-start | bytes 393224 | tf_op jit(solution)/shard_map/ppermute | solution.py:449
  54.0 8.4 %collective-permute-start.24 = (bf16[2,4,32,256]{3,2,1,0:T(8,128)(2,1)}, bf16[2,4,32,256]{3,2,1,0:T(8,128)(2,1)}, u32[]{:S(2)}, u32[]{:S(2)}) collective-permute-start(bf16[2,4,32,256]{3,2,1,0:T(8,128)(2,1)} %get-tuple-element.29), channel_id=1, source_target_pairs={{0,16},{1,17},{2,18},{3,19},{16,0},{17,1},{18,2},{19,3},{4,20},{5,... | collective-permute-start | bytes 393224 | tf_op jit(solution)/shard_map/ppermute | solution.py:449
  54.0 8.4 %collective-permute-start.25 = (bf16[2,4,32,256]{3,2,1,0:T(8,128)(2,1)}, bf16[2,4,32,256]{3,2,1,0:T(8,128)(2,1)}, u32[]{:S(2)}, u32[]{:S(2)}) collective-permute-start(bf16[2,4,32,256]{3,2,1,0:T(8,128)(2,1)} %get-tuple-element.30), channel_id=1, source_target_pairs={{0,17},{1,16},{2,19},{3,18},{16,1},{17,0},{18,3},{19,2},{4,21},{5,... | collective-permute-start | bytes 393224 | tf_op jit(solution)/shard_map/ppermute | solution.py:449
  58.4 9.2 %collective-permute-start.26 = (bf16[2,4,32,256]{3,2,1,0:T(8,128)(2,1)}, bf16[2,4,32,256]{3,2,1,0:T(8,128)(2,1)}, u32[]{:S(2)}, u32[]{:S(2)}) collective-permute-start(bf16[2,4,32,256]{3,2,1,0:T(8,128)(2,1)} %get-tuple-element.31), channel_id=1, source_target_pairs={{0,18},{1,19},{2,16},{3,17},{16,2},{17,3},{18,0},{19,1},{4,22},{5,... | collective-permute-start | bytes 393224 | tf_op jit(solution)/shard_map/ppermute | solution.py:449
  59.8 9.1 %collective-permute-start.27 = (bf16[2,4,32,256]{3,2,1,0:T(8,128)(2,1)}, bf16[2,4,32,256]{3,2,1,0:T(8,128)(2,1)}, u32[]{:S(2)}, u32[]{:S(2)}) collective-permute-start(bf16[2,4,32,256]{3,2,1,0:T(8,128)(2,1)} %get-tuple-element.32), channel_id=1, source_target_pairs={{0,19},{1,18},{2,17},{3,16},{16,3},{17,2},{18,1},{19,0},{4,23},{5,... | collective-permute-start | bytes 393224 | tf_op jit(solution)/shard_map/ppermute | solution.py:449
  71.5 6.7 %collective-permute-start.31 = (bf16[256,256]{1,0:T(8,128)(2,1)}, bf16[256,256]{1,0:T(8,128)(2,1)}, u32[]{:S(2)}, u32[]{:S(2)}) collective-permute-start(bf16[256,256]{1,0:T(8,128)(2,1)} %get-tuple-element.35.refs_8_), channel_id=1, source_target_pairs={{0,12},{4,0},{8,4},{12,8},{1,13},{5,1},{9,5},{13,9},{2,14},{6,2},{... | collective-permute-start | bytes 393224 | tf_op jit(solution)/shard_map/ppermute | solution.py:36
  73.7 8.6 %collective-permute-start.32 = (bf16[256,256]{1,0:T(8,128)(2,1)}, bf16[256,256]{1,0:T(8,128)(2,1)}, u32[]{:S(2)}, u32[]{:S(2)}) collective-permute-start(bf16[256,256]{1,0:T(8,128)(2,1)} %get-tuple-element.36.refs_9_), channel_id=1, source_target_pairs={{0,12},{4,0},{8,4},{12,8},{1,13},{5,1},{9,5},{13,9},{2,14},{6,2},{... | collective-permute-start | bytes 393224 | tf_op jit(solution)/shard_map/ppermute | solution.py:36
  73.7 11.3 %collective-permute-start.33 = (bf16[256,256]{1,0:T(8,128)(2,1)}, bf16[256,256]{1,0:T(8,128)(2,1)}, u32[]{:S(2)}, u32[]{:S(2)}) collective-permute-start(bf16[256,256]{1,0:T(8,128)(2,1)} %get-tuple-element.35.refs_8_), channel_id=1, source_target_pairs={{0,4},{4,8},{8,12},{12,0},{1,5},{5,9},{9,13},{13,1},{2,6},{6,10},{... | collective-permute-start | bytes 393224 | tf_op jit(solution)/shard_map/ppermute | solution.py:36
  75.7 11.1 %collective-permute-start.34 = (bf16[256,256]{1,0:T(8,128)(2,1)}, bf16[256,256]{1,0:T(8,128)(2,1)}, u32[]{:S(2)}, u32[]{:S(2)}) collective-permute-start(bf16[256,256]{1,0:T(8,128)(2,1)} %get-tuple-element.36.refs_9_), channel_id=1, source_target_pairs={{0,4},{4,8},{8,12},{12,0},{1,5},{5,9},{9,13},{13,1},{2,6},{6,10},{... | collective-permute-start | bytes 393224 | tf_op jit(solution)/shard_map/ppermute | solution.py:36
  78.3 11.3 %collective-permute-start.35 = (bf16[256,256]{1,0:T(8,128)(2,1)}, bf16[256,256]{1,0:T(8,128)(2,1)}, u32[]{:S(2)}, u32[]{:S(2)}) collective-permute-start(bf16[256,256]{1,0:T(8,128)(2,1)} %collective-permute-done.31.refs_10_), channel_id=1, source_target_pairs={{0,12},{4,0},{8,4},{12,8},{1,13},{5,1},{9,5},{13,9},{2,14},{6,2},{... | collective-permute-start | bytes 393224 | tf_op jit(solution)/shard_map/ppermute | solution.py:36
  82.2 9.7 %collective-permute-start.36 = (bf16[256,256]{1,0:T(8,128)(2,1)}, bf16[256,256]{1,0:T(8,128)(2,1)}, u32[]{:S(2)}, u32[]{:S(2)}) collective-permute-start(bf16[256,256]{1,0:T(8,128)(2,1)} %collective-permute-done.32.refs_11_), channel_id=1, source_target_pairs={{0,12},{4,0},{8,4},{12,8},{1,13},{5,1},{9,5},{13,9},{2,14},{6,2},{... | collective-permute-start | bytes 393224 | tf_op jit(solution)/shard_map/ppermute | solution.py:36
  94.1 4.8 %collective-permute-start.37 = (bf16[2,64,256]{2,1,0:T(8,128)(2,1)}, bf16[2,64,256]{2,1,0:T(8,128)(2,1)}, u32[]{:S(2)}, u32[]{:S(2)}) collective-permute-start(bf16[2,64,256]{2,1,0:T(8,128)(2,1)} %get-tuple-element.38), channel_id=1, source_target_pairs={{0,2},{1,3},{2,0},{3,1},{4,6},{5,7},{6,4},{7,5},{8,10},{9,11},{10,... | collective-permute-start | bytes 196616 | tf_op jit(solution)/shard_map/ppermute | solution.py:31
  95.3 4.7 %collective-permute-start.38 = (bf16[2,64,256]{2,1,0:T(8,128)(2,1)}, bf16[2,64,256]{2,1,0:T(8,128)(2,1)}, u32[]{:S(2)}, u32[]{:S(2)}) collective-permute-start(bf16[2,64,256]{2,1,0:T(8,128)(2,1)} %get-tuple-element.39), channel_id=1, source_target_pairs={{0,3},{1,2},{2,1},{3,0},{4,7},{5,6},{6,5},{7,4},{8,11},{9,10},{10,... | collective-permute-start | bytes 196616 | tf_op jit(solution)/shard_map/ppermute | solution.py:31
  97.4 2.6 %collective-permute-start.39 = (bf16[2,64,256]{2,1,0:T(8,128)(2,1)}, bf16[2,64,256]{2,1,0:T(8,128)(2,1)}, u32[]{:S(2)}, u32[]{:S(2)}) collective-permute-start(bf16[2,64,256]{2,1,0:T(8,128)(2,1)} %get-tuple-element.40), channel_id=1, source_target_pairs={{0,1},{1,0},{2,3},{3,2},{4,5},{5,4},{6,7},{7,6},{8,9},{9,8},{10,11... | collective-permute-start | bytes 196616 | tf_op jit(solution)/shard_map/ppermute | solution.py:31

commit v4 on v3

--- a/solution.py
+++ b/solution.py
@@ -13,6 +13,8 @@
 
 damping = 0.3
 
+BATCH = 1
+
 FULL = pltpu.CompilerParams(vmem_limit_bytes=67043328)
 HBM = pl.BlockSpec(memory_space=pltpu.HBM)
 VMEM = pl.BlockSpec(memory_space=pltpu.VMEM)
@@ -74,7 +76,7 @@
     row_pieces = refs[: len(row_keys)]
     pieces = refs[len(row_pieces) :][: places * len(groups)]
     rest = refs[len(row_pieces) + len(pieces) :]
-    outs, (rows, cols, scaled, greens, factors, spectral, sems, out_sem) = rest[:-8], rest[-8:]
+    outs, (rows, cols, scaled, factors, spectral, sems, out_sem) = rest[:-7], rest[-7:]
     tm, p = lax.axis_index("tm"), lax.axis_index("col")
     part = cols.shape[2]
     local_freqs = freqs // (len(outs) // col_count)
@@ -96,36 +98,43 @@
         factors[arr] = jnp.exp(-rate[...] * (0.25 * (steps + 0.5)))
     block = mix.shape[0] // freqs
     span = block * times
-
-    def green(arr, n):
-        slot = (arr * places + n) % scaled.shape[0]
-        for g in range(part // block):
-            values = cols[arr, n, pl.ds(g * block, block), :].astype(jnp.float32)
-            for j in range(times):
-                factor = factors[arr, pl.ds(j, 1), :]
-                scaled[slot, pl.ds(g * span + j * block, block), :] = (values * factor).astype(
+    batch = scaled.shape[1] // (part * times)
+    for first in range(0, places, batch):
+        greens = []
+        for arr in range(2):
+            if first == 0:
+                wait_for(arriving[arr])
+            for m in range(batch):
+                for g in range(part // block):
+                    values = cols[arr, first + m, pl.ds(g * block, block), :].astype(jnp.float32)
+                    start = m * part * times + g * span
+                    for j in range(times):
+                        factor = factors[arr, pl.ds(j, 1), :]
+                        scaled[arr, pl.ds(start + j * block, block), :] = (values * factor).astype(
+                            jnp.bfloat16
+                        )
+            greens.append(
+                lax.dot_general(
+                    scaled[arr],
+                    rows[arr],
+                    (((1,), (1,)), ((), ())),
+                    preferred_element_type=jnp.float32,
+                )
+            )
+        polar = (-2.0 * greens[0] * greens[1]).astype(jnp.bfloat16)
+        for m in range(batch):
+            for g in range(part // block):
+                start = m * part * times + g * span
+                total = jnp.dot(
+                    mix[...], polar[start : start + span], preferred_element_type=jnp.float32
+                )
+                spectral[first + m, :, pl.ds(g * block, block), :] = total.astype(
                     jnp.bfloat16
-                )
-        return lax.dot_general(
-            scaled[slot], rows[arr], (((1,), (1,)), ((), ())), preferred_element_type=jnp.float32
-        )
-
-    wait_for(arriving[0])
-    for n in range(places):
-        greens[n] = -2.0 * green(0, n)
-    wait_for(arriving[1])
-    for n in range(places):
-        polar = (greens[n] * green(1, n)).astype(jnp.bfloat16)
-        for g in range(part // block):
-            total = jnp.dot(
-                mix[...], polar[g * span : (g + 1) * span], preferred_element_type=jnp.float32
-            )
-            spectral[n, :, pl.ds(g * block, block), :] = total.astype(jnp.bfloat16).reshape(
-                freqs, block, total.shape[1]
-            )
+                ).reshape(freqs, block, total.shape[1])
+        n = first + batch - 1
         if len(outs) <= 8 or n == places - 1:
-            done = slice(n, n + 1) if len(outs) <= 8 else slice(0, places)
-            leaving = leaving if n else []
+            done = slice(first, n + 1) if len(outs) <= 8 else slice(0, places)
+            leaving = leaving if first else []
             for r, ref in enumerate(outs):
                 to_tm, to_col = tm ^ (r // col_count), p ^ (r % col_count)
                 start = to_tm * local_freqs + (to_col // splits) * own_freqs
@@ -409,8 +418,7 @@
         scratch_shapes=[
             pltpu.VMEM((2, tile_rows, orbitals), jnp.bfloat16),
             pltpu.VMEM((2, row_count, part, orbitals), jnp.bfloat16),
-            pltpu.VMEM((2, NT * part, orbitals), jnp.bfloat16),
-            pltpu.VMEM((row_count, NT * part, tile_rows), jnp.float32),
+            pltpu.VMEM((2, BATCH * NT * part, orbitals), jnp.bfloat16),
             pltpu.VMEM((2, NT, orbitals), jnp.float32),
             pltpu.VMEM((row_count, NF, part, tile_rows), jnp.bfloat16),
             pltpu.SemaphoreType.DMA((2,)),

time: 102 us -> 101 us (level)
  Pallas kernels: 27.4 us -> 26.3 us
    pallas_call x1, Pallas kernels: 10.7 us -> 9.65 us  [shards(): pl.pallas_call(functools.partial(tile_kernel, row_keys, groups, (NT, NF,...]
  transfers between devices with their start and end apart: 40 -> 40, of which waited for: 16 -> 16; matrix products, arithmetic and copies ran while one was open for 0% -> 0% of each run, Pallas kernels for 20% -> 19%
where the time goes in v4:
time: 101 us
  starting transfers between devices  44.7 us (44%)
  waiting for transfers between devices  28.1 us (28%)
  Pallas kernels  26.3 us (26%)
  local copies, waits for them, and re-layouts  1.33 us (1%)
    ppermute x12, starting transfers between devices, shift(): lax.ppermute(value, axis, [(i, (i + step) % size) for i in range(size)])  24.6 us
    ppermute x21, starting transfers between devices, swap(): return lax.ppermute(value, axis, [(i, i ^ bit) for i in range(size)])  13.6 us
    ppermute x12, waiting for transfers between devices, shift(): lax.ppermute(value, axis, [(i, (i + step) % size) for i in range(size)])  11.7 us
    pallas_call x1, Pallas kernels, shards(): pl.pallas_call(functools.partial(tile_kernel, row_keys, groups, (NT, NF,...  9.65 us
    ppermute x7, waiting for transfers between devices, shards(): tiles[r] = lax.ppermute(sent[r], ('tm', 'col'), pairs)  9.22 us
    ppermute x21, waiting for transfers between devices, swap(): return lax.ppermute(value, axis, [(i, i ^ bit) for i in range(size)])  7.25 us
    ppermute x7, starting transfers between devices, shards(): tiles[r] = lax.ppermute(sent[r], ('tm', 'col'), pairs)  6.5 us
    pallas_call x2, Pallas kernels, shards(): pl.pallas_call(functools.partial(far_kernel, (tm_count, col_count, last,...  4.26 us
  transfers between devices with their start and end apart: 40, of which 16 were waited for; matrix products, arithmetic and copies ran while one was open for 0% of the time, Pallas kernels for 19%

profile of v4, /device:TPU:0, one launch (start us, length us, event | category | flops | bytes accessed | tf_op | source)
XLA Modules:
  0.0 100.7 jit_solution(17532172717039954100)
XLA Ops:
  0.0 3.0 %collective-permute-start.6 = (bf16[64,1024]{1,0:T(8,128)(2,1)}, bf16[64,1024]{1,0:T(8,128)(2,1)}, u32[]{:S(2)}, u32[]{:S(2)}) collective-permute-start(bf16[64,1024]{1,0:T(8,128)(2,1)} %refs_0_.1), channel_id=1, source_target_pairs={{0,16},{16,0},{1,17},{17,1},{2,18},{18,2},{3,19},{19,3},{4,20},{20... | collective-permute-start | bytes 393224 | tf_op jit(solution)/shard_map/ppermute | solution.py:33
  3.0 1.5 %collective-permute-start = (bf16[64,1024]{1,0:T(8,128)(2,1)}, bf16[64,1024]{1,0:T(8,128)(2,1)}, u32[]{:S(2)}, u32[]{:S(2)}) collective-permute-start(bf16[64,1024]{1,0:T(8,128)(2,1)} %refs_0_.1), channel_id=1, source_target_pairs={{0,2},{1,3},{2,0},{3,1},{4,6},{5,7},{6,4},{7,5},{8,10},{9,11},{10,... | collective-permute-start | bytes 393224 | tf_op jit(solution)/shard_map/ppermute | solution.py:33
  4.5 0.5 collective-permute-start.10
  5.0 0.0 collective-permute-start.4
  5.0 1.7 %collective-permute-done.6.refs_8_ = bf16[64,1024]{1,0:T(8,128)(2,1)} collective-permute-done((bf16[64,1024]{1,0:T(8,128)(2,1)}, bf16[64,1024]{1,0:T(8,128)(2,1)}, u32[]{:S(2)}, u32[]{:S(2)}) %collective-permute-start.6) | collective-permute-done | bytes 131104 | tf_op jit(solution)/shard_map/ppermute | solution.py:33
  6.8 2.2 %collective-permute-start.3 = (bf16[64,1024]{1,0:T(8,128)(2,1)}, bf16[64,1024]{1,0:T(8,128)(2,1)}, u32[]{:S(2)}, u32[]{:S(2)}) collective-permute-start(bf16[64,1024]{1,0:T(8,128)(2,1)} %refs_4_.1), channel_id=1, source_target_pairs={{0,2},{1,3},{2,0},{3,1},{4,6},{5,7},{6,4},{7,5},{8,10},{9,11},{10,... | collective-permute-start | bytes 393224 | tf_op jit(solution)/shard_map/ppermute | solution.py:33
  9.0 1.7 %pack.1 = (bf16[32,2560]{1,0:T(8,128)(2,1)}, bf16[1,32,2048]{2,1,0:T(8,128)(2,1)}) custom-call(bf16[64,1024]{1,0:T(8,128)(2,1)} %refs_0_.1, bf16[64,1024]{1,0:T(8,128)(2,1)} %refs_4_.1, bf16[64,256]{1,0:T(8,128)(2,1)} %columns.5), custom_call_target="tpu_custom_call" | custom-call | tf_op jit(solution)/shard_map/pack/pallas_call | solution.py:331
  10.6 0.0 collective-permute-done.1.refs_2_
  10.6 2.3 %collective-permute-start.14 = (bf16[32,2048]{1,0:T(8,128)(2,1)}, bf16[32,2048]{1,0:T(8,128)(2,1)}, u32[]{:S(2)}, u32[]{:S(2)}) collective-permute-start(bf16[32,2048]{1,0:T(8,128)(2,1)} %bitcast.5), channel_id=1, source_target_pairs={{0,16},{16,0},{1,17},{17,1},{2,18},{18,2},{3,19},{19,3},{4,20},{20... | collective-permute-start | bytes 393224 | tf_op jit(solution)/shard_map/ppermute | solution.py:33
  12.9 3.6 %collective-permute-start.15 = (bf16[32,2560]{1,0:T(8,128)(2,1)}, bf16[32,2560]{1,0:T(8,128)(2,1)S(1)}, u32[]{:S(2)}, u32[]{:S(2)}) collective-permute-start(bf16[32,2560]{1,0:T(8,128)(2,1)} %get-tuple-element.23.refs_16_.refs_0_), channel_id=1, source_target_pairs={{0,12},{4,0},{8,4},{12,8},{1,13},{5,1},{9,5},{13,9},{2,14},{6,2},{... | collective-permute-start | bytes 491528 | tf_op jit(solution)/shard_map/ppermute | solution.py:38
  16.5 0.0 collective-permute-done.10.refs_12_
  16.5 0.0 collective-permute-start.19
  16.5 0.0 collective-permute-done.4.refs_6_
  16.5 0.1 collective-permute-start.8
  16.6 0.1 collective-permute-start.7
  16.7 0.5 collective-permute-start.2
  17.2 2.5 %collective-permute-done.15.refs_18_.refs_1_ = bf16[32,2560]{1,0:T(8,128)(2,1)S(1)} collective-permute-done((bf16[32,2560]{1,0:T(8,128)(2,1)}, bf16[32,2560]{1,0:T(8,128)(2,1)S(1)}, u32[]{:S(2)}, u32[]{:S(2)}) %collective-permute-start.15) | collective-permute-done | bytes 163872 | tf_op jit(solution)/shard_map/ppermute | solution.py:38
  19.7 0.7 copy-done
  20.4 4.2 %collective-permute-start.17 = (bf16[32,2560]{1,0:T(8,128)(2,1)S(1)}, bf16[32,2560]{1,0:T(8,128)(2,1)S(1)}, u32[]{:S(2)}, u32[]{:S(2)}) collective-permute-start(bf16[32,2560]{1,0:T(8,128)(2,1)S(1)} %collective-permute-done.15.refs_18_.refs_1_), channel_id=1, source_target_pairs={{0,12},{4,0},{8,4},{12,8},{1,13},{5,1},{9,5},{13,9},{2,14},{6,2},{... | collective-permute-start | bytes 491528 | tf_op jit(solution)/shard_map/ppermute | solution.py:38
  24.6 0.5 collective-permute-done.19.refs_22_.refs_3_
  25.2 0.1 collective-permute-start.11
  25.3 1.3 %collective-permute-start.16 = (bf16[32,2048]{1,0:T(8,128)(2,1)}, bf16[32,2048]{1,0:T(8,128)(2,1)}, u32[]{:S(2)}, u32[]{:S(2)}) collective-permute-start(bf16[32,2048]{1,0:T(8,128)(2,1)} %collective-permute-done.14.refs_17_), channel_id=1, source_target_pairs={{0,12},{4,0},{8,4},{12,8},{1,13},{5,1},{9,5},{13,9},{2,14},{6,2},{... | collective-permute-start | bytes 393224 | tf_op jit(solution)/shard_map/ppermute | solution.py:38
  26.6 0.1 collective-permute-done.12.refs_14_
  26.7 0.8 collective-permute-start.20
  27.5 3.9 %collective-permute-done.11.refs_13_ = bf16[64,1024]{1,0:T(8,128)(2,1)} collective-permute-done((bf16[64,1024]{1,0:T(8,128)(2,1)}, bf16[64,1024]{1,0:T(8,128)(2,1)}, u32[]{:S(2)}, u32[]{:S(2)}) %collective-permute-start.11) | collective-permute-done | bytes 131104 | tf_op jit(solution)/shard_map/ppermute | solution.py:33
  31.4 0.1 collective-permute-done.16.refs_19_
  31.5 0.4 collective-permute-start.13
  31.9 0.6 copy-done.2
  32.6 3.8 %collective-permute-start.18 = (bf16[32,2048]{1,0:T(8,128)(2,1)}, bf16[32,2048]{1,0:T(8,128)(2,1)}, u32[]{:S(2)}, u32[]{:S(2)}) collective-permute-start(bf16[32,2048]{1,0:T(8,128)(2,1)} %collective-permute-done.16.refs_19_), channel_id=1, source_target_pairs={{0,12},{4,0},{8,4},{12,8},{1,13},{5,1},{9,5},{13,9},{2,14},{6,2},{... | collective-permute-start | bytes 393224 | tf_op jit(solution)/shard_map/ppermute | solution.py:38
  36.3 1.5 %pick.1.refs_0_ = bf16[4,32,512]{2,1,0:T(8,128)(2,1)} custom-call(bf16[32,2560]{1,0:T(8,128)(2,1)} %get-tuple-element.23.refs_16_.refs_0_, bf16[32,2560]{1,0:T(8,128)(2,1)} %copy-done, bf16[32,2560]{1,0:T(8,128)(2,1)} %copy-done.2, bf16[32,2560]{1,0:T(8,128)(2,1)} %copy-done.1), custom_call_target="tpu_custom_call" | custom-call | tf_op jit(solution)/shard_map/pick/pallas_call | solution.py:384
  37.8 0.4 collective-permute-start.28
  38.2 0.2 collective-permute-start.29
  38.4 1.7 %collective-permute-done.18.refs_21_ = bf16[32,2048]{1,0:T(8,128)(2,1)} collective-permute-done((bf16[32,2048]{1,0:T(8,128)(2,1)}, bf16[32,2048]{1,0:T(8,128)(2,1)}, u32[]{:S(2)}, u32[]{:S(2)}) %collective-permute-start.18) | collective-permute-done | bytes 131104 | tf_op jit(solution)/shard_map/ppermute | solution.py:38
  40.1 9.7 %tile.1 = (bf16[2,4,32,256]{3,2,1,0:T(8,128)(2,1)}, bf16[2,4,32,256]{3,2,1,0:T(8,128)(2,1)}, bf16[2,4,32,256]{3,2,1,0:T(8,128)(2,1)}, bf16[2,4,32,256]{3,2,1,0:T...) custom-call(bf16[256,256]{1,0:T(8,128)(2,1)} %constant.2.clone.mix, ...), custom_call_target="tpu_custom_call" | custom-call | tf_op jit(solution)/shard_map/tile/pallas_call | solution.py:405
  49.7 0.1 collective-permute-start.21
  49.8 2.9 %collective-permute-start.22 = (bf16[2,4,32,256]{3,2,1,0:T(8,128)(2,1)}, bf16[2,4,32,256]{3,2,1,0:T(8,128)(2,1)}, u32[]{:S(2)}, u32[]{:S(2)}) collective-permute-start(bf16[2,4,32,256]{3,2,1,0:T(8,128)(2,1)} %get-tuple-element.27), channel_id=1, source_target_pairs={{0,2},{1,3},{2,0},{3,1},{16,18},{17,19},{18,16},{19,17},{4,6},{5,7... | collective-permute-start | bytes 393224 | tf_op jit(solution)/shard_map/ppermute | solution.py:457
  52.7 0.2 collective-permute-start.30
  52.8 0.1 collective-permute-start.23
  52.9 1.7 %collective-permute-start.25 = (bf16[2,4,32,256]{3,2,1,0:T(8,128)(2,1)}, bf16[2,4,32,256]{3,2,1,0:T(8,128)(2,1)}, u32[]{:S(2)}, u32[]{:S(2)}) collective-permute-start(bf16[2,4,32,256]{3,2,1,0:T(8,128)(2,1)} %get-tuple-element.30), channel_id=1, source_target_pairs={{0,17},{1,16},{2,19},{3,18},{16,1},{17,0},{18,3},{19,2},{4,21},{5,... | collective-permute-start | bytes 393224 | tf_op jit(solution)/shard_map/ppermute | solution.py:457
  54.6 2.8 %collective-permute-done.22.refs_2_ = bf16[2,4,32,256]{3,2,1,0:T(8,128)(2,1)} collective-permute-done((bf16[2,4,32,256]{3,2,1,0:T(8,128)(2,1)}, bf16[2,4,32,256]{3,2,1,0:T(8,128)(2,1)}, u32[]{:S(2)}, u32[]{:S(2)}) %collective-permute-start.22) | collective-permute-done | bytes 131104 | tf_op jit(solution)/shard_map/ppermute | solution.py:457
  57.3 1.3 %collective-permute-start.26 = (bf16[2,4,32,256]{3,2,1,0:T(8,128)(2,1)}, bf16[2,4,32,256]{3,2,1,0:T(8,128)(2,1)}, u32[]{:S(2)}, u32[]{:S(2)}) collective-permute-start(bf16[2,4,32,256]{3,2,1,0:T(8,128)(2,1)} %get-tuple-element.31), channel_id=1, source_target_pairs={{0,18},{1,19},{2,16},{3,17},{16,2},{17,3},{18,0},{19,1},{4,22},{5,... | collective-permute-start | bytes 393224 | tf_op jit(solution)/shard_map/ppermute | solution.py:457
  58.7 0.5 collective-permute-start.27
  59.2 2.1 %columns.4 = (bf16[256,1024]{1,0:T(8,128)(2,1)}, bf16[256,256]{1,0:T(8,128)(2,1)}) custom-call(bf16[4,32,512]{2,1,0:T(8,128)(2,1)} %pick.1.refs_0_, bf16[4,32,512]{2,1,0:T(8,128)(2,1)} %collective-permute-done.28.refs_1_, bf16[4,32,512]{2,1,0:T(8,128)(2,1)} %collective-permute-done.29.refs_2_, bf16[4,32,512]{2,1,0:T(8,128)(2,1)} %collective-permute-done.30.refs_3_), custom_call_target="tpu_custom_call" | custom-call | tf_op jit(solution)/shard_map/columns/pallas_call | solution.py:432
  61.3 5.3 %collective-permute-done.26.refs_6_ = bf16[2,4,32,256]{3,2,1,0:T(8,128)(2,1)} collective-permute-done((bf16[2,4,32,256]{3,2,1,0:T(8,128)(2,1)}, bf16[2,4,32,256]{3,2,1,0:T(8,128)(2,1)}, u32[]{:S(2)}, u32[]{:S(2)}) %collective-permute-start.26) | collective-permute-done | bytes 131104 | tf_op jit(solution)/shard_map/ppermute | solution.py:457
  66.6 1.2 %collective-permute-done.27.refs_7_ = bf16[2,4,32,256]{3,2,1,0:T(8,128)(2,1)} collective-permute-done((bf16[2,4,32,256]{3,2,1,0:T(8,128)(2,1)}, bf16[2,4,32,256]{3,2,1,0:T(8,128)(2,1)}, u32[]{:S(2)}, u32[]{:S(2)}) %collective-permute-start.27) | collective-permute-done | bytes 131104 | tf_op jit(solution)/shard_map/ppermute | solution.py:457
  67.7 2.7 %first.1 = (bf16[256,256]{1,0:T(8,128)(2,1)}, bf16[256,256]{1,0:T(8,128)(2,1)}) custom-call(bf16[256,1024]{1,0:T(8,128)(2,1)} %get-tuple-element.33.all_columns, bf16[256,256]{1,0:T(8,128)(2,1)} %get-tuple-element.34.own, bf16[2,4,32,256]{3,2,1,0:T(8,128)(2,1)} %get-tuple-element.25.refs_0_, bf16[2,4,32,256]{3,2,1,0:T(8,128)(2,1)} %collective-permute-done.21.refs_1_, ...), custom_call_target="tpu_custom_call" | custom-call | tf_op jit(solution)/shard_map/first/pallas_call | solution.py:460
  70.4 2.1 %collective-permute-start.31 = (bf16[256,256]{1,0:T(8,128)(2,1)}, bf16[256,256]{1,0:T(8,128)(2,1)}, u32[]{:S(2)}, u32[]{:S(2)}) collective-permute-start(bf16[256,256]{1,0:T(8,128)(2,1)} %get-tuple-element.35.refs_8_), channel_id=1, source_target_pairs={{0,12},{4,0},{8,4},{12,8},{1,13},{5,1},{9,5},{13,9},{2,14},{6,2},{... | collective-permute-start | bytes 393224 | tf_op jit(solution)/shard_map/ppermute | solution.py:38
  72.6 0.1 collective-permute-start.32
  72.6 2.0 %collective-permute-start.33 = (bf16[256,256]{1,0:T(8,128)(2,1)}, bf16[256,256]{1,0:T(8,128)(2,1)}, u32[]{:S(2)}, u32[]{:S(2)}) collective-permute-start(bf16[256,256]{1,0:T(8,128)(2,1)} %get-tuple-element.35.refs_8_), channel_id=1, source_target_pairs={{0,4},{4,8},{8,12},{12,0},{1,5},{5,9},{9,13},{13,1},{2,6},{6,10},{... | collective-permute-start | bytes 393224 | tf_op jit(solution)/shard_map/ppermute | solution.py:38
  74.6 0.0 collective-permute-start.34
  74.6 2.6 %collective-permute-done.31.refs_10_ = bf16[256,256]{1,0:T(8,128)(2,1)} collective-permute-done((bf16[256,256]{1,0:T(8,128)(2,1)}, bf16[256,256]{1,0:T(8,128)(2,1)}, u32[]{:S(2)}, u32[]{:S(2)}) %collective-permute-start.31) | collective-permute-done | bytes 131104 | tf_op jit(solution)/shard_map/ppermute | solution.py:38
  77.2 4.0 %collective-permute-start.35 = (bf16[256,256]{1,0:T(8,128)(2,1)}, bf16[256,256]{1,0:T(8,128)(2,1)}, u32[]{:S(2)}, u32[]{:S(2)}) collective-permute-start(bf16[256,256]{1,0:T(8,128)(2,1)} %collective-permute-done.31.refs_10_), channel_id=1, source_target_pairs={{0,12},{4,0},{8,4},{12,8},{1,13},{5,1},{9,5},{13,9},{2,14},{6,2},{... | collective-permute-start | bytes 393224 | tf_op jit(solution)/shard_map/ppermute | solution.py:38
  81.2 2.8 %collective-permute-start.36 = (bf16[256,256]{1,0:T(8,128)(2,1)}, bf16[256,256]{1,0:T(8,128)(2,1)}, u32[]{:S(2)}, u32[]{:S(2)}) collective-permute-start(bf16[256,256]{1,0:T(8,128)(2,1)} %collective-permute-done.32.refs_11_), channel_id=1, source_target_pairs={{0,12},{4,0},{8,4},{12,8},{1,13},{5,1},{9,5},{13,9},{2,14},{6,2},{... | collective-permute-start | bytes 393224 | tf_op jit(solution)/shard_map/ppermute | solution.py:38
  83.9 1.8 %collective-permute-done.34.refs_13_ = bf16[256,256]{1,0:T(8,128)(2,1)} collective-permute-done((bf16[256,256]{1,0:T(8,128)(2,1)}, bf16[256,256]{1,0:T(8,128)(2,1)}, u32[]{:S(2)}, u32[]{:S(2)}) %collective-permute-start.34) | collective-permute-done | bytes 131104 | tf_op jit(solution)/shard_map/ppermute | solution.py:38
  85.7 2.6 %near.1.refs_8_ = f32[2,256,256]{2,1,0:T(8,128)} custom-call(bf16[2,4,32,256]{3,2,1,0:T(8,128)(2,1)} %get-tuple-element.25.refs_0_, bf16[2,4,32,256]{3,2,1,0:T(8,128)(2,1)} %collective-permute-done.21.refs_1_, bf16[2,4,32,256]{3,2,1,0:T(8,128)(2,1)} %collective-permute-done.22.refs_2_, bf16[2,4,32,256]{3,2,1,0:T(8,128)(2,1)} %collective-permute-done.23.refs_3_, ...), custom_call_target="tpu_custom_call" | custom-call | tf_op jit(solution)/shard_map/near/pallas_call | solution.py:489
  88.4 0.2 collective-permute-done.35.refs_9_
  88.5 2.4 %collective-permute-done.36.refs_10_ = bf16[256,256]{1,0:T(8,128)(2,1)} collective-permute-done((bf16[256,256]{1,0:T(8,128)(2,1)}, bf16[256,256]{1,0:T(8,128)(2,1)}, u32[]{:S(2)}, u32[]{:S(2)}) %collective-permute-start.36) | collective-permute-done | bytes 131104 | tf_op jit(solution)/shard_map/ppermute | solution.py:38
  90.9 2.1 %shard_map.65 = (bf16[2,64,256]{2,1,0:T(8,128)(2,1)}, bf16[2,64,256]{2,1,0:T(8,128)(2,1)}) custom-call(bf16[2,4,32,256]{3,2,1,0:T(8,128)(2,1)} %get-tuple-element.25.refs_0_, bf16[2,4,32,256]{3,2,1,0:T(8,128)(2,1)} %collective-permute-done.21.refs_1_, bf16[2,4,32,256]{3,2,1,0:T(8,128)(2,1)} %collective-permute-done.22.refs_2_, ...), custom_call_target="tpu_custom_call" | custom-call | tf_op jit(solution)/shard_map/pallas_call | solution.py:508
  93.0 1.1 %collective-permute-start.37 = (bf16[2,64,256]{2,1,0:T(8,128)(2,1)}, bf16[2,64,256]{2,1,0:T(8,128)(2,1)}, u32[]{:S(2)}, u32[]{:S(2)}) collective-permute-start(bf16[2,64,256]{2,1,0:T(8,128)(2,1)} %get-tuple-element.38), channel_id=1, source_target_pairs={{0,2},{1,3},{2,0},{3,1},{4,6},{5,7},{6,4},{7,5},{8,10},{9,11},{10,... | collective-permute-start | bytes 196616 | tf_op jit(solution)/shard_map/ppermute | solution.py:33
  94.2 2.1 %shard_map.64 = (bf16[2,64,256]{2,1,0:T(8,128)(2,1)}, bf16[2,64,256]{2,1,0:T(8,128)(2,1)}) custom-call(bf16[2,4,32,256]{3,2,1,0:T(8,128)(2,1)} %get-tuple-element.25.refs_0_, bf16[2,4,32,256]{3,2,1,0:T(8,128)(2,1)} %collective-permute-done.21.refs_1_, bf16[2,4,32,256]{3,2,1,0:T(8,128)(2,1)} %collective-permute-done.22.refs_2_, ...), custom_call_target="tpu_custom_call" | custom-call | tf_op jit(solution)/shard_map/pallas_call | solution.py:508
  96.3 1.1 %collective-permute-start.39 = (bf16[2,64,256]{2,1,0:T(8,128)(2,1)}, bf16[2,64,256]{2,1,0:T(8,128)(2,1)}, u32[]{:S(2)}, u32[]{:S(2)}) collective-permute-start(bf16[2,64,256]{2,1,0:T(8,128)(2,1)} %get-tuple-element.40), channel_id=1, source_target_pairs={{0,1},{1,0},{2,3},{3,2},{4,5},{5,4},{6,7},{7,6},{8,9},{9,8},{10,11... | collective-permute-start | bytes 196616 | tf_op jit(solution)/shard_map/ppermute | solution.py:33
  97.4 0.4 collective-permute-done.37.refs_1_
  97.9 1.0 %collective-permute-done.38.refs_2_ = bf16[2,64,256]{2,1,0:T(8,128)(2,1)} collective-permute-done((bf16[2,64,256]{2,1,0:T(8,128)(2,1)}, bf16[2,64,256]{2,1,0:T(8,128)(2,1)}, u32[]{:S(2)}, u32[]{:S(2)}) %collective-permute-start.38) | collective-permute-done | bytes 65568 | tf_op jit(solution)/shard_map/ppermute | solution.py:33
  98.9 1.8 %final.1 = f32[64,8,256]{2,1,0:T(8,128)} custom-call(bf16[64,256]{1,0:T(8,128)(2,1)} %columns.5, bf16[2,64,256]{2,1,0:T(8,128)(2,1)} %get-tuple-element.37.refs_0_, bf16[2,64,256]{2,1,0:T(8,128)(2,1)} %collective-permute-done.37.refs_1_, bf16[2,64,256]{2,1,0:T(8,128)(2,1)} %collective-permute-done.38.refs_2_, bf16[2,64,256]{2,1,0:T(8,128)(2,1)} %collective-permute-done.39.refs_3_), custom_call_target="tpu_custom_call" | custom-call | tf_op jit(solution)/shard_map/final/pallas_call | solution.py:529
  (37 shorter events, 0.1 us)
Async XLA Ops:
  0.0 6.8 %collective-permute-start.6 = (bf16[64,1024]{1,0:T(8,128)(2,1)}, bf16[64,1024]{1,0:T(8,128)(2,1)}, u32[]{:S(2)}, u32[]{:S(2)}) collective-permute-start(bf16[64,1024]{1,0:T(8,128)(2,1)} %refs_0_.1), channel_id=1, source_target_pairs={{0,16},{16,0},{1,17},{17,1},{2,18},{18,2},{3,19},{19,3},{4,20},{20... | collective-permute-start | bytes 393224 | tf_op jit(solution)/shard_map/ppermute | solution.py:33
  3.0 7.7 %collective-permute-start.1 = (bf16[64,1024]{1,0:T(8,128)(2,1)}, bf16[64,1024]{1,0:T(8,128)(2,1)}, u32[]{:S(2)}, u32[]{:S(2)}) collective-permute-start(bf16[64,1024]{1,0:T(8,128)(2,1)} %refs_0_.1), channel_id=1, source_target_pairs={{0,1},{1,0},{2,3},{3,2},{4,5},{5,4},{6,7},{7,6},{8,9},{9,8},{10,11... | collective-permute-start | bytes 393224 | tf_op jit(solution)/shard_map/ppermute | solution.py:33
  3.0 9.9 %collective-permute-start = (bf16[64,1024]{1,0:T(8,128)(2,1)}, bf16[64,1024]{1,0:T(8,128)(2,1)}, u32[]{:S(2)}, u32[]{:S(2)}) collective-permute-start(bf16[64,1024]{1,0:T(8,128)(2,1)} %refs_0_.1), channel_id=1, source_target_pairs={{0,2},{1,3},{2,0},{3,1},{4,6},{5,7},{6,4},{7,5},{8,10},{9,11},{10,... | collective-permute-start | bytes 393224 | tf_op jit(solution)/shard_map/ppermute | solution.py:33
  4.5 12.0 %collective-permute-start.10 = (bf16[64,1024]{1,0:T(8,128)(2,1)}, bf16[64,1024]{1,0:T(8,128)(2,1)}, u32[]{:S(2)}, u32[]{:S(2)}) collective-permute-start(bf16[64,1024]{1,0:T(8,128)(2,1)} %refs_4_.1), channel_id=1, source_target_pairs={{0,16},{16,0},{1,17},{17,1},{2,18},{18,2},{3,19},{19,3},{4,20},{20... | collective-permute-start | bytes 393224 | tf_op jit(solution)/shard_map/ppermute | solution.py:33
  5.0 11.5 %collective-permute-start.4 = (bf16[64,1024]{1,0:T(8,128)(2,1)}, bf16[64,1024]{1,0:T(8,128)(2,1)}, u32[]{:S(2)}, u32[]{:S(2)}) collective-permute-start(bf16[64,1024]{1,0:T(8,128)(2,1)} %refs_4_.1), channel_id=1, source_target_pairs={{0,1},{1,0},{2,3},{3,2},{4,5},{5,4},{6,7},{7,6},{8,9},{9,8},{10,11... | collective-permute-start | bytes 393224 | tf_op jit(solution)/shard_map/ppermute | solution.py:33
  6.8 9.8 %collective-permute-start.3 = (bf16[64,1024]{1,0:T(8,128)(2,1)}, bf16[64,1024]{1,0:T(8,128)(2,1)}, u32[]{:S(2)}, u32[]{:S(2)}) collective-permute-start(bf16[64,1024]{1,0:T(8,128)(2,1)} %refs_4_.1), channel_id=1, source_target_pairs={{0,2},{1,3},{2,0},{3,1},{4,6},{5,7},{6,4},{7,5},{8,10},{9,11},{10,... | collective-permute-start | bytes 393224 | tf_op jit(solution)/shard_map/ppermute | solution.py:33
  10.6 6.1 %collective-permute-start.14 = (bf16[32,2048]{1,0:T(8,128)(2,1)}, bf16[32,2048]{1,0:T(8,128)(2,1)}, u32[]{:S(2)}, u32[]{:S(2)}) collective-permute-start(bf16[32,2048]{1,0:T(8,128)(2,1)} %bitcast.5), channel_id=1, source_target_pairs={{0,16},{16,0},{1,17},{17,1},{2,18},{18,2},{3,19},{19,3},{4,20},{20... | collective-permute-start | bytes 393224 | tf_op jit(solution)/shard_map/ppermute | solution.py:33
  12.9 6.8 %collective-permute-start.15 = (bf16[32,2560]{1,0:T(8,128)(2,1)}, bf16[32,2560]{1,0:T(8,128)(2,1)S(1)}, u32[]{:S(2)}, u32[]{:S(2)}) collective-permute-start(bf16[32,2560]{1,0:T(8,128)(2,1)} %get-tuple-element.23.refs_16_.refs_0_), channel_id=1, source_target_pairs={{0,12},{4,0},{8,4},{12,8},{1,13},{5,1},{9,5},{13,9},{2,14},{6,2},{... | collective-permute-start | bytes 491528 | tf_op jit(solution)/shard_map/ppermute | solution.py:38
  16.5 8.6 %collective-permute-start.19 = (bf16[32,2560]{1,0:T(8,128)(2,1)}, bf16[32,2560]{1,0:T(8,128)(2,1)S(1)}, u32[]{:S(2)}, u32[]{:S(2)}) collective-permute-start(bf16[32,2560]{1,0:T(8,128)(2,1)} %get-tuple-element.23.refs_16_.refs_0_), channel_id=1, source_target_pairs={{0,4},{4,8},{8,12},{12,0},{1,5},{5,9},{9,13},{13,1},{2,6},{6,10},{... | collective-permute-start | bytes 491528 | tf_op jit(solution)/shard_map/ppermute | solution.py:38
  16.5 8.6 %collective-permute-start.8 = (bf16[64,1024]{1,0:T(8,128)(2,1)}, bf16[64,1024]{1,0:T(8,128)(2,1)S(1)}, u32[]{:S(2)}, u32[]{:S(2)}) collective-permute-start(bf16[64,1024]{1,0:T(8,128)(2,1)} %collective-permute-done.6.refs_8_), channel_id=1, source_target_pairs={{0,1},{1,0},{2,3},{3,2},{4,5},{5,4},{6,7},{7,6},{8,9},{9,8},{10,11... | collective-permute-start | bytes 393224 | tf_op jit(solution)/shard_map/ppermute | solution.py:33
  16.6 8.6 %collective-permute-start.7 = (bf16[64,1024]{1,0:T(8,128)(2,1)}, bf16[64,1024]{1,0:T(8,128)(2,1)}, u32[]{:S(2)}, u32[]{:S(2)}) collective-permute-start(bf16[64,1024]{1,0:T(8,128)(2,1)} %collective-permute-done.6.refs_8_), channel_id=1, source_target_pairs={{0,2},{1,3},{2,0},{3,1},{4,6},{5,7},{6,4},{7,5},{8,10},{9,11},{10,... | collective-permute-start | bytes 393224 | tf_op jit(solution)/shard_map/ppermute | solution.py:33
  16.7 9.9 %collective-permute-start.2 = (bf16[64,1024]{1,0:T(8,128)(2,1)}, bf16[64,1024]{1,0:T(8,128)(2,1)S(1)}, u32[]{:S(2)}, u32[]{:S(2)}) collective-permute-start(bf16[64,1024]{1,0:T(8,128)(2,1)} %collective-permute-done.refs_1_), channel_id=1, source_target_pairs={{0,1},{1,0},{2,3},{3,2},{4,5},{5,4},{6,7},{7,6},{8,9},{9,8},{10,11... | collective-permute-start | bytes 393224 | tf_op jit(solution)/shard_map/ppermute | solution.py:33
  19.7 0.7 copy-start
  20.4 11.5 %collective-permute-start.17 = (bf16[32,2560]{1,0:T(8,128)(2,1)S(1)}, bf16[32,2560]{1,0:T(8,128)(2,1)S(1)}, u32[]{:S(2)}, u32[]{:S(2)}) collective-permute-start(bf16[32,2560]{1,0:T(8,128)(2,1)S(1)} %collective-permute-done.15.refs_18_.refs_1_), channel_id=1, source_target_pairs={{0,12},{4,0},{8,4},{12,8},{1,13},{5,1},{9,5},{13,9},{2,14},{6,2},{... | collective-permute-start | bytes 491528 | tf_op jit(solution)/shard_map/ppermute | solution.py:38
  25.2 6.8 %copy-start.1 = (bf16[32,2560]{1,0:T(8,128)(2,1)}, bf16[32,2560]{1,0:T(8,128)(2,1)S(1)}, u32[]{:S(2)}) copy-start(bf16[32,2560]{1,0:T(8,128)(2,1)S(1)} %collective-permute-done.19.refs_22_.refs_3_) | copy-start | bytes 491524
  25.2 1.6 %collective-permute-start.12 = (bf16[64,1024]{1,0:T(8,128)(2,1)}, bf16[64,1024]{1,0:T(8,128)(2,1)S(1)}, u32[]{:S(2)}, u32[]{:S(2)}) collective-permute-start(bf16[64,1024]{1,0:T(8,128)(2,1)} %collective-permute-done.10.refs_12_), channel_id=1, source_target_pairs={{0,1},{1,0},{2,3},{3,2},{4,5},{5,4},{6,7},{7,6},{8,9},{9,8},{10,11... | collective-permute-start | bytes 393224 | tf_op jit(solution)/shard_map/ppermute | solution.py:33
  25.2 6.7 %copy-start.3 = (bf16[64,1024]{1,0:T(8,128)(2,1)}, bf16[64,1024]{1,0:T(8,128)(2,1)S(1)}, u32[]{:S(2)}) copy-start(bf16[64,1024]{1,0:T(8,128)(2,1)S(1)} %collective-permute-done.8.refs_10_) | copy-start | bytes 393220
  25.2 6.2 %collective-permute-start.11 = (bf16[64,1024]{1,0:T(8,128)(2,1)}, bf16[64,1024]{1,0:T(8,128)(2,1)}, u32[]{:S(2)}, u32[]{:S(2)}) collective-permute-start(bf16[64,1024]{1,0:T(8,128)(2,1)} %collective-permute-done.10.refs_12_), channel_id=1, source_target_pairs={{0,2},{1,3},{2,0},{3,1},{4,6},{5,7},{6,4},{7,5},{8,10},{9,11},{10,... | collective-permute-start | bytes 393224 | tf_op jit(solution)/shard_map/ppermute | solution.py:33
  25.3 6.2 %collective-permute-start.16 = (bf16[32,2048]{1,0:T(8,128)(2,1)}, bf16[32,2048]{1,0:T(8,128)(2,1)}, u32[]{:S(2)}, u32[]{:S(2)}) collective-permute-start(bf16[32,2048]{1,0:T(8,128)(2,1)} %collective-permute-done.14.refs_17_), channel_id=1, source_target_pairs={{0,12},{4,0},{8,4},{12,8},{1,13},{5,1},{9,5},{13,9},{2,14},{6,2},{... | collective-permute-start | bytes 393224 | tf_op jit(solution)/shard_map/ppermute | solution.py:38
  26.6 5.3 %copy-start.4 = (bf16[64,1024]{1,0:T(8,128)(2,1)}, bf16[64,1024]{1,0:T(8,128)(2,1)S(1)}, u32[]{:S(2)}) copy-start(bf16[64,1024]{1,0:T(8,128)(2,1)S(1)} %collective-permute-done.2.refs_3_) | copy-start | bytes 393220
  26.6 11.2 %collective-permute-start.5 = (bf16[64,1024]{1,0:T(8,128)(2,1)}, bf16[64,1024]{1,0:T(8,128)(2,1)}, u32[]{:S(2)}, u32[]{:S(2)}) collective-permute-start(bf16[64,1024]{1,0:T(8,128)(2,1)} %collective-permute-done.3.refs_5_), channel_id=1, source_target_pairs={{0,1},{1,0},{2,3},{3,2},{4,5},{5,4},{6,7},{7,6},{8,9},{9,8},{10,11... | collective-permute-start | bytes 393224 | tf_op jit(solution)/shard_map/ppermute | solution.py:33
  26.7 5.2 %copy-start.5 = (bf16[64,1024]{1,0:T(8,128)(2,1)}, bf16[64,1024]{1,0:T(8,128)(2,1)S(1)}, u32[]{:S(2)}) copy-start(bf16[64,1024]{1,0:T(8,128)(2,1)S(1)} %collective-permute-done.12.refs_14_) | copy-start | bytes 393220
  26.7 11.5 %collective-permute-start.20 = (bf16[32,2048]{1,0:T(8,128)(2,1)}, bf16[32,2048]{1,0:T(8,128)(2,1)}, u32[]{:S(2)}, u32[]{:S(2)}) collective-permute-start(bf16[32,2048]{1,0:T(8,128)(2,1)} %collective-permute-done.14.refs_17_), channel_id=1, source_target_pairs={{0,4},{4,8},{8,12},{12,0},{1,5},{5,9},{9,13},{13,1},{2,6},{6,10},{... | collective-permute-start | bytes 393224 | tf_op jit(solution)/shard_map/ppermute | solution.py:38
  31.4 7.0 %collective-permute-start.9 = (bf16[64,1024]{1,0:T(8,128)(2,1)}, bf16[64,1024]{1,0:T(8,128)(2,1)}, u32[]{:S(2)}, u32[]{:S(2)}) collective-permute-start(bf16[64,1024]{1,0:T(8,128)(2,1)} %collective-permute-done.7.refs_9_), channel_id=1, source_target_pairs={{0,1},{1,0},{2,3},{3,2},{4,5},{5,4},{6,7},{7,6},{8,9},{9,8},{10,11... | collective-permute-start | bytes 393224 | tf_op jit(solution)/shard_map/ppermute | solution.py:33
  31.5 7.0 %collective-permute-start.13 = (bf16[64,1024]{1,0:T(8,128)(2,1)}, bf16[64,1024]{1,0:T(8,128)(2,1)}, u32[]{:S(2)}, u32[]{:S(2)}) collective-permute-start(bf16[64,1024]{1,0:T(8,128)(2,1)} %collective-permute-done.11.refs_13_), channel_id=1, source_target_pairs={{0,1},{1,0},{2,3},{3,2},{4,5},{5,4},{6,7},{7,6},{8,9},{9,8},{10,11... | collective-permute-start | bytes 393224 | tf_op jit(solution)/shard_map/ppermute | solution.py:33
  31.9 0.7 copy-start.2
  32.6 7.5 %collective-permute-start.18 = (bf16[32,2048]{1,0:T(8,128)(2,1)}, bf16[32,2048]{1,0:T(8,128)(2,1)}, u32[]{:S(2)}, u32[]{:S(2)}) collective-permute-start(bf16[32,2048]{1,0:T(8,128)(2,1)} %collective-permute-done.16.refs_19_), channel_id=1, source_target_pairs={{0,12},{4,0},{8,4},{12,8},{1,13},{5,1},{9,5},{13,9},{2,14},{6,2},{... | collective-permute-start | bytes 393224 | tf_op jit(solution)/shard_map/ppermute | solution.py:38
  37.8 14.9 %collective-permute-start.28 = (bf16[4,32,512]{2,1,0:T(8,128)(2,1)}, bf16[4,32,512]{2,1,0:T(8,128)(2,1)}, u32[]{:S(2)}, u32[]{:S(2)}) collective-permute-start(bf16[4,32,512]{2,1,0:T(8,128)(2,1)} %pick.1.refs_0_), channel_id=1, source_target_pairs={{0,2},{1,3},{2,0},{3,1},{4,6},{5,7},{6,4},{7,5},{8,10},{9,11},{10,... | collective-permute-start | bytes 393224 | tf_op jit(solution)/shard_map/ppermute | solution.py:33
  38.2 14.7 %collective-permute-start.29 = (bf16[4,32,512]{2,1,0:T(8,128)(2,1)}, bf16[4,32,512]{2,1,0:T(8,128)(2,1)}, u32[]{:S(2)}, u32[]{:S(2)}) collective-permute-start(bf16[4,32,512]{2,1,0:T(8,128)(2,1)} %pick.1.refs_0_), channel_id=1, source_target_pairs={{0,1},{1,0},{2,3},{3,2},{4,5},{5,4},{6,7},{7,6},{8,9},{9,8},{10,11... | collective-permute-start | bytes 393224 | tf_op jit(solution)/shard_map/ppermute | solution.py:33
  49.7 3.1 %collective-permute-start.21 = (bf16[2,4,32,256]{3,2,1,0:T(8,128)(2,1)}, bf16[2,4,32,256]{3,2,1,0:T(8,128)(2,1)}, u32[]{:S(2)}, u32[]{:S(2)}) collective-permute-start(bf16[2,4,32,256]{3,2,1,0:T(8,128)(2,1)} %get-tuple-element.26), channel_id=1, source_target_pairs={{0,1},{1,0},{2,3},{3,2},{16,17},{17,16},{18,19},{19,18},{4,5},{5,4... | collective-permute-start | bytes 393224 | tf_op jit(solution)/shard_map/ppermute | solution.py:457
  49.8 7.5 %collective-permute-start.22 = (bf16[2,4,32,256]{3,2,1,0:T(8,128)(2,1)}, bf16[2,4,32,256]{3,2,1,0:T(8,128)(2,1)}, u32[]{:S(2)}, u32[]{:S(2)}) collective-permute-start(bf16[2,4,32,256]{3,2,1,0:T(8,128)(2,1)} %get-tuple-element.27), channel_id=1, source_target_pairs={{0,2},{1,3},{2,0},{3,1},{16,18},{17,19},{18,16},{19,17},{4,6},{5,7... | collective-permute-start | bytes 393224 | tf_op jit(solution)/shard_map/ppermute | solution.py:457
  52.7 6.0 %collective-permute-start.30 = (bf16[4,32,512]{2,1,0:T(8,128)(2,1)}, bf16[4,32,512]{2,1,0:T(8,128)(2,1)}, u32[]{:S(2)}, u32[]{:S(2)}) collective-permute-start(bf16[4,32,512]{2,1,0:T(8,128)(2,1)} %collective-permute-done.28.refs_1_), channel_id=1, source_target_pairs={{0,1},{1,0},{2,3},{3,2},{4,5},{5,4},{6,7},{7,6},{8,9},{9,8},{10,11... | collective-permute-start | bytes 393224 | tf_op jit(solution)/shard_map/ppermute | solution.py:33
  52.8 8.4 %collective-permute-start.23 = (bf16[2,4,32,256]{3,2,1,0:T(8,128)(2,1)}, bf16[2,4,32,256]{3,2,1,0:T(8,128)(2,1)}, u32[]{:S(2)}, u32[]{:S(2)}) collective-permute-start(bf16[2,4,32,256]{3,2,1,0:T(8,128)(2,1)} %get-tuple-element.28), channel_id=1, source_target_pairs={{0,3},{1,2},{2,1},{3,0},{16,19},{17,18},{18,17},{19,16},{4,7},{5,6... | collective-permute-start | bytes 393224 | tf_op jit(solution)/shard_map/ppermute | solution.py:457
  52.9 8.4 %collective-permute-start.24 = (bf16[2,4,32,256]{3,2,1,0:T(8,128)(2,1)}, bf16[2,4,32,256]{3,2,1,0:T(8,128)(2,1)}, u32[]{:S(2)}, u32[]{:S(2)}) collective-permute-start(bf16[2,4,32,256]{3,2,1,0:T(8,128)(2,1)} %get-tuple-element.29), channel_id=1, source_target_pairs={{0,16},{1,17},{2,18},{3,19},{16,0},{17,1},{18,2},{19,3},{4,20},{5,... | collective-permute-start | bytes 393224 | tf_op jit(solution)/shard_map/ppermute | solution.py:457
  52.9 8.4 %collective-permute-start.25 = (bf16[2,4,32,256]{3,2,1,0:T(8,128)(2,1)}, bf16[2,4,32,256]{3,2,1,0:T(8,128)(2,1)}, u32[]{:S(2)}, u32[]{:S(2)}) collective-permute-start(bf16[2,4,32,256]{3,2,1,0:T(8,128)(2,1)} %get-tuple-element.30), channel_id=1, source_target_pairs={{0,17},{1,16},{2,19},{3,18},{16,1},{17,0},{18,3},{19,2},{4,21},{5,... | collective-permute-start | bytes 393224 | tf_op jit(solution)/shard_map/ppermute | solution.py:457
  57.3 9.2 %collective-permute-start.26 = (bf16[2,4,32,256]{3,2,1,0:T(8,128)(2,1)}, bf16[2,4,32,256]{3,2,1,0:T(8,128)(2,1)}, u32[]{:S(2)}, u32[]{:S(2)}) collective-permute-start(bf16[2,4,32,256]{3,2,1,0:T(8,128)(2,1)} %get-tuple-element.31), channel_id=1, source_target_pairs={{0,18},{1,19},{2,16},{3,17},{16,2},{17,3},{18,0},{19,1},{4,22},{5,... | collective-permute-start | bytes 393224 | tf_op jit(solution)/shard_map/ppermute | solution.py:457
  58.7 9.1 %collective-permute-start.27 = (bf16[2,4,32,256]{3,2,1,0:T(8,128)(2,1)}, bf16[2,4,32,256]{3,2,1,0:T(8,128)(2,1)}, u32[]{:S(2)}, u32[]{:S(2)}) collective-permute-start(bf16[2,4,32,256]{3,2,1,0:T(8,128)(2,1)} %get-tuple-element.32), channel_id=1, source_target_pairs={{0,19},{1,18},{2,17},{3,16},{16,3},{17,2},{18,1},{19,0},{4,23},{5,... | collective-permute-start | bytes 393224 | tf_op jit(solution)/shard_map/ppermute | solution.py:457
  70.4 6.7 %collective-permute-start.31 = (bf16[256,256]{1,0:T(8,128)(2,1)}, bf16[256,256]{1,0:T(8,128)(2,1)}, u32[]{:S(2)}, u32[]{:S(2)}) collective-permute-start(bf16[256,256]{1,0:T(8,128)(2,1)} %get-tuple-element.35.refs_8_), channel_id=1, source_target_pairs={{0,12},{4,0},{8,4},{12,8},{1,13},{5,1},{9,5},{13,9},{2,14},{6,2},{... | collective-permute-start | bytes 393224 | tf_op jit(solution)/shard_map/ppermute | solution.py:38
  72.6 8.6 %collective-permute-start.32 = (bf16[256,256]{1,0:T(8,128)(2,1)}, bf16[256,256]{1,0:T(8,128)(2,1)}, u32[]{:S(2)}, u32[]{:S(2)}) collective-permute-start(bf16[256,256]{1,0:T(8,128)(2,1)} %get-tuple-element.36.refs_9_), channel_id=1, source_target_pairs={{0,12},{4,0},{8,4},{12,8},{1,13},{5,1},{9,5},{13,9},{2,14},{6,2},{... | collective-permute-start | bytes 393224 | tf_op jit(solution)/shard_map/ppermute | solution.py:38
  72.6 11.3 %collective-permute-start.33 = (bf16[256,256]{1,0:T(8,128)(2,1)}, bf16[256,256]{1,0:T(8,128)(2,1)}, u32[]{:S(2)}, u32[]{:S(2)}) collective-permute-start(bf16[256,256]{1,0:T(8,128)(2,1)} %get-tuple-element.35.refs_8_), channel_id=1, source_target_pairs={{0,4},{4,8},{8,12},{12,0},{1,5},{5,9},{9,13},{13,1},{2,6},{6,10},{... | collective-permute-start | bytes 393224 | tf_op jit(solution)/shard_map/ppermute | solution.py:38
  74.6 11.1 %collective-permute-start.34 = (bf16[256,256]{1,0:T(8,128)(2,1)}, bf16[256,256]{1,0:T(8,128)(2,1)}, u32[]{:S(2)}, u32[]{:S(2)}) collective-permute-start(bf16[256,256]{1,0:T(8,128)(2,1)} %get-tuple-element.36.refs_9_), channel_id=1, source_target_pairs={{0,4},{4,8},{8,12},{12,0},{1,5},{5,9},{9,13},{13,1},{2,6},{6,10},{... | collective-permute-start | bytes 393224 | tf_op jit(solution)/shard_map/ppermute | solution.py:38
  77.2 11.3 %collective-permute-start.35 = (bf16[256,256]{1,0:T(8,128)(2,1)}, bf16[256,256]{1,0:T(8,128)(2,1)}, u32[]{:S(2)}, u32[]{:S(2)}) collective-permute-start(bf16[256,256]{1,0:T(8,128)(2,1)} %collective-permute-done.31.refs_10_), channel_id=1, source_target_pairs={{0,12},{4,0},{8,4},{12,8},{1,13},{5,1},{9,5},{13,9},{2,14},{6,2},{... | collective-permute-start | bytes 393224 | tf_op jit(solution)/shard_map/ppermute | solution.py:38
  81.2 9.7 %collective-permute-start.36 = (bf16[256,256]{1,0:T(8,128)(2,1)}, bf16[256,256]{1,0:T(8,128)(2,1)}, u32[]{:S(2)}, u32[]{:S(2)}) collective-permute-start(bf16[256,256]{1,0:T(8,128)(2,1)} %collective-permute-done.32.refs_11_), channel_id=1, source_target_pairs={{0,12},{4,0},{8,4},{12,8},{1,13},{5,1},{9,5},{13,9},{2,14},{6,2},{... | collective-permute-start | bytes 393224 | tf_op jit(solution)/shard_map/ppermute | solution.py:38
  93.0 4.8 %collective-permute-start.37 = (bf16[2,64,256]{2,1,0:T(8,128)(2,1)}, bf16[2,64,256]{2,1,0:T(8,128)(2,1)}, u32[]{:S(2)}, u32[]{:S(2)}) collective-permute-start(bf16[2,64,256]{2,1,0:T(8,128)(2,1)} %get-tuple-element.38), channel_id=1, source_target_pairs={{0,2},{1,3},{2,0},{3,1},{4,6},{5,7},{6,4},{7,5},{8,10},{9,11},{10,... | collective-permute-start | bytes 196616 | tf_op jit(solution)/shard_map/ppermute | solution.py:33
  94.2 4.7 %collective-permute-start.38 = (bf16[2,64,256]{2,1,0:T(8,128)(2,1)}, bf16[2,64,256]{2,1,0:T(8,128)(2,1)}, u32[]{:S(2)}, u32[]{:S(2)}) collective-permute-start(bf16[2,64,256]{2,1,0:T(8,128)(2,1)} %get-tuple-element.39), channel_id=1, source_target_pairs={{0,3},{1,2},{2,1},{3,0},{4,7},{5,6},{6,5},{7,4},{8,11},{9,10},{10,... | collective-permute-start | bytes 196616 | tf_op jit(solution)/shard_map/ppermute | solution.py:33
  96.3 2.6 %collective-permute-start.39 = (bf16[2,64,256]{2,1,0:T(8,128)(2,1)}, bf16[2,64,256]{2,1,0:T(8,128)(2,1)}, u32[]{:S(2)}, u32[]{:S(2)}) collective-permute-start(bf16[2,64,256]{2,1,0:T(8,128)(2,1)} %get-tuple-element.40), channel_id=1, source_target_pairs={{0,1},{1,0},{2,3},{3,2},{4,5},{5,4},{6,7},{7,6},{8,9},{9,8},{10,11... | collective-permute-start | bytes 196616 | tf_op jit(solution)/shard_map/ppermute | solution.py:33

commit v5 on v4

--- a/solution.py
+++ b/solution.py
@@ -198,30 +198,17 @@
     return (tm ^ (r // col_count)) * col_count + (p ^ (r % col_count))
 
 
-def first_kernel(col_count, all_columns, own, *refs):
-    columns_v, own_v, tiles_v, middle_v, sems = refs[-5:]
-    (freqs, sources, places, part, rows) = tiles_v.shape
-    tiles, outs = refs[:sources], refs[sources : sources + freqs]
-    arriving = [copies_of([(all_columns, columns_v), (own, own_v)], sems.at[freqs])]
-    arriving += [
-        copies_of(
-            [
-                (ref.at[k], tiles_v.at[k, source_of(r, col_count)])
-                for r, ref in enumerate(tiles)
-            ],
-            sems.at[k],
-        )
-        for k in range(freqs)
-    ]
-    wait_for(arriving[0])
-    leaving = []
-    for k in range(freqs):
-        wait_for(arriving[1 + k])
-        weights = tiles_v[k].reshape(sources * places * part, rows)
-        first = jnp.dot(columns_v[...], weights, preferred_element_type=jnp.float32)
-        middle_v[k] = (own_v[...].astype(jnp.float32) + damping * first).astype(jnp.bfloat16)
-        leaving += copies_of([(middle_v.at[k], outs[k])], sems.at[freqs + 1])
-    wait_for(leaving)
+def first_kernel(dims, all_columns, own, *refs):
+    (col_count, k) = dims
+    out, columns_v, own_v, tiles_v, middle_v, sem = refs[-6:]
+    tiles = refs[:-6]
+    (sources, places, part, rows) = tiles_v.shape
+    pairs = [(ref.at[k], tiles_v.at[source_of(r, col_count)]) for r, ref in enumerate(tiles)]
+    wait_for(copies_of(pairs + [(all_columns, columns_v), (own, own_v)], sem))
+    weights = tiles_v[...].reshape(sources * places * part, rows)
+    first = jnp.dot(columns_v[...], weights, preferred_element_type=jnp.float32)
+    middle_v[...] = (own_v[...].astype(jnp.float32) + damping * first).astype(jnp.bfloat16)
+    wait_for(copies_of([(middle_v, out)], sem))
 
 
 def weights_of(tiles_v, k, index, dims):
@@ -457,22 +444,22 @@
         tiles[r] = lax.ppermute(sent[r], ("tm", "col"), pairs)
 
     first_shape = (own_freqs, columns_own, tile_rows)
-    middle = pl.pallas_call(
-        functools.partial(first_kernel, col_count),
-        out_shape=[jax.ShapeDtypeStruct(first_shape[1:], jnp.bfloat16)] * own_freqs,
-        in_specs=[HBM] * (2 + sources),
-        out_specs=[HBM] * own_freqs,
-        scratch_shapes=[
-            pltpu.VMEM((columns_own, sources * width), jnp.bfloat16),
-            pltpu.VMEM((columns_own, tile_rows), jnp.bfloat16),
-            pltpu.VMEM((own_freqs, sources, row_count, part, tile_rows), jnp.bfloat16),
-            pltpu.VMEM(first_shape, jnp.bfloat16),
-            pltpu.SemaphoreType.DMA((own_freqs + 2,)),
-        ],
-        compiler_params=FULL,
-        name="first",
-    )(all_columns, own_columns, *tiles)
-    middles = {(0, k): value for k, value in enumerate(middle)}
+    middles = {}
+    for k in range(own_freqs):
+        middles[(0, k)] = pl.pallas_call(
+            functools.partial(first_kernel, (col_count, k)),
+            out_shape=jax.ShapeDtypeStruct(first_shape[1:], jnp.bfloat16),
+            in_specs=[HBM] * (2 + sources),
+            out_specs=HBM,
+            scratch_shapes=[
+                pltpu.VMEM((columns_own, sources * width), jnp.bfloat16),
+                pltpu.VMEM((columns_own, tile_rows), jnp.bfloat16),
+                pltpu.VMEM((sources, row_count, part, tile_rows), jnp.bfloat16),
+                pltpu.VMEM(first_shape[1:], jnp.bfloat16),
+                pltpu.SemaphoreType.DMA,
+            ],
+            compiler_params=FULL,
+        )(all_columns, own_columns, *tiles)
 
     def middle_step(source, target, step):
         for k in range(own_freqs):

time: 101 us -> 103 us (1.020)
  starting transfers between devices: 44.7 us -> 42.2 us
  waiting for transfers between devices: 28.1 us -> 30.1 us
  Pallas kernels: 26.3 us -> 28.2 us
    ppermute x12, starting transfers between devices: 24.6 us -> 22.1 us  [shift(): lax.ppermute(value, axis, [(i, (i + step) % size) for i in range(size)])]
    pallas_call x1 -> x2, Pallas kernels: 2.69 us -> 4.6 us  [shards(): pl.pallas_call(functools.partial(first_kernel, (col_count, k)), out_shape...]
    ppermute x12, waiting for transfers between devices: 11.7 us -> 13.5 us  [shift(): lax.ppermute(value, axis, [(i, (i + step) % size) for i in range(size)])]
  transfers between devices with their start and end apart: 40 -> 40, of which waited for: 16 -> 15; matrix products, arithmetic and copies ran while one was open for 0% -> 0% of each run, Pallas kernels for 19% -> 22%
where the time goes in v5:
time: 103 us; the launch traced here: 102 us
  starting transfers between devices  42.2 us (41%)
  waiting for transfers between devices  30.1 us (29%)
  Pallas kernels  28.2 us (27%)
  local copies, waits for them, and re-layouts  1.33 us (1%)
    ppermute x12, starting transfers between devices, shift(): lax.ppermute(value, axis, [(i, (i + step) % size) for i in range(size)])  22.1 us
    ppermute x21, starting transfers between devices, swap(): return lax.ppermute(value, axis, [(i, i ^ bit) for i in range(size)])  13.6 us
    ppermute x12, waiting for transfers between devices, shift(): lax.ppermute(value, axis, [(i, (i + step) % size) for i in range(size)])  13.5 us
    pallas_call x1, Pallas kernels, shards(): pl.pallas_call(functools.partial(tile_kernel, row_keys, groups, (NT, NF,...  9.64 us
    ppermute x7, waiting for transfers between devices, shards(): tiles[r] = lax.ppermute(sent[r], ('tm', 'col'), pairs)  9.2 us
    ppermute x21, waiting for transfers between devices, swap(): return lax.ppermute(value, axis, [(i, i ^ bit) for i in range(size)])  7.44 us
    ppermute x7, starting transfers between devices, shards(): tiles[r] = lax.ppermute(sent[r], ('tm', 'col'), pairs)  6.5 us
    pallas_call x2, Pallas kernels, shards(): pl.pallas_call(functools.partial(first_kernel, (col_count, k)), out_shape...  4.6 us
  transfers between devices with their start and end apart: 40, of which 15 were waited for; matrix products, arithmetic and copies ran while one was open for 0% of the time, Pallas kernels for 22%

profile of v5, /device:TPU:0, one launch (start us, length us, event | category | flops | bytes accessed | tf_op | source)
XLA Modules:
  0.0 102.1 jit_solution(15300945455663696187)
XLA Ops:
  0.0 3.0 %collective-permute-start.6 = (bf16[64,1024]{1,0:T(8,128)(2,1)}, bf16[64,1024]{1,0:T(8,128)(2,1)}, u32[]{:S(2)}, u32[]{:S(2)}) collective-permute-start(bf16[64,1024]{1,0:T(8,128)(2,1)} %refs_0_.1), channel_id=1, source_target_pairs={{0,16},{16,0},{1,17},{17,1},{2,18},{18,2},{3,19},{19,3},{4,20},{20... | collective-permute-start | bytes 393224 | tf_op jit(solution)/shard_map/ppermute | solution.py:33
  3.0 1.5 %collective-permute-start = (bf16[64,1024]{1,0:T(8,128)(2,1)}, bf16[64,1024]{1,0:T(8,128)(2,1)}, u32[]{:S(2)}, u32[]{:S(2)}) collective-permute-start(bf16[64,1024]{1,0:T(8,128)(2,1)} %refs_0_.1), channel_id=1, source_target_pairs={{0,2},{1,3},{2,0},{3,1},{4,6},{5,7},{6,4},{7,5},{8,10},{9,11},{10,... | collective-permute-start | bytes 393224 | tf_op jit(solution)/shard_map/ppermute | solution.py:33
  4.5 0.5 collective-permute-start.10
  5.0 0.0 collective-permute-start.4
  5.0 1.7 %collective-permute-done.6.refs_8_ = bf16[64,1024]{1,0:T(8,128)(2,1)} collective-permute-done((bf16[64,1024]{1,0:T(8,128)(2,1)}, bf16[64,1024]{1,0:T(8,128)(2,1)}, u32[]{:S(2)}, u32[]{:S(2)}) %collective-permute-start.6) | collective-permute-done | bytes 131104 | tf_op jit(solution)/shard_map/ppermute | solution.py:33
  6.8 2.2 %collective-permute-start.3 = (bf16[64,1024]{1,0:T(8,128)(2,1)}, bf16[64,1024]{1,0:T(8,128)(2,1)}, u32[]{:S(2)}, u32[]{:S(2)}) collective-permute-start(bf16[64,1024]{1,0:T(8,128)(2,1)} %refs_4_.1), channel_id=1, source_target_pairs={{0,2},{1,3},{2,0},{3,1},{4,6},{5,7},{6,4},{7,5},{8,10},{9,11},{10,... | collective-permute-start | bytes 393224 | tf_op jit(solution)/shard_map/ppermute | solution.py:33
  9.0 1.6 %pack.1 = (bf16[32,2560]{1,0:T(8,128)(2,1)}, bf16[1,32,2048]{2,1,0:T(8,128)(2,1)}) custom-call(bf16[64,1024]{1,0:T(8,128)(2,1)} %refs_0_.1, bf16[64,1024]{1,0:T(8,128)(2,1)} %refs_4_.1, bf16[64,256]{1,0:T(8,128)(2,1)} %columns.5), custom_call_target="tpu_custom_call" | custom-call | tf_op jit(solution)/shard_map/pack/pallas_call | solution.py:318
  10.6 0.0 collective-permute-done.1.refs_2_
  10.6 2.3 %collective-permute-start.14 = (bf16[32,2048]{1,0:T(8,128)(2,1)}, bf16[32,2048]{1,0:T(8,128)(2,1)}, u32[]{:S(2)}, u32[]{:S(2)}) collective-permute-start(bf16[32,2048]{1,0:T(8,128)(2,1)} %bitcast.5), channel_id=1, source_target_pairs={{0,16},{16,0},{1,17},{17,1},{2,18},{18,2},{3,19},{19,3},{4,20},{20... | collective-permute-start | bytes 393224 | tf_op jit(solution)/shard_map/ppermute | solution.py:33
  12.9 0.0 collective-permute-done.refs_1_
  12.9 3.6 %collective-permute-start.15 = (bf16[32,2560]{1,0:T(8,128)(2,1)}, bf16[32,2560]{1,0:T(8,128)(2,1)S(1)}, u32[]{:S(2)}, u32[]{:S(2)}) collective-permute-start(bf16[32,2560]{1,0:T(8,128)(2,1)} %get-tuple-element.21.refs_16_.refs_0_), channel_id=1, source_target_pairs={{0,12},{4,0},{8,4},{12,8},{1,13},{5,1},{9,5},{13,9},{2,14},{6,2},{... | collective-permute-start | bytes 491528 | tf_op jit(solution)/shard_map/ppermute | solution.py:38
  16.5 0.1 collective-permute-start.8
  16.6 0.0 collective-permute-done.3.refs_5_
  16.6 0.1 collective-permute-start.7
  16.7 0.0 collective-permute-done.14.refs_17_
  16.7 0.5 collective-permute-start.2
  17.2 2.5 %collective-permute-done.15.refs_18_.refs_1_ = bf16[32,2560]{1,0:T(8,128)(2,1)S(1)} collective-permute-done((bf16[32,2560]{1,0:T(8,128)(2,1)}, bf16[32,2560]{1,0:T(8,128)(2,1)S(1)}, u32[]{:S(2)}, u32[]{:S(2)}) %collective-permute-start.15) | collective-permute-done | bytes 163872 | tf_op jit(solution)/shard_map/ppermute | solution.py:38
  19.7 0.7 copy-done
  20.4 4.2 %collective-permute-start.17 = (bf16[32,2560]{1,0:T(8,128)(2,1)S(1)}, bf16[32,2560]{1,0:T(8,128)(2,1)S(1)}, u32[]{:S(2)}, u32[]{:S(2)}) collective-permute-start(bf16[32,2560]{1,0:T(8,128)(2,1)S(1)} %collective-permute-done.15.refs_18_.refs_1_), channel_id=1, source_target_pairs={{0,12},{4,0},{8,4},{12,8},{1,13},{5,1},{9,5},{13,9},{2,14},{6,2},{... | collective-permute-start | bytes 491528 | tf_op jit(solution)/shard_map/ppermute | solution.py:38
  24.6 0.5 collective-permute-done.19.refs_22_.refs_3_
  25.1 0.0 collective-permute-start.12
  25.2 0.1 collective-permute-start.11
  25.3 1.3 %collective-permute-start.16 = (bf16[32,2048]{1,0:T(8,128)(2,1)}, bf16[32,2048]{1,0:T(8,128)(2,1)}, u32[]{:S(2)}, u32[]{:S(2)}) collective-permute-start(bf16[32,2048]{1,0:T(8,128)(2,1)} %collective-permute-done.14.refs_17_), channel_id=1, source_target_pairs={{0,12},{4,0},{8,4},{12,8},{1,13},{5,1},{9,5},{13,9},{2,14},{6,2},{... | collective-permute-start | bytes 393224 | tf_op jit(solution)/shard_map/ppermute | solution.py:38
  26.6 0.1 collective-permute-done.12.refs_14_
  26.7 0.8 collective-permute-start.20
  27.5 3.9 %collective-permute-done.11.refs_13_ = bf16[64,1024]{1,0:T(8,128)(2,1)} collective-permute-done((bf16[64,1024]{1,0:T(8,128)(2,1)}, bf16[64,1024]{1,0:T(8,128)(2,1)}, u32[]{:S(2)}, u32[]{:S(2)}) %collective-permute-start.11) | collective-permute-done | bytes 131104 | tf_op jit(solution)/shard_map/ppermute | solution.py:33
  31.4 0.1 collective-permute-done.16.refs_19_
  31.4 0.4 collective-permute-start.13
  31.9 0.7 copy-done.2
  32.6 3.8 %collective-permute-start.18 = (bf16[32,2048]{1,0:T(8,128)(2,1)}, bf16[32,2048]{1,0:T(8,128)(2,1)}, u32[]{:S(2)}, u32[]{:S(2)}) collective-permute-start(bf16[32,2048]{1,0:T(8,128)(2,1)} %collective-permute-done.16.refs_19_), channel_id=1, source_target_pairs={{0,12},{4,0},{8,4},{12,8},{1,13},{5,1},{9,5},{13,9},{2,14},{6,2},{... | collective-permute-start | bytes 393224 | tf_op jit(solution)/shard_map/ppermute | solution.py:38
  36.3 1.5 %pick.1.refs_0_ = bf16[4,32,512]{2,1,0:T(8,128)(2,1)} custom-call(bf16[32,2560]{1,0:T(8,128)(2,1)} %get-tuple-element.21.refs_16_.refs_0_, bf16[32,2560]{1,0:T(8,128)(2,1)} %copy-done, bf16[32,2560]{1,0:T(8,128)(2,1)} %copy-done.2, bf16[32,2560]{1,0:T(8,128)(2,1)} %copy-done.1), custom_call_target="tpu_custom_call" | custom-call | tf_op jit(solution)/shard_map/pick/pallas_call | solution.py:371
  37.8 0.4 collective-permute-start.28
  38.2 0.2 collective-permute-start.29
  38.4 1.6 %collective-permute-done.18.refs_21_ = bf16[32,2048]{1,0:T(8,128)(2,1)} collective-permute-done((bf16[32,2048]{1,0:T(8,128)(2,1)}, bf16[32,2048]{1,0:T(8,128)(2,1)}, u32[]{:S(2)}, u32[]{:S(2)}) %collective-permute-start.18) | collective-permute-done | bytes 131104 | tf_op jit(solution)/shard_map/ppermute | solution.py:38
  40.1 9.6 %tile.1 = (bf16[2,4,32,256]{3,2,1,0:T(8,128)(2,1)}, bf16[2,4,32,256]{3,2,1,0:T(8,128)(2,1)}, bf16[2,4,32,256]{3,2,1,0:T(8,128)(2,1)}, bf16[2,4,32,256]{3,2,1,0:T...) custom-call(bf16[256,256]{1,0:T(8,128)(2,1)} %constant.2.clone.mix, ...), custom_call_target="tpu_custom_call" | custom-call | tf_op jit(solution)/shard_map/tile/pallas_call | solution.py:392
  49.7 0.1 collective-permute-start.21
  49.8 2.8 %collective-permute-start.22 = (bf16[2,4,32,256]{3,2,1,0:T(8,128)(2,1)}, bf16[2,4,32,256]{3,2,1,0:T(8,128)(2,1)}, u32[]{:S(2)}, u32[]{:S(2)}) collective-permute-start(bf16[2,4,32,256]{3,2,1,0:T(8,128)(2,1)} %get-tuple-element.25), channel_id=1, source_target_pairs={{0,2},{1,3},{2,0},{3,1},{16,18},{17,19},{18,16},{19,17},{4,6},{5,7... | collective-permute-start | bytes 393224 | tf_op jit(solution)/shard_map/ppermute | solution.py:444
  52.7 0.2 collective-permute-start.30
  52.8 0.1 collective-permute-start.23
  52.9 1.7 %collective-permute-start.25 = (bf16[2,4,32,256]{3,2,1,0:T(8,128)(2,1)}, bf16[2,4,32,256]{3,2,1,0:T(8,128)(2,1)}, u32[]{:S(2)}, u32[]{:S(2)}) collective-permute-start(bf16[2,4,32,256]{3,2,1,0:T(8,128)(2,1)} %get-tuple-element.28), channel_id=1, source_target_pairs={{0,17},{1,16},{2,19},{3,18},{16,1},{17,0},{18,3},{19,2},{4,21},{5,... | collective-permute-start | bytes 393224 | tf_op jit(solution)/shard_map/ppermute | solution.py:444
  54.6 2.8 %collective-permute-done.22.refs_2_ = bf16[2,4,32,256]{3,2,1,0:T(8,128)(2,1)} collective-permute-done((bf16[2,4,32,256]{3,2,1,0:T(8,128)(2,1)}, bf16[2,4,32,256]{3,2,1,0:T(8,128)(2,1)}, u32[]{:S(2)}, u32[]{:S(2)}) %collective-permute-start.22) | collective-permute-done | bytes 131104 | tf_op jit(solution)/shard_map/ppermute | solution.py:444
  57.3 1.3 %collective-permute-start.26 = (bf16[2,4,32,256]{3,2,1,0:T(8,128)(2,1)}, bf16[2,4,32,256]{3,2,1,0:T(8,128)(2,1)}, u32[]{:S(2)}, u32[]{:S(2)}) collective-permute-start(bf16[2,4,32,256]{3,2,1,0:T(8,128)(2,1)} %get-tuple-element.29), channel_id=1, source_target_pairs={{0,18},{1,19},{2,16},{3,17},{16,2},{17,3},{18,0},{19,1},{4,22},{5,... | collective-permute-start | bytes 393224 | tf_op jit(solution)/shard_map/ppermute | solution.py:444
  58.7 0.5 collective-permute-start.27
  59.2 2.1 %columns.4 = (bf16[256,1024]{1,0:T(8,128)(2,1)}, bf16[256,256]{1,0:T(8,128)(2,1)}) custom-call(bf16[4,32,512]{2,1,0:T(8,128)(2,1)} %pick.1.refs_0_, bf16[4,32,512]{2,1,0:T(8,128)(2,1)} %collective-permute-done.28.refs_1_, bf16[4,32,512]{2,1,0:T(8,128)(2,1)} %collective-permute-done.29.refs_2_, bf16[4,32,512]{2,1,0:T(8,128)(2,1)} %collective-permute-done.30.refs_3_), custom_call_target="tpu_custom_call" | custom-call | tf_op jit(solution)/shard_map/columns/pallas_call | solution.py:419
  61.3 5.3 %collective-permute-done.26.refs_6_ = bf16[2,4,32,256]{3,2,1,0:T(8,128)(2,1)} collective-permute-done((bf16[2,4,32,256]{3,2,1,0:T(8,128)(2,1)}, bf16[2,4,32,256]{3,2,1,0:T(8,128)(2,1)}, u32[]{:S(2)}, u32[]{:S(2)}) %collective-permute-start.26) | collective-permute-done | bytes 131104 | tf_op jit(solution)/shard_map/ppermute | solution.py:444
  66.5 1.2 %collective-permute-done.27.refs_7_ = bf16[2,4,32,256]{3,2,1,0:T(8,128)(2,1)} collective-permute-done((bf16[2,4,32,256]{3,2,1,0:T(8,128)(2,1)}, bf16[2,4,32,256]{3,2,1,0:T(8,128)(2,1)}, u32[]{:S(2)}, u32[]{:S(2)}) %collective-permute-start.27) | collective-permute-done | bytes 131104 | tf_op jit(solution)/shard_map/ppermute | solution.py:444
  67.7 2.3 %shard_map.64.refs_8_ = bf16[256,256]{1,0:T(8,128)(2,1)} custom-call(bf16[256,1024]{1,0:T(8,128)(2,1)} %get-tuple-element.31.all_columns, bf16[256,256]{1,0:T(8,128)(2,1)} %get-tuple-element.32.own, bf16[2,4,32,256]{3,2,1,0:T(8,128)(2,1)} %get-tuple-element.23.refs_0_, bf16[2,4,32,256]{3,2,1,0:T(8,128)(2,1)} %collective-permute-done.21.refs_1_, ...), custom_call_target="tpu_custom_call" | custom-call | tf_op jit(solution)/shard_map/pallas_call | solution.py:449
  70.0 2.1 %collective-permute-start.31 = (bf16[256,256]{1,0:T(8,128)(2,1)}, bf16[256,256]{1,0:T(8,128)(2,1)}, u32[]{:S(2)}, u32[]{:S(2)}) collective-permute-start(bf16[256,256]{1,0:T(8,128)(2,1)} %shard_map.64.refs_8_), channel_id=1, source_target_pairs={{0,12},{4,0},{8,4},{12,8},{1,13},{5,1},{9,5},{13,9},{2,14},{6,2},{... | collective-permute-start | bytes 393224 | tf_op jit(solution)/shard_map/ppermute | solution.py:38
  72.1 2.3 %shard_map.65.refs_9_ = bf16[256,256]{1,0:T(8,128)(2,1)} custom-call(bf16[256,1024]{1,0:T(8,128)(2,1)} %get-tuple-element.31.all_columns, bf16[256,256]{1,0:T(8,128)(2,1)} %get-tuple-element.32.own, bf16[2,4,32,256]{3,2,1,0:T(8,128)(2,1)} %get-tuple-element.23.refs_0_, bf16[2,4,32,256]{3,2,1,0:T(8,128)(2,1)} %collective-permute-done.21.refs_1_, ...), custom_call_target="tpu_custom_call" | custom-call | tf_op jit(solution)/shard_map/pallas_call | solution.py:449
  74.5 0.1 collective-permute-start.32
  74.5 2.0 %collective-permute-start.33 = (bf16[256,256]{1,0:T(8,128)(2,1)}, bf16[256,256]{1,0:T(8,128)(2,1)}, u32[]{:S(2)}, u32[]{:S(2)}) collective-permute-start(bf16[256,256]{1,0:T(8,128)(2,1)} %shard_map.64.refs_8_), channel_id=1, source_target_pairs={{0,4},{4,8},{8,12},{12,0},{1,5},{5,9},{9,13},{13,1},{2,6},{6,10},{... | collective-permute-start | bytes 393224 | tf_op jit(solution)/shard_map/ppermute | solution.py:38
  76.5 0.0 collective-permute-start.34
  76.6 4.2 %collective-permute-start.35 = (bf16[256,256]{1,0:T(8,128)(2,1)}, bf16[256,256]{1,0:T(8,128)(2,1)}, u32[]{:S(2)}, u32[]{:S(2)}) collective-permute-start(bf16[256,256]{1,0:T(8,128)(2,1)} %collective-permute-done.31.refs_10_), channel_id=1, source_target_pairs={{0,12},{4,0},{8,4},{12,8},{1,13},{5,1},{9,5},{13,9},{2,14},{6,2},{... | collective-permute-start | bytes 393224 | tf_op jit(solution)/shard_map/ppermute | solution.py:38
  80.7 6.1 %collective-permute-done.32.refs_11_ = bf16[256,256]{1,0:T(8,128)(2,1)} collective-permute-done((bf16[256,256]{1,0:T(8,128)(2,1)}, bf16[256,256]{1,0:T(8,128)(2,1)}, u32[]{:S(2)}, u32[]{:S(2)}) %collective-permute-start.32) | collective-permute-done | bytes 131104 | tf_op jit(solution)/shard_map/ppermute | solution.py:38
  86.8 2.7 %near.1.refs_8_ = f32[2,256,256]{2,1,0:T(8,128)} custom-call(bf16[2,4,32,256]{3,2,1,0:T(8,128)(2,1)} %get-tuple-element.23.refs_0_, bf16[2,4,32,256]{3,2,1,0:T(8,128)(2,1)} %collective-permute-done.21.refs_1_, bf16[2,4,32,256]{3,2,1,0:T(8,128)(2,1)} %collective-permute-done.22.refs_2_, bf16[2,4,32,256]{3,2,1,0:T(8,128)(2,1)} %collective-permute-done.23.refs_3_, ...), custom_call_target="tpu_custom_call" | custom-call | tf_op jit(solution)/shard_map/near/pallas_call | solution.py:476
  89.5 0.1 collective-permute-done.35.refs_9_
  89.6 2.5 %collective-permute-done.36.refs_10_ = bf16[256,256]{1,0:T(8,128)(2,1)} collective-permute-done((bf16[256,256]{1,0:T(8,128)(2,1)}, bf16[256,256]{1,0:T(8,128)(2,1)}, u32[]{:S(2)}, u32[]{:S(2)}) %collective-permute-start.36) | collective-permute-done | bytes 131104 | tf_op jit(solution)/shard_map/ppermute | solution.py:38
  92.1 2.1 %shard_map.67 = (bf16[2,64,256]{2,1,0:T(8,128)(2,1)}, bf16[2,64,256]{2,1,0:T(8,128)(2,1)}) custom-call(bf16[2,4,32,256]{3,2,1,0:T(8,128)(2,1)} %get-tuple-element.23.refs_0_, bf16[2,4,32,256]{3,2,1,0:T(8,128)(2,1)} %collective-permute-done.21.refs_1_, bf16[2,4,32,256]{3,2,1,0:T(8,128)(2,1)} %collective-permute-done.22.refs_2_, ...), custom_call_target="tpu_custom_call" | custom-call | tf_op jit(solution)/shard_map/pallas_call | solution.py:495
  94.2 1.5 %collective-permute-start.37 = (bf16[2,64,256]{2,1,0:T(8,128)(2,1)}, bf16[2,64,256]{2,1,0:T(8,128)(2,1)}, u32[]{:S(2)}, u32[]{:S(2)}) collective-permute-start(bf16[2,64,256]{2,1,0:T(8,128)(2,1)} %get-tuple-element.34), channel_id=1, source_target_pairs={{0,2},{1,3},{2,0},{3,1},{4,6},{5,7},{6,4},{7,5},{8,10},{9,11},{10,... | collective-permute-start | bytes 196616 | tf_op jit(solution)/shard_map/ppermute | solution.py:33
  95.7 2.1 %shard_map.66 = (bf16[2,64,256]{2,1,0:T(8,128)(2,1)}, bf16[2,64,256]{2,1,0:T(8,128)(2,1)}) custom-call(bf16[2,4,32,256]{3,2,1,0:T(8,128)(2,1)} %get-tuple-element.23.refs_0_, bf16[2,4,32,256]{3,2,1,0:T(8,128)(2,1)} %collective-permute-done.21.refs_1_, bf16[2,4,32,256]{3,2,1,0:T(8,128)(2,1)} %collective-permute-done.22.refs_2_, ...), custom_call_target="tpu_custom_call" | custom-call | tf_op jit(solution)/shard_map/pallas_call | solution.py:495
  97.9 0.8 collective-permute-start.39
  98.7 0.2 collective-permute-done.37.refs_1_
  98.9 1.4 %collective-permute-done.38.refs_2_ = bf16[2,64,256]{2,1,0:T(8,128)(2,1)} collective-permute-done((bf16[2,64,256]{2,1,0:T(8,128)(2,1)}, bf16[2,64,256]{2,1,0:T(8,128)(2,1)}, u32[]{:S(2)}, u32[]{:S(2)}) %collective-permute-start.38) | collective-permute-done | bytes 65568 | tf_op jit(solution)/shard_map/ppermute | solution.py:33
  100.3 1.8 %final.1 = f32[64,8,256]{2,1,0:T(8,128)} custom-call(bf16[64,256]{1,0:T(8,128)(2,1)} %columns.5, bf16[2,64,256]{2,1,0:T(8,128)(2,1)} %get-tuple-element.33.refs_0_, bf16[2,64,256]{2,1,0:T(8,128)(2,1)} %collective-permute-done.37.refs_1_, bf16[2,64,256]{2,1,0:T(8,128)(2,1)} %collective-permute-done.38.refs_2_, bf16[2,64,256]{2,1,0:T(8,128)(2,1)} %collective-permute-done.39.refs_3_), custom_call_target="tpu_custom_call" | custom-call | tf_op jit(solution)/shard_map/final/pallas_call | solution.py:516
  (38 shorter events, 0.1 us)
Async XLA Ops:
  0.0 6.8 %collective-permute-start.6 = (bf16[64,1024]{1,0:T(8,128)(2,1)}, bf16[64,1024]{1,0:T(8,128)(2,1)}, u32[]{:S(2)}, u32[]{:S(2)}) collective-permute-start(bf16[64,1024]{1,0:T(8,128)(2,1)} %refs_0_.1), channel_id=1, source_target_pairs={{0,16},{16,0},{1,17},{17,1},{2,18},{18,2},{3,19},{19,3},{4,20},{20... | collective-permute-start | bytes 393224 | tf_op jit(solution)/shard_map/ppermute | solution.py:33
  3.0 7.6 %collective-permute-start.1 = (bf16[64,1024]{1,0:T(8,128)(2,1)}, bf16[64,1024]{1,0:T(8,128)(2,1)}, u32[]{:S(2)}, u32[]{:S(2)}) collective-permute-start(bf16[64,1024]{1,0:T(8,128)(2,1)} %refs_0_.1), channel_id=1, source_target_pairs={{0,1},{1,0},{2,3},{3,2},{4,5},{5,4},{6,7},{7,6},{8,9},{9,8},{10,11... | collective-permute-start | bytes 393224 | tf_op jit(solution)/shard_map/ppermute | solution.py:33
  3.0 9.9 %collective-permute-start = (bf16[64,1024]{1,0:T(8,128)(2,1)}, bf16[64,1024]{1,0:T(8,128)(2,1)}, u32[]{:S(2)}, u32[]{:S(2)}) collective-permute-start(bf16[64,1024]{1,0:T(8,128)(2,1)} %refs_0_.1), channel_id=1, source_target_pairs={{0,2},{1,3},{2,0},{3,1},{4,6},{5,7},{6,4},{7,5},{8,10},{9,11},{10,... | collective-permute-start | bytes 393224 | tf_op jit(solution)/shard_map/ppermute | solution.py:33
  4.5 12.0 %collective-permute-start.10 = (bf16[64,1024]{1,0:T(8,128)(2,1)}, bf16[64,1024]{1,0:T(8,128)(2,1)}, u32[]{:S(2)}, u32[]{:S(2)}) collective-permute-start(bf16[64,1024]{1,0:T(8,128)(2,1)} %refs_4_.1), channel_id=1, source_target_pairs={{0,16},{16,0},{1,17},{17,1},{2,18},{18,2},{3,19},{19,3},{4,20},{20... | collective-permute-start | bytes 393224 | tf_op jit(solution)/shard_map/ppermute | solution.py:33
  5.0 11.5 %collective-permute-start.4 = (bf16[64,1024]{1,0:T(8,128)(2,1)}, bf16[64,1024]{1,0:T(8,128)(2,1)}, u32[]{:S(2)}, u32[]{:S(2)}) collective-permute-start(bf16[64,1024]{1,0:T(8,128)(2,1)} %refs_4_.1), channel_id=1, source_target_pairs={{0,1},{1,0},{2,3},{3,2},{4,5},{5,4},{6,7},{7,6},{8,9},{9,8},{10,11... | collective-permute-start | bytes 393224 | tf_op jit(solution)/shard_map/ppermute | solution.py:33
  6.8 9.8 %collective-permute-start.3 = (bf16[64,1024]{1,0:T(8,128)(2,1)}, bf16[64,1024]{1,0:T(8,128)(2,1)}, u32[]{:S(2)}, u32[]{:S(2)}) collective-permute-start(bf16[64,1024]{1,0:T(8,128)(2,1)} %refs_4_.1), channel_id=1, source_target_pairs={{0,2},{1,3},{2,0},{3,1},{4,6},{5,7},{6,4},{7,5},{8,10},{9,11},{10,... | collective-permute-start | bytes 393224 | tf_op jit(solution)/shard_map/ppermute | solution.py:33
  10.6 6.1 %collective-permute-start.14 = (bf16[32,2048]{1,0:T(8,128)(2,1)}, bf16[32,2048]{1,0:T(8,128)(2,1)}, u32[]{:S(2)}, u32[]{:S(2)}) collective-permute-start(bf16[32,2048]{1,0:T(8,128)(2,1)} %bitcast.5), channel_id=1, source_target_pairs={{0,16},{16,0},{1,17},{17,1},{2,18},{18,2},{3,19},{19,3},{4,20},{20... | collective-permute-start | bytes 393224 | tf_op jit(solution)/shard_map/ppermute | solution.py:33
  12.9 6.8 %collective-permute-start.15 = (bf16[32,2560]{1,0:T(8,128)(2,1)}, bf16[32,2560]{1,0:T(8,128)(2,1)S(1)}, u32[]{:S(2)}, u32[]{:S(2)}) collective-permute-start(bf16[32,2560]{1,0:T(8,128)(2,1)} %get-tuple-element.21.refs_16_.refs_0_), channel_id=1, source_target_pairs={{0,12},{4,0},{8,4},{12,8},{1,13},{5,1},{9,5},{13,9},{2,14},{6,2},{... | collective-permute-start | bytes 491528 | tf_op jit(solution)/shard_map/ppermute | solution.py:38
  16.5 8.6 %collective-permute-start.19 = (bf16[32,2560]{1,0:T(8,128)(2,1)}, bf16[32,2560]{1,0:T(8,128)(2,1)S(1)}, u32[]{:S(2)}, u32[]{:S(2)}) collective-permute-start(bf16[32,2560]{1,0:T(8,128)(2,1)} %get-tuple-element.21.refs_16_.refs_0_), channel_id=1, source_target_pairs={{0,4},{4,8},{8,12},{12,0},{1,5},{5,9},{9,13},{13,1},{2,6},{6,10},{... | collective-permute-start | bytes 491528 | tf_op jit(solution)/shard_map/ppermute | solution.py:38
  16.5 8.6 %collective-permute-start.8 = (bf16[64,1024]{1,0:T(8,128)(2,1)}, bf16[64,1024]{1,0:T(8,128)(2,1)S(1)}, u32[]{:S(2)}, u32[]{:S(2)}) collective-permute-start(bf16[64,1024]{1,0:T(8,128)(2,1)} %collective-permute-done.6.refs_8_), channel_id=1, source_target_pairs={{0,1},{1,0},{2,3},{3,2},{4,5},{5,4},{6,7},{7,6},{8,9},{9,8},{10,11... | collective-permute-start | bytes 393224 | tf_op jit(solution)/shard_map/ppermute | solution.py:33
  16.6 8.6 %collective-permute-start.7 = (bf16[64,1024]{1,0:T(8,128)(2,1)}, bf16[64,1024]{1,0:T(8,128)(2,1)}, u32[]{:S(2)}, u32[]{:S(2)}) collective-permute-start(bf16[64,1024]{1,0:T(8,128)(2,1)} %collective-permute-done.6.refs_8_), channel_id=1, source_target_pairs={{0,2},{1,3},{2,0},{3,1},{4,6},{5,7},{6,4},{7,5},{8,10},{9,11},{10,... | collective-permute-start | bytes 393224 | tf_op jit(solution)/shard_map/ppermute | solution.py:33
  16.7 9.9 %collective-permute-start.2 = (bf16[64,1024]{1,0:T(8,128)(2,1)}, bf16[64,1024]{1,0:T(8,128)(2,1)S(1)}, u32[]{:S(2)}, u32[]{:S(2)}) collective-permute-start(bf16[64,1024]{1,0:T(8,128)(2,1)} %collective-permute-done.refs_1_), channel_id=1, source_target_pairs={{0,1},{1,0},{2,3},{3,2},{4,5},{5,4},{6,7},{7,6},{8,9},{9,8},{10,11... | collective-permute-start | bytes 393224 | tf_op jit(solution)/shard_map/ppermute | solution.py:33
  19.7 0.7 copy-start
  20.4 11.5 %collective-permute-start.17 = (bf16[32,2560]{1,0:T(8,128)(2,1)S(1)}, bf16[32,2560]{1,0:T(8,128)(2,1)S(1)}, u32[]{:S(2)}, u32[]{:S(2)}) collective-permute-start(bf16[32,2560]{1,0:T(8,128)(2,1)S(1)} %collective-permute-done.15.refs_18_.refs_1_), channel_id=1, source_target_pairs={{0,12},{4,0},{8,4},{12,8},{1,13},{5,1},{9,5},{13,9},{2,14},{6,2},{... | collective-permute-start | bytes 491528 | tf_op jit(solution)/shard_map/ppermute | solution.py:38
  25.1 6.8 %copy-start.1 = (bf16[32,2560]{1,0:T(8,128)(2,1)}, bf16[32,2560]{1,0:T(8,128)(2,1)S(1)}, u32[]{:S(2)}) copy-start(bf16[32,2560]{1,0:T(8,128)(2,1)S(1)} %collective-permute-done.19.refs_22_.refs_3_) | copy-start | bytes 491524
  25.1 1.6 %collective-permute-start.12 = (bf16[64,1024]{1,0:T(8,128)(2,1)}, bf16[64,1024]{1,0:T(8,128)(2,1)S(1)}, u32[]{:S(2)}, u32[]{:S(2)}) collective-permute-start(bf16[64,1024]{1,0:T(8,128)(2,1)} %collective-permute-done.10.refs_12_), channel_id=1, source_target_pairs={{0,1},{1,0},{2,3},{3,2},{4,5},{5,4},{6,7},{7,6},{8,9},{9,8},{10,11... | collective-permute-start | bytes 393224 | tf_op jit(solution)/shard_map/ppermute | solution.py:33
  25.2 6.7 %copy-start.3 = (bf16[64,1024]{1,0:T(8,128)(2,1)}, bf16[64,1024]{1,0:T(8,128)(2,1)S(1)}, u32[]{:S(2)}) copy-start(bf16[64,1024]{1,0:T(8,128)(2,1)S(1)} %collective-permute-done.8.refs_10_) | copy-start | bytes 393220
  25.2 6.2 %collective-permute-start.11 = (bf16[64,1024]{1,0:T(8,128)(2,1)}, bf16[64,1024]{1,0:T(8,128)(2,1)}, u32[]{:S(2)}, u32[]{:S(2)}) collective-permute-start(bf16[64,1024]{1,0:T(8,128)(2,1)} %collective-permute-done.10.refs_12_), channel_id=1, source_target_pairs={{0,2},{1,3},{2,0},{3,1},{4,6},{5,7},{6,4},{7,5},{8,10},{9,11},{10,... | collective-permute-start | bytes 393224 | tf_op jit(solution)/shard_map/ppermute | solution.py:33
  25.3 6.2 %collective-permute-start.16 = (bf16[32,2048]{1,0:T(8,128)(2,1)}, bf16[32,2048]{1,0:T(8,128)(2,1)}, u32[]{:S(2)}, u32[]{:S(2)}) collective-permute-start(bf16[32,2048]{1,0:T(8,128)(2,1)} %collective-permute-done.14.refs_17_), channel_id=1, source_target_pairs={{0,12},{4,0},{8,4},{12,8},{1,13},{5,1},{9,5},{13,9},{2,14},{6,2},{... | collective-permute-start | bytes 393224 | tf_op jit(solution)/shard_map/ppermute | solution.py:38
  26.6 5.3 %copy-start.4 = (bf16[64,1024]{1,0:T(8,128)(2,1)}, bf16[64,1024]{1,0:T(8,128)(2,1)S(1)}, u32[]{:S(2)}) copy-start(bf16[64,1024]{1,0:T(8,128)(2,1)S(1)} %collective-permute-done.2.refs_3_) | copy-start | bytes 393220
  26.6 11.3 %collective-permute-start.5 = (bf16[64,1024]{1,0:T(8,128)(2,1)}, bf16[64,1024]{1,0:T(8,128)(2,1)}, u32[]{:S(2)}, u32[]{:S(2)}) collective-permute-start(bf16[64,1024]{1,0:T(8,128)(2,1)} %collective-permute-done.3.refs_5_), channel_id=1, source_target_pairs={{0,1},{1,0},{2,3},{3,2},{4,5},{5,4},{6,7},{7,6},{8,9},{9,8},{10,11... | collective-permute-start | bytes 393224 | tf_op jit(solution)/shard_map/ppermute | solution.py:33
  26.7 5.2 %copy-start.5 = (bf16[64,1024]{1,0:T(8,128)(2,1)}, bf16[64,1024]{1,0:T(8,128)(2,1)S(1)}, u32[]{:S(2)}) copy-start(bf16[64,1024]{1,0:T(8,128)(2,1)S(1)} %collective-permute-done.12.refs_14_) | copy-start | bytes 393220
  26.7 11.5 %collective-permute-start.20 = (bf16[32,2048]{1,0:T(8,128)(2,1)}, bf16[32,2048]{1,0:T(8,128)(2,1)}, u32[]{:S(2)}, u32[]{:S(2)}) collective-permute-start(bf16[32,2048]{1,0:T(8,128)(2,1)} %collective-permute-done.14.refs_17_), channel_id=1, source_target_pairs={{0,4},{4,8},{8,12},{12,0},{1,5},{5,9},{9,13},{13,1},{2,6},{6,10},{... | collective-permute-start | bytes 393224 | tf_op jit(solution)/shard_map/ppermute | solution.py:38
  31.4 7.1 %collective-permute-start.9 = (bf16[64,1024]{1,0:T(8,128)(2,1)}, bf16[64,1024]{1,0:T(8,128)(2,1)}, u32[]{:S(2)}, u32[]{:S(2)}) collective-permute-start(bf16[64,1024]{1,0:T(8,128)(2,1)} %collective-permute-done.7.refs_9_), channel_id=1, source_target_pairs={{0,1},{1,0},{2,3},{3,2},{4,5},{5,4},{6,7},{7,6},{8,9},{9,8},{10,11... | collective-permute-start | bytes 393224 | tf_op jit(solution)/shard_map/ppermute | solution.py:33
  31.4 7.0 %collective-permute-start.13 = (bf16[64,1024]{1,0:T(8,128)(2,1)}, bf16[64,1024]{1,0:T(8,128)(2,1)}, u32[]{:S(2)}, u32[]{:S(2)}) collective-permute-start(bf16[64,1024]{1,0:T(8,128)(2,1)} %collective-permute-done.11.refs_13_), channel_id=1, source_target_pairs={{0,1},{1,0},{2,3},{3,2},{4,5},{5,4},{6,7},{7,6},{8,9},{9,8},{10,11... | collective-permute-start | bytes 393224 | tf_op jit(solution)/shard_map/ppermute | solution.py:33
  31.9 0.7 copy-start.2
  32.6 7.5 %collective-permute-start.18 = (bf16[32,2048]{1,0:T(8,128)(2,1)}, bf16[32,2048]{1,0:T(8,128)(2,1)}, u32[]{:S(2)}, u32[]{:S(2)}) collective-permute-start(bf16[32,2048]{1,0:T(8,128)(2,1)} %collective-permute-done.16.refs_19_), channel_id=1, source_target_pairs={{0,12},{4,0},{8,4},{12,8},{1,13},{5,1},{9,5},{13,9},{2,14},{6,2},{... | collective-permute-start | bytes 393224 | tf_op jit(solution)/shard_map/ppermute | solution.py:38
  37.8 14.8 %collective-permute-start.28 = (bf16[4,32,512]{2,1,0:T(8,128)(2,1)}, bf16[4,32,512]{2,1,0:T(8,128)(2,1)}, u32[]{:S(2)}, u32[]{:S(2)}) collective-permute-start(bf16[4,32,512]{2,1,0:T(8,128)(2,1)} %pick.1.refs_0_), channel_id=1, source_target_pairs={{0,2},{1,3},{2,0},{3,1},{4,6},{5,7},{6,4},{7,5},{8,10},{9,11},{10,... | collective-permute-start | bytes 393224 | tf_op jit(solution)/shard_map/ppermute | solution.py:33
  38.2 14.7 %collective-permute-start.29 = (bf16[4,32,512]{2,1,0:T(8,128)(2,1)}, bf16[4,32,512]{2,1,0:T(8,128)(2,1)}, u32[]{:S(2)}, u32[]{:S(2)}) collective-permute-start(bf16[4,32,512]{2,1,0:T(8,128)(2,1)} %pick.1.refs_0_), channel_id=1, source_target_pairs={{0,1},{1,0},{2,3},{3,2},{4,5},{5,4},{6,7},{7,6},{8,9},{9,8},{10,11... | collective-permute-start | bytes 393224 | tf_op jit(solution)/shard_map/ppermute | solution.py:33
  49.7 3.1 %collective-permute-start.21 = (bf16[2,4,32,256]{3,2,1,0:T(8,128)(2,1)}, bf16[2,4,32,256]{3,2,1,0:T(8,128)(2,1)}, u32[]{:S(2)}, u32[]{:S(2)}) collective-permute-start(bf16[2,4,32,256]{3,2,1,0:T(8,128)(2,1)} %get-tuple-element.24), channel_id=1, source_target_pairs={{0,1},{1,0},{2,3},{3,2},{16,17},{17,16},{18,19},{19,18},{4,5},{5,4... | collective-permute-start | bytes 393224 | tf_op jit(solution)/shard_map/ppermute | solution.py:444
  49.8 7.5 %collective-permute-start.22 = (bf16[2,4,32,256]{3,2,1,0:T(8,128)(2,1)}, bf16[2,4,32,256]{3,2,1,0:T(8,128)(2,1)}, u32[]{:S(2)}, u32[]{:S(2)}) collective-permute-start(bf16[2,4,32,256]{3,2,1,0:T(8,128)(2,1)} %get-tuple-element.25), channel_id=1, source_target_pairs={{0,2},{1,3},{2,0},{3,1},{16,18},{17,19},{18,16},{19,17},{4,6},{5,7... | collective-permute-start | bytes 393224 | tf_op jit(solution)/shard_map/ppermute | solution.py:444
  52.7 6.0 %collective-permute-start.30 = (bf16[4,32,512]{2,1,0:T(8,128)(2,1)}, bf16[4,32,512]{2,1,0:T(8,128)(2,1)}, u32[]{:S(2)}, u32[]{:S(2)}) collective-permute-start(bf16[4,32,512]{2,1,0:T(8,128)(2,1)} %collective-permute-done.28.refs_1_), channel_id=1, source_target_pairs={{0,1},{1,0},{2,3},{3,2},{4,5},{5,4},{6,7},{7,6},{8,9},{9,8},{10,11... | collective-permute-start | bytes 393224 | tf_op jit(solution)/shard_map/ppermute | solution.py:33
  52.8 8.4 %collective-permute-start.23 = (bf16[2,4,32,256]{3,2,1,0:T(8,128)(2,1)}, bf16[2,4,32,256]{3,2,1,0:T(8,128)(2,1)}, u32[]{:S(2)}, u32[]{:S(2)}) collective-permute-start(bf16[2,4,32,256]{3,2,1,0:T(8,128)(2,1)} %get-tuple-element.26), channel_id=1, source_target_pairs={{0,3},{1,2},{2,1},{3,0},{16,19},{17,18},{18,17},{19,16},{4,7},{5,6... | collective-permute-start | bytes 393224 | tf_op jit(solution)/shard_map/ppermute | solution.py:444
  52.9 8.4 %collective-permute-start.24 = (bf16[2,4,32,256]{3,2,1,0:T(8,128)(2,1)}, bf16[2,4,32,256]{3,2,1,0:T(8,128)(2,1)}, u32[]{:S(2)}, u32[]{:S(2)}) collective-permute-start(bf16[2,4,32,256]{3,2,1,0:T(8,128)(2,1)} %get-tuple-element.27), channel_id=1, source_target_pairs={{0,16},{1,17},{2,18},{3,19},{16,0},{17,1},{18,2},{19,3},{4,20},{5,... | collective-permute-start | bytes 393224 | tf_op jit(solution)/shard_map/ppermute | solution.py:444
  52.9 8.4 %collective-permute-start.25 = (bf16[2,4,32,256]{3,2,1,0:T(8,128)(2,1)}, bf16[2,4,32,256]{3,2,1,0:T(8,128)(2,1)}, u32[]{:S(2)}, u32[]{:S(2)}) collective-permute-start(bf16[2,4,32,256]{3,2,1,0:T(8,128)(2,1)} %get-tuple-element.28), channel_id=1, source_target_pairs={{0,17},{1,16},{2,19},{3,18},{16,1},{17,0},{18,3},{19,2},{4,21},{5,... | collective-permute-start | bytes 393224 | tf_op jit(solution)/shard_map/ppermute | solution.py:444
  57.3 9.2 %collective-permute-start.26 = (bf16[2,4,32,256]{3,2,1,0:T(8,128)(2,1)}, bf16[2,4,32,256]{3,2,1,0:T(8,128)(2,1)}, u32[]{:S(2)}, u32[]{:S(2)}) collective-permute-start(bf16[2,4,32,256]{3,2,1,0:T(8,128)(2,1)} %get-tuple-element.29), channel_id=1, source_target_pairs={{0,18},{1,19},{2,16},{3,17},{16,2},{17,3},{18,0},{19,1},{4,22},{5,... | collective-permute-start | bytes 393224 | tf_op jit(solution)/shard_map/ppermute | solution.py:444
  58.7 9.1 %collective-permute-start.27 = (bf16[2,4,32,256]{3,2,1,0:T(8,128)(2,1)}, bf16[2,4,32,256]{3,2,1,0:T(8,128)(2,1)}, u32[]{:S(2)}, u32[]{:S(2)}) collective-permute-start(bf16[2,4,32,256]{3,2,1,0:T(8,128)(2,1)} %get-tuple-element.30), channel_id=1, source_target_pairs={{0,19},{1,18},{2,17},{3,16},{16,3},{17,2},{18,1},{19,0},{4,23},{5,... | collective-permute-start | bytes 393224 | tf_op jit(solution)/shard_map/ppermute | solution.py:444
  70.0 6.6 %collective-permute-start.31 = (bf16[256,256]{1,0:T(8,128)(2,1)}, bf16[256,256]{1,0:T(8,128)(2,1)}, u32[]{:S(2)}, u32[]{:S(2)}) collective-permute-start(bf16[256,256]{1,0:T(8,128)(2,1)} %shard_map.64.refs_8_), channel_id=1, source_target_pairs={{0,12},{4,0},{8,4},{12,8},{1,13},{5,1},{9,5},{13,9},{2,14},{6,2},{... | collective-permute-start | bytes 393224 | tf_op jit(solution)/shard_map/ppermute | solution.py:38
  74.5 12.4 %collective-permute-start.32 = (bf16[256,256]{1,0:T(8,128)(2,1)}, bf16[256,256]{1,0:T(8,128)(2,1)}, u32[]{:S(2)}, u32[]{:S(2)}) collective-permute-start(bf16[256,256]{1,0:T(8,128)(2,1)} %shard_map.65.refs_9_), channel_id=1, source_target_pairs={{0,12},{4,0},{8,4},{12,8},{1,13},{5,1},{9,5},{13,9},{2,14},{6,2},{... | collective-permute-start | bytes 393224 | tf_op jit(solution)/shard_map/ppermute | solution.py:38
  74.5 12.3 %collective-permute-start.33 = (bf16[256,256]{1,0:T(8,128)(2,1)}, bf16[256,256]{1,0:T(8,128)(2,1)}, u32[]{:S(2)}, u32[]{:S(2)}) collective-permute-start(bf16[256,256]{1,0:T(8,128)(2,1)} %shard_map.64.refs_8_), channel_id=1, source_target_pairs={{0,4},{4,8},{8,12},{12,0},{1,5},{5,9},{9,13},{13,1},{2,6},{6,10},{... | collective-permute-start | bytes 393224 | tf_op jit(solution)/shard_map/ppermute | solution.py:38
  76.5 10.3 %collective-permute-start.34 = (bf16[256,256]{1,0:T(8,128)(2,1)}, bf16[256,256]{1,0:T(8,128)(2,1)}, u32[]{:S(2)}, u32[]{:S(2)}) collective-permute-start(bf16[256,256]{1,0:T(8,128)(2,1)} %shard_map.65.refs_9_), channel_id=1, source_target_pairs={{0,4},{4,8},{8,12},{12,0},{1,5},{5,9},{9,13},{13,1},{2,6},{6,10},{... | collective-permute-start | bytes 393224 | tf_op jit(solution)/shard_map/ppermute | solution.py:38
  76.6 13.1 %collective-permute-start.35 = (bf16[256,256]{1,0:T(8,128)(2,1)}, bf16[256,256]{1,0:T(8,128)(2,1)}, u32[]{:S(2)}, u32[]{:S(2)}) collective-permute-start(bf16[256,256]{1,0:T(8,128)(2,1)} %collective-permute-done.31.refs_10_), channel_id=1, source_target_pairs={{0,12},{4,0},{8,4},{12,8},{1,13},{5,1},{9,5},{13,9},{2,14},{6,2},{... | collective-permute-start | bytes 393224 | tf_op jit(solution)/shard_map/ppermute | solution.py:38
  86.8 5.3 %collective-permute-start.36 = (bf16[256,256]{1,0:T(8,128)(2,1)}, bf16[256,256]{1,0:T(8,128)(2,1)}, u32[]{:S(2)}, u32[]{:S(2)}) collective-permute-start(bf16[256,256]{1,0:T(8,128)(2,1)} %collective-permute-done.32.refs_11_), channel_id=1, source_target_pairs={{0,12},{4,0},{8,4},{12,8},{1,13},{5,1},{9,5},{13,9},{2,14},{6,2},{... | collective-permute-start | bytes 393224 | tf_op jit(solution)/shard_map/ppermute | solution.py:38
  94.2 4.6 %collective-permute-start.37 = (bf16[2,64,256]{2,1,0:T(8,128)(2,1)}, bf16[2,64,256]{2,1,0:T(8,128)(2,1)}, u32[]{:S(2)}, u32[]{:S(2)}) collective-permute-start(bf16[2,64,256]{2,1,0:T(8,128)(2,1)} %get-tuple-element.34), channel_id=1, source_target_pairs={{0,2},{1,3},{2,0},{3,1},{4,6},{5,7},{6,4},{7,5},{8,10},{9,11},{10,... | collective-permute-start | bytes 196616 | tf_op jit(solution)/shard_map/ppermute | solution.py:33
  95.7 4.6 %collective-permute-start.38 = (bf16[2,64,256]{2,1,0:T(8,128)(2,1)}, bf16[2,64,256]{2,1,0:T(8,128)(2,1)}, u32[]{:S(2)}, u32[]{:S(2)}) collective-permute-start(bf16[2,64,256]{2,1,0:T(8,128)(2,1)} %get-tuple-element.35), channel_id=1, source_target_pairs={{0,3},{1,2},{2,1},{3,0},{4,7},{5,6},{6,5},{7,4},{8,11},{9,10},{10,... | collective-permute-start | bytes 196616 | tf_op jit(solution)/shard_map/ppermute | solution.py:33
  97.9 2.4 %collective-permute-start.39 = (bf16[2,64,256]{2,1,0:T(8,128)(2,1)}, bf16[2,64,256]{2,1,0:T(8,128)(2,1)}, u32[]{:S(2)}, u32[]{:S(2)}) collective-permute-start(bf16[2,64,256]{2,1,0:T(8,128)(2,1)} %get-tuple-element.36), channel_id=1, source_target_pairs={{0,1},{1,0},{2,3},{3,2},{4,5},{5,4},{6,7},{7,6},{8,9},{9,8},{10,11... | collective-permute-start | bytes 196616 | tf_op jit(solution)/shard_map/ppermute | solution.py:33
